TPU v7x, 256 devices: a whole 4x4x8 slice. The times are simulated.
256 devices in a mesh: row: 16 (over y_hi, x, core), col: 16 (over z, y_lo).
Axes of the slice: x: 4, y: 4 (y_hi: 2, y_lo: 2; y = y_hi * 2 + y_lo), z: 8, core: 2. Of those that a mesh axis runs over, the one named last changes fastest.
Arguments:
- tile_matrix: bfloat16 [2, 1024, 1024], replicated
- tile_inverse: bfloat16 [2, 1024, 1024], replicated, as said below
- block_rows: int32 [16, 16, 4], P('row', 'col'), may hold values from 0 to 1, as said below
- block_cols: int32 [16, 16, 4], P('row', 'col'), may hold values from 0 to 1
- block_tiles: int32 [16, 16, 4], P('row', 'col'), may hold values from 0 to 1
- block_count: int32 [16, 16], P('row', 'col'), may hold values from 2 to 4, as said below
- column_values: float32 [64, 32768], P(None, 'col'), may hold values from -6 to 6
- column_duals: float32 [64, 32768], P(None, 'col'), may hold values from -3 to 3
- unit_cost: float32 [64, 32768], P(None, 'col'), may hold values from 0.1 to 1
- capacity: float32 [64, 32768], P(None, 'col'), may hold values from 0.5 to 3
- row_values: float32 [64, 32768], P(None, 'row'), may hold values from -6 to 6
- row_duals: float32 [64, 32768], P(None, 'row'), may hold values from -3 to 3
- row_lower: float32 [64, 32768], P(None, 'row'), may hold values from -1.5 to -0.2
- row_upper: float32 [64, 32768], P(None, 'row'), may hold values from 0.2 to 1.5
- block_image: float32 [16, 16, 4, 64, 1024], P('row', 'col'), may hold values from -6 to 6
- image_dual: float32 [16, 16, 4, 64, 1024], P('row', 'col'), may hold values from -3 to 3
- input_dual: float32 [16, 16, 4, 64, 1024], P('row', 'col'), may hold values from -3 to 3
Outputs:
- column_solution: float32 [64, 32768], P(None, 'col')
- row_solution: float32 [64, 32768], P(None, 'row')
Inputs may be any that keep to these rules, and one draw needn't show every extreme that they name: tile_inverse[t] is the inverse of I + A A^T for A = tile_matrix[t] as given, computed in float32 and rounded. On one device the live slots name different (block_rows, block_cols) pairs. Slots 0 to block_count - 1 of a device are live; some device fills all 4 slots.
All inputs are finite; a program needn't handle non-finite values.
Results may differ from a plain program's by a relative error of at most 0.0035.
Values sent between devices are 32-bit elements; how exact they have to be, the bound alone decides.
A program may use at most 64 MiB of HBM per device.

v0:
```python
import jax
import jax.numpy as jnp
from jax import lax
from jax.sharding import PartitionSpec as P

ITERS = 2


def project_block(
    x_full, matrix_t, inverse_t, image_now, image_gap_dual, input_now, column, block_width
):
    image_gap = (image_now - image_gap_dual).astype(jnp.bfloat16)
    x_column = lax.dynamic_slice_in_dim(x_full, column * block_width, block_width, 1)
    pulled = lax.dot_general(
        image_gap, matrix_t, (((1,), (1,)), ((), ())), preferred_element_type=jnp.float32
    )
    merged_input = (x_column - input_now + pulled).astype(jnp.bfloat16)
    x_proj = jnp.dot(merged_input, inverse_t, preferred_element_type=jnp.float32)
    y_proj = jnp.dot(x_proj.astype(jnp.bfloat16), matrix_t, preferred_element_type=jnp.float32)
    return (x_proj, y_proj)


def per_device(
    tile_matrix,
    tile_inverse,
    block_rows,
    block_cols,
    block_tiles,
    block_count,
    column_values,
    column_duals,
    unit_cost,
    capacity,
    row_values,
    row_duals,
    row_lower,
    row_upper,
    block_image,
    image_dual,
    input_dual,
):
    block_width = tile_matrix.shape[1]
    scenarios = column_values.shape[0]
    col_blocks = column_values.shape[1] // block_width
    row_blocks = row_values.shape[1] // block_width
    slot_total = block_rows.shape[2]
    rows_here = block_rows[0, 0]
    cols_here = block_cols[0, 0]
    tiles_here = block_tiles[0, 0]
    live_slot = jnp.arange(slot_total, dtype=jnp.int32) < block_count[0, 0]
    row_grid = row_blocks * lax.axis_size("row")
    col_grid = col_blocks * lax.axis_size("col")
    global_rows = lax.axis_index("row") * row_blocks + rows_here
    global_cols = lax.axis_index("col") * col_blocks + cols_here
    row_onehot = (
        (jnp.arange(row_grid, dtype=jnp.int32)[None, :] == global_rows[:, None])
        & live_slot[:, None]
    ).astype(jnp.float32)
    col_onehot = (jnp.arange(col_grid, dtype=jnp.int32)[None, :] == global_cols[:, None]).astype(
        jnp.float32
    )
    occupancy = jnp.dot(row_onehot.T, col_onehot, precision=lax.Precision.HIGHEST)
    occupancy = lax.psum(occupancy, ("row", "col"))
    col_count = lax.dynamic_slice_in_dim(
        jnp.sum(occupancy, axis=0), lax.axis_index("col") * col_blocks, col_blocks, 0
    )
    row_count = lax.dynamic_slice_in_dim(
        jnp.sum(occupancy, axis=1), lax.axis_index("row") * row_blocks, row_blocks, 0
    )
    col_denom = (1.0 + jnp.repeat(col_count, block_width))[None, :]
    row_denom = (1.0 + jnp.repeat(row_count, block_width))[None, :]
    x_own = column_values
    x_dual = column_duals
    y_state = row_values
    y_dual = row_duals
    x_full = column_values
    images = [block_image[0, 0, slot_index] for slot_index in range(slot_total)]
    image_duals = [image_dual[0, 0, slot_index] for slot_index in range(slot_total)]
    input_duals = [input_dual[0, 0, slot_index] for slot_index in range(slot_total)]
    zero_block = jnp.zeros((scenarios, block_width), jnp.float32)
    for iteration in range(ITERS):
        x_half = jnp.clip(x_own - x_dual - unit_cost, 0.0, capacity)
        y_half = jnp.clip(y_state - y_dual, row_lower, row_upper)
        y_anchor = y_half + y_dual
        col_terms = jnp.zeros((scenarios, col_blocks, block_width), jnp.float32)
        row_terms = jnp.zeros((scenarios, row_blocks, block_width), jnp.float32)
        projected = []
        for slot_index in range(slot_total):

            def active(slot_index=slot_index):
                matrix_t = lax.dynamic_index_in_dim(
                    tile_matrix, tiles_here[slot_index], 0, keepdims=False
                )
                inverse_t = lax.dynamic_index_in_dim(
                    tile_inverse, tiles_here[slot_index], 0, keepdims=False
                )
                return project_block(
                    x_full,
                    matrix_t,
                    inverse_t,
                    images[slot_index],
                    image_duals[slot_index],
                    input_duals[slot_index],
                    cols_here[slot_index],
                    block_width,
                )

            def skipped():
                return (zero_block, zero_block)

            x_proj, y_proj = lax.cond(live_slot[slot_index], active, skipped)
            col_pick = (
                (jnp.arange(col_blocks, dtype=jnp.int32) == cols_here[slot_index])
                & live_slot[slot_index]
            ).astype(jnp.float32)
            row_pick = (
                (jnp.arange(row_blocks, dtype=jnp.int32) == rows_here[slot_index])
                & live_slot[slot_index]
            ).astype(jnp.float32)
            col_terms = (
                col_terms + col_pick[None, :, None] * (x_proj + input_duals[slot_index])[:, None, :]
            )
            row_terms = (
                row_terms + row_pick[None, :, None] * (y_proj + image_duals[slot_index])[:, None, :]
            )
            projected.append((x_proj, y_proj))
        col_terms = col_terms.reshape(scenarios, col_blocks * block_width)
        row_terms = row_terms.reshape(scenarios, row_blocks * block_width)
        col_total = lax.psum(col_terms, "row")
        x_own = (x_half + x_dual + col_total) / col_denom
        x_dual = x_dual + x_half - x_own
        x_full = x_own
        row_total = lax.psum(row_terms, "col")
        shift_full = (row_total - y_anchor) / row_denom
        y_state = y_anchor + shift_full
        y_dual = y_dual + y_half - y_state
        for slot_index in range(slot_total):
            x_proj, y_proj = projected[slot_index]
            x_column = lax.dynamic_slice_in_dim(
                x_full, cols_here[slot_index] * block_width, block_width, 1
            )
            input_duals[slot_index] = input_duals[slot_index] + x_proj - x_column
            shift_rows = lax.dynamic_slice_in_dim(
                shift_full, rows_here[slot_index] * block_width, block_width, 1
            )
            new_image = y_proj + image_duals[slot_index] - shift_rows
            image_duals[slot_index] = image_duals[slot_index] + y_proj - new_image
            images[slot_index] = new_image
    column_final = jnp.clip(x_own - x_dual - unit_cost, 0.0, capacity)
    row_final = jnp.clip(y_state - y_dual, row_lower, row_upper)
    return (column_final, row_final)


def solution(mesh):
    placed = (
        P(),
        P(),
        P("row", "col", None),
        P("row", "col", None),
        P("row", "col", None),
        P("row", "col"),
        P(None, "col"),
        P(None, "col"),
        P(None, "col"),
        P(None, "col"),
        P(None, "row"),
        P(None, "row"),
        P(None, "row"),
        P(None, "row"),
        P("row", "col", None, None, None),
        P("row", "col", None, None, None),
        P("row", "col", None, None, None),
    )
    return jax.shard_map(
        per_device,
        mesh=mesh,
        in_specs=placed,
        out_specs=(P(None, "col"), P(None, "row")),
        check_vma=False,
    )
```

profile of v0, /device:TPU:1, one launch (start us, length us, event | category | flops | bytes accessed | tf_op | source)
XLA Modules:
  0.0 693.4 jit_solution(4663216549494634539)
XLA Ops:
  8.0 1.5 fusion.220
  9.5 0.6 fusion.222
  12.7 1.5 fusion.221
  14.1 1.9 and_convert_fusion.1
  16.2 1.8 and_convert_fusion
  18.1 1.9 and_convert_fusion.2
  20.0 1.8 and_convert_fusion.3
  21.9 2.4 slice_bitcast_fusion.6
  24.3 7.2 %conditional.8 = (f32[64,1024]{1,0:T(8,128)}, f32[64,1024]{1,0:T(8,128)}) conditional(s32[]{:T(128)} %convert_element_type.155, () %tuple.72, (s32[4]{0:T(128)S(1)}, f32[64,2048]{1,0:T(8,128)S(1)}, f32[64,1024]{1,0:T(8,128)}, f32[1,1,4,64,1024]{4,3,2,1,0:T(8,128)S(1)}, f32[64,1024]{1,0:T(8,128)S(1)}, /*index=5*/s32[4]{0:T(128)S(1)}, ...), branch_computations={%region_0.0_spmd, %region_1.0_spmd} | conditional | flops 403046400 | bytes 8128100 | solution.py:111
  24.5 4.2 fusion
  28.6 2.9 fusion.2
  31.5 10.0 %conditional.9 = (f32[64,1024]{1,0:T(8,128)}, f32[64,1024]{1,0:T(8,128)S(1)}) conditional(s32[]{:T(128)} %convert_element_type.157, () %tuple.74, (s32[4]{0:T(128)S(1)}, f32[64,2048]{1,0:T(8,128)S(1)}, f32[64,1024]{1,0:T(8,128)S(1)}, f32[1,1,4,64,1024]{4,3,2,1,0:T(8,128)S(1)}, f32[64,1024]{1,0:T(8,128)S(1)}, /*index=5*/s32[4]{0:T(128)S(1)}, ...), branch_computations={%region_2.0_spmd, %region_3.4_spmd} | conditional | flops 403046400 | bytes 8128116 | solution.py:111
  31.5 0.6 slice.44
  34.0 0.6 slice.42
  35.3 4.1 fusion.26
  39.4 2.2 fusion.28
  41.5 0.7 copy-done.17
  42.3 1.5 conditional.11
  42.3 0.7 broadcast_in_dim.6.clone
  43.0 0.7 broadcast_in_dim.6
  43.7 10.3 %conditional.10 = (f32[64,1024]{1,0:T(8,128)}, f32[64,1024]{1,0:T(8,128)S(1)}) conditional(s32[]{:T(128)} %convert_element_type.159, () %tuple.76, (s32[4]{0:T(128)S(1)}, f32[64,2048]{1,0:T(8,128)S(1)}, f32[64,1024]{1,0:T(8,128)S(1)}, f32[1,1,4,64,1024]{4,3,2,1,0:T(8,128)S(1)}, f32[64,1024]{1,0:T(8,128)S(1)}, /*index=5*/s32[4]{0:T(128)S(1)}, ...), branch_computations={%region_4.5_spmd, %region_5.6_spmd} | conditional | flops 403046400 | bytes 8128116 | solution.py:111
  43.7 0.7 slice.52
  46.5 0.7 slice.45
  47.8 4.1 fusion.52
  51.9 2.2 fusion.54
  54.1 0.7 copy-done.18
  54.8 1.3 fusion.208
  57.6 1.0 multiply_add_fusion.2
  58.8 1.3 fusion.207
  61.7 1.0 multiply_add_fusion.3
  68.0 89.9 %psum.36 = f32[32,32]{1,0:T(8,128)S(1)} all-reduce(f32[32,32]{1,0:T(8,128)S(1)} %fusion.202), channel_id=1, replica_groups=mesh['row'=16,'col'=16] {'row','col'}, use_global_device_ids=true, to_apply=%region_9.10 | all-reduce | flops 1024 | bytes 8192 | tf_op jit(solution)/shard_map/psum | solution.py:63
  158.3 40.1 %all-reduce.7.cloned.1.call-done = f32[64,2048]{1,0:T(8,128)} async-done(((f32[64,2048]{1,0:T(8,128)}), f32[64,2048]{1,0:T(8,128)}) %all-reduce.7.cloned.1.call-update) | async-done | bytes 524304 | tf_op jit(solution)/shard_map/psum | solution.py:133
  198.4 1.7 subtract_divide_fusion
  200.1 1.4 fusion.216
  201.5 153.8 %all-reduce.5.cloned.1.call-done = f32[64,2048]{1,0:T(8,128)} async-done(((f32[64,2048]{1,0:T(8,128)}), f32[64,2048]{1,0:T(8,128)}) %all-reduce.5.cloned.1.call-update) | async-done | bytes 524304 | tf_op jit(solution)/shard_map/psum | solution.py:129
  355.3 1.5 add_divide_fusion
  357.1 0.8 conditional.15
  357.1 0.7 broadcast_in_dim.14
  358.2 10.0 %conditional.13 = (f32[64,1024]{1,0:T(8,128)}, f32[64,1024]{1,0:T(8,128)S(1)}) conditional(s32[]{:T(128)} %convert_element_type.157, () %tuple.82, (s32[4]{0:T(128)S(1)}, f32[64,2048]{1,0:T(8,128)S(1)}, f32[64,1024]{1,0:T(8,128)S(1)}, f32[64,1024]{1,0:T(8,128)S(1)}, f32[64,1024]{1,0:T(8,128)S(1)}, /*index=5*/s32[4]{0:T(128)S(1)}, ...), branch_computations={%region_15.16_spmd, %region_16.17_spmd} | conditional | flops 403046400 | bytes 8128116 | solution.py:111
  360.7 0.6 slice.84
  362.0 4.1 fusion.127
  366.0 2.2 fusion.129
  368.3 10.1 %conditional.14 = (f32[64,1024]{1,0:T(8,128)}, f32[64,1024]{1,0:T(8,128)S(1)}) conditional(s32[]{:T(128)} %convert_element_type.159, () %tuple.84, (s32[4]{0:T(128)S(1)}, f32[64,2048]{1,0:T(8,128)S(1)}, f32[64,1024]{1,0:T(8,128)S(1)}, f32[64,1024]{1,0:T(8,128)}, f32[64,1024]{1,0:T(8,128)S(1)}, /*index=5*/s32[4]{0:T(128)S(1)}, ...), branch_computations={%region_17.18_spmd, %region_18.19_spmd} | conditional | flops 403046400 | bytes 8128116 | solution.py:111
  368.3 0.6 slice.87
  370.8 0.6 slice.86
  372.0 4.2 fusion.150
  376.2 2.2 fusion.152
  378.4 0.7 copy-done.19
  379.1 1.0 add.352
  380.1 6.5 conditional.12
  380.2 4.1 fusion.104
  384.4 2.2 fusion.106
  386.6 0.7 copy-done.20
  387.3 1.0 add.349
  389.7 1.0 multiply_add_fusion
  390.7 1.0 add.344
  391.7 1.0 add.336
  392.7 1.0 add.340
  393.7 1.0 add.333
  396.1 1.0 multiply_add_fusion.1
  397.1 130.3 %all-reduce.11.cloned.1.call-done = f32[64,2048]{1,0:T(8,128)} async-done(((f32[64,2048]{1,0:T(8,128)}), f32[64,2048]{1,0:T(8,128)}) %all-reduce.11.cloned.1.call-update) | async-done | bytes 524304 | tf_op jit(solution)/shard_map/psum | solution.py:133
  527.4 2.4 fusion.200
  529.8 154.3 %all-reduce.9.cloned.1.call-done = f32[64,2048]{1,0:T(8,128)} async-done(((f32[64,2048]{1,0:T(8,128)}), f32[64,2048]{1,0:T(8,128)}) %all-reduce.9.cloned.1.call-update) | async-done | bytes 524304 | tf_op jit(solution)/shard_map/psum | solution.py:129
  684.2 2.7 fusion.198
  (117 shorter events, 8.2 us)
Async XLA Ops:
  7.2 17.1 %copy-start.23 = (s32[1,1,4]{2,1,0:T(1,128)S(1)}, s32[1,1,4]{2,1,0:T(1,128)}, u32[]{:S(2)}) copy-start(s32[1,1,4]{2,1,0:T(1,128)} %param.36) | copy-start | bytes 52
  7.2 17.1 %copy-start = (f32[64,2048]{1,0:T(8,128)S(1)}, f32[64,2048]{1,0:T(8,128)}, u32[]{:S(2)}) copy-start(f32[64,2048]{1,0:T(8,128)} %param.39) | copy-start | bytes 1572868
  7.2 17.1 %copy-start.16 = (f32[1,1,4,64,1024]{4,3,2,1,0:T(8,128)S(1)}, f32[1,1,4,64,1024]{4,3,2,1,0:T(8,128)}, u32[]{:S(2)}) copy-start(f32[1,1,4,64,1024]{4,3,2,1,0:T(8,128)} %param.47) | copy-start | bytes 3145732
  7.2 17.1 %copy-start.24 = (s32[1,1,4]{2,1,0:T(1,128)S(1)}, s32[1,1,4]{2,1,0:T(1,128)}, u32[]{:S(2)}) copy-start(s32[1,1,4]{2,1,0:T(1,128)} %param.37) | copy-start | bytes 52
  7.2 191.2 %all-reduce.7.cloned.1.call-start = ((), (), s32[]{:S(2)}) async-start(), calls=%async_computation.1 | async-start | bytes 1048576 | tf_op jit(solution)/shard_map/psum | solution.py:133
  41.5 0.7 copy-start.17
  43.7 11.1 %copy-start.1 = (f32[1,1,4,64,1024]{4,3,2,1,0:T(8,128)S(1)}, f32[1,1,4,64,1024]{4,3,2,1,0:T(8,128)}, u32[]{:S(2)}) copy-start(f32[1,1,4,64,1024]{4,3,2,1,0:T(8,128)} %param.48) | copy-start | bytes 3145732
  54.1 0.7 copy-start.18
  56.1 2.4 copy-start.3
  56.5 2.3 copy-start.2
  58.6 296.8 %all-reduce.5.cloned.1.call-start = ((), (), s32[]{:S(2)}) async-start(), calls=%async_computation | async-start | bytes 1048576 | tf_op jit(solution)/shard_map/psum | solution.py:129
  60.6 2.2 copy-start.22
  60.8 137.6 %copy-start.9 = (f32[64,2048]{1,0:T(8,128)S(1)}, f32[64,2048]{1,0:T(8,128)}, u32[]{:S(2)}) copy-start(f32[64,2048]{1,0:T(8,128)} %param.44) | copy-start | bytes 1572868
  61.3 138.8 %copy-start.4 = (f32[64,1024]{1,0:T(8,128)S(1)}, f32[64,1024]{1,0:T(8,128)}, u32[]{:S(2)}) copy-start(f32[64,1024]{1,0:T(8,128)} %copy-done.3) | copy-start | bytes 786436
  62.7 464.7 %all-reduce.11.cloned.1.call-start = ((), (), s32[]{:S(2)}) async-start(), calls=%async_computation.3 | async-start | bytes 1048576 | tf_op jit(solution)/shard_map/psum | solution.py:133
  200.1 155.2 %copy-start.14 = (f32[64,2048]{1,0:T(8,128)S(1)}, f32[64,2048]{1,0:T(8,128)}, u32[]{:S(2)}) copy-start(f32[64,2048]{1,0:T(8,128)} %param.42) | copy-start | bytes 1572868
  201.5 155.5 %copy-start.8 = (f32[64,1024]{1,0:T(8,128)S(1)}, f32[64,1024]{1,0:T(8,128)}, u32[]{:S(2)}) copy-start(f32[64,1024]{1,0:T(8,128)} %get-tuple-element.260) | copy-start | bytes 786436
  357.1 1.0 copy-start.7
  357.1 1.1 copy-start.21
  358.2 10.0 %copy-start.6 = (f32[64,1024]{1,0:T(8,128)S(1)}, f32[64,1024]{1,0:T(8,128)}, u32[]{:S(2)}) copy-start(f32[64,1024]{1,0:T(8,128)} %get-tuple-element.262) | copy-start | bytes 786436
  368.2 11.8 %copy-start.5 = (f32[64,1024]{1,0:T(8,128)S(1)}, f32[64,1024]{1,0:T(8,128)}, u32[]{:S(2)}) copy-start(f32[64,1024]{1,0:T(8,128)} %get-tuple-element.236) | copy-start | bytes 786436
  378.4 0.7 copy-start.19
  386.5 0.7 copy-start.20
  390.7 293.5 %all-reduce.9.cloned.1.call-start = ((), (), s32[]{:S(2)}) async-start(), calls=%async_computation.2 | async-start | bytes 1048576 | tf_op jit(solution)/shard_map/psum | solution.py:129
  395.0 132.4 %copy-start.10 = (f32[64,2048]{1,0:T(8,128)S(1)}, f32[64,2048]{1,0:T(8,128)}, u32[]{:S(2)}) copy-start(f32[64,2048]{1,0:T(8,128)} %param.44) | copy-start | bytes 1572868
  395.0 132.4 %copy-start.11 = (f32[64,2048]{1,0:T(8,128)S(1)}, f32[64,2048]{1,0:T(8,128)}, u32[]{:S(2)}) copy-start(f32[64,2048]{1,0:T(8,128)} %param.46) | copy-start | bytes 1572868
  395.0 132.4 %copy-start.12 = (f32[64,2048]{1,0:T(8,128)S(1)}, f32[64,2048]{1,0:T(8,128)}, u32[]{:S(2)}) copy-start(f32[64,2048]{1,0:T(8,128)} %param.45) | copy-start | bytes 1572868
  395.0 132.4 %copy-start.13 = (f32[64,2048]{1,0:T(8,128)S(1)}, f32[64,2048]{1,0:T(8,128)}, u32[]{:S(2)}) copy-start(f32[64,2048]{1,0:T(8,128)} %param.43) | copy-start | bytes 1572868
  395.8 288.4 %copy-start.15 = (f32[64,2048]{1,0:T(8,128)S(1)}, f32[64,2048]{1,0:T(8,128)}, u32[]{:S(2)}) copy-start(f32[64,2048]{1,0:T(8,128)} %param.42) | copy-start | bytes 1572868
Sparse Core Ops, SparseCore 0:
  58.7 139.6 all-reduce.6
  201.8 153.5 all-reduce.4
  390.8 136.5 all-reduce.10
  530.6 153.4 all-reduce.8
where the time goes:
time: 695 us; the launch traced here: 693 us
  waiting for transfers between devices  479 us (69%)
  blocking collectives  89.9 us (13%)
  matrix products  38.7 us (6%)
  other arithmetic  30 us (4%)
  between operations  22.6 us (3%)
  local copies, waits for them, and re-layouts  22.4 us (3%)
  loops' own time  11 us (2%)
    psum x2, waiting for transfers between devices, per_device(): col_total = lax.psum(col_terms, 'row')  308 us
    psum x2, waiting for transfers between devices, per_device(): row_total = lax.psum(row_terms, 'col')  170 us
    psum x1, blocking collectives, per_device(): occupancy = lax.psum(occupancy, ('row', 'col'))  89.9 us
    dot_general x6, matrix products, project_block(): jnp.dot(merged_input, inverse_t, preferred_element_type=jnp.float32)  24.7 us
  transfers between devices with their start and end apart: 4, of which 4 were waited for; matrix products, arithmetic and copies ran while one was open for 2% of the time, Pallas kernels for 0%

commit v1 on v0

--- a/solution.py
+++ b/solution.py
@@ -1,9 +1,136 @@
+import functools
+
 import jax
 import jax.numpy as jnp
 from jax import lax
+from jax.experimental import pallas as pl
+from jax.experimental.pallas import tpu as pltpu
 from jax.sharding import PartitionSpec as P
 
 ITERS = 2
+MESH = pl.DeviceIdType.MESH
+AXES = ("row", "col")
+
+
+def peer_id(axis, peer):
+    if axis == "row":
+        return (peer, lax.axis_index("col"))
+    return (lax.axis_index("row"), peer)
+
+
+def reduce_kernel(n, group_axes, *refs):
+    groups = len(group_axes)
+    ins = refs[:groups]
+    outs = refs[groups : 2 * groups]
+    scratch = refs[2 * groups :]
+    per = [scratch[6 * g : 6 * g + 6] for g in range(groups)]
+    barrier = pltpu.get_barrier_semaphore()
+    for axis in group_axes:
+        me = lax.axis_index(axis)
+        for k in range(1, n):
+            peer = lax.rem(me + k, n)
+            pl.semaphore_signal(barrier, inc=1, device_id=peer_id(axis, peer), device_id_type=MESH)
+    pl.semaphore_wait(barrier, groups * (n - 1))
+
+    width = ins[0].shape[1] // n
+
+    def cols(index):
+        return pl.ds(pl.multiple_of(index * width, width), width)
+
+    scatter = []
+    for g, axis in enumerate(group_axes):
+        recv, gathered, s1, r1, s2, r2 = per[g]
+        me = lax.axis_index(axis)
+        copies = []
+        for k in range(1, n):
+            peer = lax.rem(me + k, n)
+            copy = pltpu.make_async_remote_copy(
+                src_ref=ins[g].at[:, cols(peer)],
+                dst_ref=recv.at[me],
+                send_sem=s1.at[peer],
+                recv_sem=r1.at[me],
+                device_id=peer_id(axis, peer),
+                device_id_type=MESH,
+            )
+            copy.start()
+            copies.append(copy)
+        scatter.append(copies)
+
+    gathers = []
+    for g, axis in enumerate(group_axes):
+        recv, gathered, s1, r1, s2, r2 = per[g]
+        me = lax.axis_index(axis)
+        for k in range(1, n):
+            source = lax.rem(me + n - k, n)
+            pltpu.make_async_remote_copy(
+                src_ref=ins[g].at[:, cols(source)],
+                dst_ref=recv.at[source],
+                send_sem=s1.at[source],
+                recv_sem=r1.at[source],
+                device_id=peer_id(axis, source),
+                device_id_type=MESH,
+            ).wait_recv()
+        total = ins[g][:, cols(me)]
+        for k in range(1, n):
+            total = total + recv[lax.rem(me + k, n)]
+        gathered[me] = total
+        copies = []
+        for k in range(1, n):
+            peer = lax.rem(me + k, n)
+            copy = pltpu.make_async_remote_copy(
+                src_ref=gathered.at[me],
+                dst_ref=gathered.at[me],
+                send_sem=s2.at[peer],
+                recv_sem=r2.at[me],
+                device_id=peer_id(axis, peer),
+                device_id_type=MESH,
+            )
+            copy.start()
+            copies.append(copy)
+        gathers.append(copies)
+
+    for g, axis in enumerate(group_axes):
+        recv, gathered, s1, r1, s2, r2 = per[g]
+        me = lax.axis_index(axis)
+        for copy in scatter[g]:
+            copy.wait_send()
+        for k in range(1, n):
+            source = lax.rem(me + n - k, n)
+            pltpu.make_async_remote_copy(
+                src_ref=gathered.at[source],
+                dst_ref=gathered.at[source],
+                send_sem=s2.at[source],
+                recv_sem=r2.at[source],
+                device_id=peer_id(axis, source),
+                device_id_type=MESH,
+            ).wait_recv()
+        for copy in gathers[g]:
+            copy.wait_send()
+        for index in range(n):
+            outs[g][:, index * width : (index + 1) * width] = gathered[index]
+
+
+def all_reduce(arrays, group_axes, n, collective_id):
+    shapes = [a.shape for a in arrays]
+    width = shapes[0][1] // n
+    scratch = []
+    for rows, _ in shapes:
+        scratch += [
+            pltpu.VMEM((n, rows, width), jnp.float32),
+            pltpu.VMEM((n, rows, width), jnp.float32),
+            pltpu.SemaphoreType.DMA((n,)),
+            pltpu.SemaphoreType.DMA((n,)),
+            pltpu.SemaphoreType.DMA((n,)),
+            pltpu.SemaphoreType.DMA((n,)),
+        ]
+    return pl.pallas_call(
+        functools.partial(reduce_kernel, n, group_axes),
+        out_shape=tuple(jax.ShapeDtypeStruct(s, jnp.float32) for s in shapes),
+        in_specs=[pl.BlockSpec(memory_space=pltpu.VMEM)] * len(arrays),
+        out_specs=tuple(pl.BlockSpec(memory_space=pltpu.VMEM) for _ in arrays),
+        scratch_shapes=scratch,
+        compiler_params=pltpu.CompilerParams(collective_id=collective_id, has_side_effects=True),
+    )(*arrays)
 
 
 def project_block(
@@ -44,31 +171,12 @@
     col_blocks = column_values.shape[1] // block_width
     row_blocks = row_values.shape[1] // block_width
     slot_total = block_rows.shape[2]
+    n_row = lax.axis_size("row")
+    n_col = lax.axis_size("col")
     rows_here = block_rows[0, 0]
     cols_here = block_cols[0, 0]
     tiles_here = block_tiles[0, 0]
     live_slot = jnp.arange(slot_total, dtype=jnp.int32) < block_count[0, 0]
-    row_grid = row_blocks * lax.axis_size("row")
-    col_grid = col_blocks * lax.axis_size("col")
-    global_rows = lax.axis_index("row") * row_blocks + rows_here
-    global_cols = lax.axis_index("col") * col_blocks + cols_here
-    row_onehot = (
-        (jnp.arange(row_grid, dtype=jnp.int32)[None, :] == global_rows[:, None])
-        & live_slot[:, None]
-    ).astype(jnp.float32)
-    col_onehot = (jnp.arange(col_grid, dtype=jnp.int32)[None, :] == global_cols[:, None]).astype(
-        jnp.float32
-    )
-    occupancy = jnp.dot(row_onehot.T, col_onehot, precision=lax.Precision.HIGHEST)
-    occupancy = lax.psum(occupancy, ("row", "col"))
-    col_count = lax.dynamic_slice_in_dim(
-        jnp.sum(occupancy, axis=0), lax.axis_index("col") * col_blocks, col_blocks, 0
-    )
-    row_count = lax.dynamic_slice_in_dim(
-        jnp.sum(occupancy, axis=1), lax.axis_index("row") * row_blocks, row_blocks, 0
-    )
-    col_denom = (1.0 + jnp.repeat(col_count, block_width))[None, :]
-    row_denom = (1.0 + jnp.repeat(row_count, block_width))[None, :]
     x_own = column_values
     x_dual = column_duals
     y_state = row_values
@@ -78,12 +186,16 @@
     image_duals = [image_dual[0, 0, slot_index] for slot_index in range(slot_total)]
     input_duals = [input_dual[0, 0, slot_index] for slot_index in range(slot_total)]
     zero_block = jnp.zeros((scenarios, block_width), jnp.float32)
+    col_denom = None
+    row_denom = None
     for iteration in range(ITERS):
         x_half = jnp.clip(x_own - x_dual - unit_cost, 0.0, capacity)
         y_half = jnp.clip(y_state - y_dual, row_lower, row_upper)
         y_anchor = y_half + y_dual
         col_terms = jnp.zeros((scenarios, col_blocks, block_width), jnp.float32)
         row_terms = jnp.zeros((scenarios, row_blocks, block_width), jnp.float32)
+        col_live = jnp.zeros((col_blocks,), jnp.float32)
+        row_live = jnp.zeros((row_blocks,), jnp.float32)
         projected = []
         for slot_index in range(slot_total):
 
@@ -117,6 +229,8 @@
                 (jnp.arange(row_blocks, dtype=jnp.int32) == rows_here[slot_index])
                 & live_slot[slot_index]
             ).astype(jnp.float32)
+            col_live = col_live + col_pick
+            row_live = row_live + row_pick
             col_terms = (
                 col_terms + col_pick[None, :, None] * (x_proj + input_duals[slot_index])[:, None, :]
             )
@@ -126,11 +240,31 @@
             projected.append((x_proj, y_proj))
         col_terms = col_terms.reshape(scenarios, col_blocks * block_width)
         row_terms = row_terms.reshape(scenarios, row_blocks * block_width)
-        col_total = lax.psum(col_terms, "row")
+        if iteration == 0:
+            col_extra = jnp.zeros((8, col_blocks * block_width), jnp.float32).at[0].set(
+                jnp.repeat(col_live, block_width)
+            )
+            row_extra = jnp.zeros((8, row_blocks * block_width), jnp.float32).at[0].set(
+                jnp.repeat(row_live, block_width)
+            )
+            col_total, row_total = all_reduce(
+                [
+                    jnp.concatenate([col_terms, col_extra], axis=0),
+                    jnp.concatenate([row_terms, row_extra], axis=0),
+                ],
+                AXES,
+                n_row,
+                0,
+            )
+            col_denom = 1.0 + col_total[scenarios : scenarios + 1]
+            row_denom = 1.0 + row_total[scenarios : scenarios + 1]
+            col_total = col_total[:scenarios]
+            row_total = row_total[:scenarios]
+        else:
+            col_total, row_total = all_reduce([col_terms, row_terms], AXES, n_row, 1)
         x_own = (x_half + x_dual + col_total) / col_denom
         x_dual = x_dual + x_half - x_own
         x_full = x_own
-        row_total = lax.psum(row_terms, "col")
         shift_full = (row_total - y_anchor) / row_denom
         y_state = y_anchor + shift_full
         y_dual = y_dual + y_half - y_state

time: 695 us -> 220 us (0.32)
  waiting for transfers between devices: 479 us -> 0 us
  Pallas kernels: 0 us -> 103 us
  blocking collectives: 89.9 us -> 0 us
  between operations: 22.6 us -> 9.8 us
    psum x4 -> x0, waiting for transfers between devices: 479 us -> none  [the longest x2 308 us: per_device(): col_total = lax.psum(col_terms, 'row')]
    pallas_call x0 -> x2, Pallas kernels: none -> 103 us  [all_reduce(): pl.pallas_call(functools.partial(reduce_kernel, n, group_axes), out_shape...]
    psum x1 -> x0, blocking collectives: 89.9 us -> none  [per_device(): occupancy = lax.psum(occupancy, ('row', 'col'))]
    add x4 -> x3, other arithmetic: 1.41 us -> 9.31 us  [the longest x1 7.56 us: per_device(): row_live = row_live + row_pick]
    convert_element_type x4 -> x0, other arithmetic: 7.44 us -> none  [per_device(): row_pick = ((jnp.arange(row_blocks, dtype=jnp.int32) == rows_here[slot_in...]
  transfers between devices with their start and end apart: 4 -> 0, of which waited for: 4 -> 0; matrix products, arithmetic and copies ran while one was open for 2% -> 0% of each run, Pallas kernels for 0% -> 0%
where the time goes in v1:
time: 220 us; the launch traced here: 218 us
  Pallas kernels  103 us (47%)
  matrix products  38.5 us (18%)
  other arithmetic  33.6 us (15%)
  local copies, waits for them, and re-layouts  23.6 us (11%)
  loops' own time  10.3 us (5%)
  between operations  9.8 us (4%)
    pallas_call x2, Pallas kernels, all_reduce(): pl.pallas_call(functools.partial(reduce_kernel, n, group_axes), out_shape...  103 us
    dot_general x6, matrix products, project_block(): jnp.dot(merged_input, inverse_t, preferred_element_type=jnp.float32)  24.8 us
    dot_general x6, matrix products, project_block(): jnp.dot(x_proj.astype(jnp.bfloat16), matrix_t, preferred_element_type=jnp...  13.7 us
    another operation x8, loops' own time, per_device(): x_proj, y_proj = lax.cond(live_slot[slot_index], active, skipped)  10.3 us
    unnamed x106, local copies, waits for them, and re-layouts  8.43 us
    add x1, other arithmetic, per_device(): row_live = row_live + row_pick  7.56 us
    add x5, other arithmetic, per_device(): y_proj + image_duals[slot_index]  5.5 us
    add x5, other arithmetic, per_device(): x_proj + input_duals[slot_index]  5.24 us

profile of v1, /device:TPU:1, one launch (start us, length us, event | category | flops | bytes accessed | tf_op | source)
XLA Modules:
  0.0 218.5 jit_solution(14378555512505308446)
XLA Ops:
  1.4 0.6 fusion.215
  4.6 1.5 fusion.213
  8.6 1.5 fusion.214
  12.6 7.6 %add_add_fusion = (f32[2]{0:T(128)S(1)}, f32[2]{0:T(128)S(1)}, f32[2]{0:T(128)S(1)}, f32[2]{0:T(128)S(1)}, f32[2]{0:T(128)S(1)}, /*index=5*/f32[2]{0:T(128)S(1)}...) fusion(pred[]{:T(512)} %bitcast.44, s32[]{:T(128)} %bitcast.56, pred[]{:T(512)} %bitcast.38, s32[]{:T(128)} %bitcast.55, ...), kind=kLoop, calls=%fused_computation.202 | loop fusion | flops 60 | bytes 116 | tf_op jit(solution)/shard_map/add | solution.py:233
  20.9 2.4 %slice_bitcast_fusion.6 = (f32[64,1024]{1,0:T(8,128)S(1)}, f32[64,1024]{1,0:T(8,128)S(1)}, f32[64,1024]{1,0:T(8,128)S(1)}, f32[64,1024]{1,0:T(8,128)S(1)}, f32[6...) fusion(f32[1,1,4,64,1024]{4,3,2,1,0:T(8,128)} %param.52, ...), kind=kLoop, calls=%fused_computation.172 | loop fusion | bytes 4194304 | tf_op jit(solution)/shard_map/squeeze | solution.py:186
  23.3 7.2 %conditional.8 = (f32[64,1024]{1,0:T(8,128)}, f32[64,1024]{1,0:T(8,128)}) conditional(s32[]{:T(128)} %convert_element_type.153, () %tuple.80, (s32[4]{0:T(128)S(1)}, f32[64,2048]{1,0:T(8,128)S(1)}, f32[64,1024]{1,0:T(8,128)}, f32[1,1,4,64,1024]{4,3,2,1,0:T(8,128)S(1)}, f32[64,1024]{1,0:T(8,128)S(1)}, /*index=5*/s32[4]{0:T(128)S(1)}, ...), branch_computations={%region_0.1_spmd, %region_1.2_spmd} | conditional | flops 403046400 | bytes 8128100 | solution.py:223
  23.5 4.2 %fusion = f32[64,1024]{1,0:T(8,128)} fusion(bf16[2,1024,1024]{2,1,0:T(8,128)(2,1)} %get-tuple-element.167, s32[]{:T(128)S(6)} %select_n.58, bf16[2,1024,1024]{2,1,0:T(8,128)(2,1)} %get-tuple-element.165, f32[64,1024]{1,0:T(8,128)} %get-tuple-element.162, f32[64,2048]{1,0:T(8,128)S(1)} %get-tuple-element.160, s32[]{:T(128)S(6)} %select_n.57, ...), kind=kOutput, calls=%fused_computation | convolution fusion | flops 268763136 | bytes 5506560 | tf_op jit(solution)/shard_map/cond/branch_1_fun/dot_general | solution.py:145
  27.7 2.9 %fusion.2 = f32[64,1024]{1,0:T(8,128)} fusion(bf16[2,1024,1024]{2,1,0:T(8,128)(2,1)} %get-tuple-element.165, s32[]{:T(128)S(6)} %select_n.58, f32[64,1024]{1,0:T(8,128)} %fusion), kind=kOutput, calls=%fused_computation.2 | convolution fusion | flops 134283264 | bytes 2621444 | tf_op jit(solution)/shard_map/cond/branch_1_fun/dot_general | solution.py:146
  30.5 10.0 %conditional.9 = (f32[64,1024]{1,0:T(8,128)}, f32[64,1024]{1,0:T(8,128)S(1)}) conditional(s32[]{:T(128)} %convert_element_type.155, () %tuple.82, (s32[4]{0:T(128)S(1)}, f32[64,2048]{1,0:T(8,128)S(1)}, f32[64,1024]{1,0:T(8,128)S(1)}, f32[1,1,4,64,1024]{4,3,2,1,0:T(8,128)S(1)}, f32[64,1024]{1,0:T(8,128)S(1)}, /*index=5*/s32[4]{0:T(128)S(1)}, ...), branch_computations={%region_2.3_spmd, %region_3.4_spmd} | conditional | flops 403046400 | bytes 8128116 | solution.py:223
  33.1 0.6 slice.111
  34.3 4.1 %fusion.26 = f32[64,1024]{1,0:T(8,128)} fusion(bf16[2,1024,1024]{2,1,0:T(8,128)(2,1)} %get-tuple-element.175, s32[]{:T(128)S(6)} %select_n.60, bf16[2,1024,1024]{2,1,0:T(8,128)(2,1)} %get-tuple-element.173, f32[64,1024]{1,0:T(8,128)S(1)} %get-tuple-element.170, f32[64,2048]{1,0:T(8,128)S(1)} %get-tuple-element.168, s32[]{:T(128)S(6)} %select_n.59, ...), kind=kOutput, calls=%fused_computation.18 | convolution fusion | flops 268763136 | bytes 5506560 | tf_op jit(solution)/shard_map/cond/branch_1_fun/dot_general | solution.py:145
  38.4 2.2 fusion.28
  40.6 0.7 copy-done.26
  41.3 0.7 conditional.11
  41.3 0.7 broadcast_in_dim.12
  42.0 0.7 copy-done.27
  42.7 9.8 %conditional.10 = (f32[64,1024]{1,0:T(8,128)}, f32[64,1024]{1,0:T(8,128)S(1)}) conditional(s32[]{:T(128)} %convert_element_type.157, () %tuple.84, (s32[4]{0:T(128)S(1)}, f32[64,2048]{1,0:T(8,128)S(1)}, f32[64,1024]{1,0:T(8,128)S(1)}, f32[1,1,4,64,1024]{4,3,2,1,0:T(8,128)}, f32[64,1024]{1,0:T(8,128)S(1)}, /*index=5*/s32[4]{0:T(128)S(1)}, ...), branch_computations={%region_4.5_spmd, %region_5.6_spmd} | conditional | flops 403046400 | bytes 8128116 | solution.py:223
  42.7 0.6 slice.180
  45.1 0.6 slice.178
  46.2 4.1 %fusion.52 = f32[64,1024]{1,0:T(8,128)} fusion(bf16[2,1024,1024]{2,1,0:T(8,128)(2,1)} %get-tuple-element.183, s32[]{:T(128)S(6)} %select_n.62, bf16[2,1024,1024]{2,1,0:T(8,128)(2,1)} %get-tuple-element.181, f32[64,1024]{1,0:T(8,128)S(1)} %get-tuple-element.178, f32[64,2048]{1,0:T(8,128)S(1)} %get-tuple-element.176, s32[]{:T(128)S(6)} %select_n.61, ...), kind=kOutput, calls=%fused_computation.36 | convolution fusion | flops 268763136 | bytes 5506560 | tf_op jit(solution)/shard_map/cond/branch_1_fun/dot_general | solution.py:145
  50.3 2.2 fusion.54
  52.5 0.7 copy-done.28
  53.2 1.3 fusion.201
  54.6 1.6 fusion.202
  57.8 0.9 select_maximum_fusion.refs_1_
  60.4 0.9 select_maximum_fusion.1.refs_0_
  61.3 51.0 %shard_map.176 = (f32[72,2048]{1,0:T(8,128)}, f32[72,2048]{1,0:T(8,128)}) custom-call(f32[72,2048]{1,0:T(8,128)} %select_maximum_fusion.1.refs_0_, f32[72,2048]{1,0:T(8,128)} %select_maximum_fusion.refs_1_), custom_call_target="tpu_custom_call" | custom-call | tf_op jit(solution)/shard_map/pallas_call | solution.py:126
  112.3 0.9 slice_add_fusion.1
  113.2 0.8 slice_add_fusion
  114.1 1.4 add_divide_fusion
  115.8 1.7 subtract_divide_fusion
  117.6 1.1 fusion.209
  118.7 10.1 %conditional.13 = (f32[64,1024]{1,0:T(8,128)}, f32[64,1024]{1,0:T(8,128)S(1)}) conditional(s32[]{:T(128)} %convert_element_type.155, () %tuple.90, (s32[4]{0:T(128)S(1)}, f32[64,2048]{1,0:T(8,128)S(1)}, f32[64,1024]{1,0:T(8,128)S(1)}, f32[64,1024]{1,0:T(8,128)}, f32[64,1024]{1,0:T(8,128)S(1)}, /*index=5*/s32[4]{0:T(128)S(1)}, ...), branch_computations={%region_10.11_spmd, %region_11.12_spmd} | conditional | flops 403046400 | bytes 8128116 | solution.py:223
  118.7 0.6 slice.187
  121.2 0.6 slice.186
  122.5 4.1 %fusion.127 = f32[64,1024]{1,0:T(8,128)} fusion(bf16[2,1024,1024]{2,1,0:T(8,128)(2,1)} %get-tuple-element.207, s32[]{:T(128)S(6)} %select_n.68, bf16[2,1024,1024]{2,1,0:T(8,128)(2,1)} %get-tuple-element.205, f32[64,1024]{1,0:T(8,128)S(1)} %get-tuple-element.202, f32[64,2048]{1,0:T(8,128)S(1)} %get-tuple-element.200, s32[]{:T(128)S(6)} %select_n.67, ...), kind=kOutput, calls=%fused_computation.89 | convolution fusion | flops 268763136 | bytes 5506560 | tf_op jit(solution)/shard_map/cond/branch_1_fun/dot_general | solution.py:145
  126.6 2.2 fusion.129
  128.8 0.7 copy-done.29
  129.5 1.0 add.304
  130.5 1.0 add.315
  131.5 10.1 %conditional.14 = (f32[64,1024]{1,0:T(8,128)}, f32[64,1024]{1,0:T(8,128)S(1)}) conditional(s32[]{:T(128)} %convert_element_type.157, () %tuple.92, (s32[4]{0:T(128)S(1)}, f32[64,2048]{1,0:T(8,128)S(1)}, f32[64,1024]{1,0:T(8,128)S(1)}, f32[64,1024]{1,0:T(8,128)}, f32[64,1024]{1,0:T(8,128)S(1)}, /*index=5*/s32[4]{0:T(128)S(1)}, ...), branch_computations={%region_12.13_spmd, %region_13.14_spmd} | conditional | flops 403046400 | bytes 8128116 | solution.py:223
  131.5 0.6 slice.189
  134.0 0.6 slice.188
  135.3 4.1 %fusion.150 = f32[64,1024]{1,0:T(8,128)} fusion(bf16[2,1024,1024]{2,1,0:T(8,128)(2,1)} %get-tuple-element.215, s32[]{:T(128)S(6)} %select_n.70, bf16[2,1024,1024]{2,1,0:T(8,128)(2,1)} %get-tuple-element.213, f32[64,1024]{1,0:T(8,128)S(1)} %get-tuple-element.210, f32[64,2048]{1,0:T(8,128)S(1)} %get-tuple-element.208, s32[]{:T(128)S(6)} %select_n.69, ...), kind=kOutput, calls=%fused_computation.106 | convolution fusion | flops 268763136 | bytes 5506560 | tf_op jit(solution)/shard_map/cond/branch_1_fun/dot_general | solution.py:145
  139.4 2.2 fusion.152
  141.6 0.7 copy-done.30
  142.3 1.0 add.308
  143.3 1.0 add.317
  144.3 0.8 conditional.15
  144.3 0.7 broadcast_in_dim.21
  145.1 0.7 copy-done.31
  145.8 1.0 add.312
  146.7 1.0 add.319
  147.7 6.5 %conditional.12 = (f32[64,1024]{1,0:T(8,128)}, f32[64,1024]{1,0:T(8,128)S(1)}) conditional(s32[]{:T(128)} %convert_element_type.153, () %tuple.88, (s32[4]{0:T(128)S(1)}, f32[64,2048]{1,0:T(8,128)S(1)}, f32[64,1024]{1,0:T(8,128)S(1)}, f32[64,1024]{1,0:T(8,128)}, f32[64,1024]{1,0:T(8,128)S(1)}, /*index=5*/s32[4]{0:T(128)S(1)}, ...), branch_computations={%region_8.9_spmd, %region_9.10_spmd} | conditional | flops 403046400 | bytes 8128100 | solution.py:223
  147.9 4.1 %fusion.104 = f32[64,1024]{1,0:T(8,128)} fusion(bf16[2,1024,1024]{2,1,0:T(8,128)(2,1)} %get-tuple-element.199, s32[]{:T(128)S(6)} %select_n.66, bf16[2,1024,1024]{2,1,0:T(8,128)(2,1)} %get-tuple-element.197, f32[64,1024]{1,0:T(8,128)S(1)} %get-tuple-element.194, f32[64,2048]{1,0:T(8,128)S(1)} %get-tuple-element.192, s32[]{:T(128)S(6)} %select_n.65, ...), kind=kOutput, calls=%fused_computation.72 | convolution fusion | flops 268763136 | bytes 5506560 | tf_op jit(solution)/shard_map/cond/branch_1_fun/dot_general | solution.py:145
  152.0 2.2 fusion.106
  154.2 0.7 copy-done.32
  154.9 1.0 add.301
  155.9 1.0 add.314
  159.4 1.0 multiply_add_fusion.refs_1_
  160.8 1.0 multiply_add_fusion.1.refs_0_
  161.7 51.6 %shard_map.177 = (f32[64,2048]{1,0:T(8,128)}, f32[64,2048]{1,0:T(8,128)}) custom-call(f32[64,2048]{1,0:T(8,128)} %multiply_add_fusion.1.refs_0_, f32[64,2048]{1,0:T(8,128)} %multiply_add_fusion.refs_1_), custom_call_target="tpu_custom_call" | custom-call | tf_op jit(solution)/shard_map/pallas_call | solution.py:126
  213.4 2.4 %fusion.200 = f32[64,2048]{1,0:T(8,128)} fusion(f32[64,2048]{1,0:T(8,128)S(1)} %copy-done.18, f32[64,2048]{1,0:T(8,128)S(1)} %copy-done.19, f32[64,2048]{1,0:T(8,128)} %get-tuple-element.265, f32[2048]{0:T(1024)S(1)} %bitcast.321, f32[64,2048]{1,0:T(8,128)S(1)} %copy-done.17, f32[64,2048]{1,0:T(8,128)S(1)} %copy-done.20, f32[72,2048]{1,0:T(8,128)} %get-tuple-element.255), kind=kLoop, calls=%fused_computation.149 | loop fusion | flops 2490368 | bytes 3678208 | tf_op jit(solution)/shard_map/jit(clip)/min | solution.py:284
  215.8 2.7 %fusion.198 = f32[64,2048]{1,0:T(8,128)} fusion(f32[64,2048]{1,0:T(8,128)S(1)} %copy-done.22, f32[64,2048]{1,0:T(8,128)} %param.45, f32[64,2048]{1,0:T(8,128)} %get-tuple-element.264, f32[2048]{0:T(1024)S(1)} %bitcast.319, f32[64,2048]{1,0:T(8,128)} %param.44, f32[64,2048]{1,0:T(8,128)S(1)} %copy-done, f32[72,2048]{1,0:T(8,128)} %get-tuple-element.254), kind=kLoop, calls=%fused_computation.147 | loop fusion | flops 2621440 | bytes 3678208 | tf_op jit(solution)/shard_map/jit(clip)/min | solution.py:283
  (122 shorter events, 7.6 us)
Async XLA Ops:
  0.6 22.7 %copy-start = (f32[64,2048]{1,0:T(8,128)S(1)}, f32[64,2048]{1,0:T(8,128)}, u32[]{:S(2)}) copy-start(f32[64,2048]{1,0:T(8,128)} %param.43) | copy-start | bytes 1572868
  0.6 22.7 %copy-start.25 = (f32[1,1,4,64,1024]{4,3,2,1,0:T(8,128)S(1)}, f32[1,1,4,64,1024]{4,3,2,1,0:T(8,128)}, u32[]{:S(2)}) copy-start(f32[1,1,4,64,1024]{4,3,2,1,0:T(8,128)} %param.51) | copy-start | bytes 3145732
  0.7 22.7 %copy-start.33 = (s32[1,1,4]{2,1,0:T(1,128)S(1)}, s32[1,1,4]{2,1,0:T(1,128)}, u32[]{:S(2)}) copy-start(s32[1,1,4]{2,1,0:T(1,128)} %param.40) | copy-start | bytes 52
  0.7 22.7 %copy-start.34 = (s32[1,1,4]{2,1,0:T(1,128)S(1)}, s32[1,1,4]{2,1,0:T(1,128)}, u32[]{:S(2)}) copy-start(s32[1,1,4]{2,1,0:T(1,128)} %param.41) | copy-start | bytes 52
  40.6 0.7 copy-start.26
  42.0 0.7 copy-start.27
  42.7 10.5 %copy-start.1 = (f32[1,1,4,64,1024]{4,3,2,1,0:T(8,128)S(1)}, f32[1,1,4,64,1024]{4,3,2,1,0:T(8,128)}, u32[]{:S(2)}) copy-start(f32[1,1,4,64,1024]{4,3,2,1,0:T(8,128)} %param.53) | copy-start | bytes 3145732
  42.7 11.8 %copy-start.2 = (f32[1,1,4,64,1024]{4,3,2,1,0:T(8,128)S(1)}, f32[1,1,4,64,1024]{4,3,2,1,0:T(8,128)}, u32[]{:S(2)}) copy-start(f32[1,1,4,64,1024]{4,3,2,1,0:T(8,128)} %param.52) | copy-start | bytes 3145732
  52.5 0.7 copy-start.28
  54.5 4.5 %copy-start.3 = (f32[64,1024]{1,0:T(8,128)}, f32[64,1024]{1,0:T(8,128)S(1)}, u32[]{:S(2)}) copy-start(f32[64,1024]{1,0:T(8,128)S(1)} %get-tuple-element.289) | copy-start | bytes 786436
  54.5 4.9 %copy-start.5 = (f32[64,1024]{1,0:T(8,128)}, f32[64,1024]{1,0:T(8,128)S(1)}, u32[]{:S(2)}) copy-start(f32[64,1024]{1,0:T(8,128)S(1)} %get-tuple-element.290) | copy-start | bytes 786436
  54.6 5.3 %copy-start.7 = (f32[64,1024]{1,0:T(8,128)}, f32[64,1024]{1,0:T(8,128)S(1)}, u32[]{:S(2)}) copy-start(f32[64,1024]{1,0:T(8,128)S(1)} %get-tuple-element.291) | copy-start | bytes 786436
  56.2 1.6 copy-start.9
  56.2 1.6 copy-start.11
  56.2 1.6 copy-start.13
  56.2 1.6 copy-start.15
  59.4 54.6 %copy-start.21 = (f32[64,2048]{1,0:T(8,128)S(1)}, f32[64,2048]{1,0:T(8,128)}, u32[]{:S(2)}) copy-start(f32[64,2048]{1,0:T(8,128)} %param.46) | copy-start | bytes 1572868
  59.5 54.6 %copy-start.23 = (f32[64,2048]{1,0:T(8,128)S(1)}, f32[64,2048]{1,0:T(8,128)}, u32[]{:S(2)}) copy-start(f32[64,2048]{1,0:T(8,128)} %param.45) | copy-start | bytes 1572868
  60.2 55.4 %copy-start.4 = (f32[64,1024]{1,0:T(8,128)S(1)}, f32[64,1024]{1,0:T(8,128)}, u32[]{:S(2)}) copy-start(f32[64,1024]{1,0:T(8,128)} %copy-done.3) | copy-start | bytes 786436
  60.2 55.4 %copy-start.6 = (f32[64,1024]{1,0:T(8,128)S(1)}, f32[64,1024]{1,0:T(8,128)}, u32[]{:S(2)}) copy-start(f32[64,1024]{1,0:T(8,128)} %copy-done.5) | copy-start | bytes 786436
  60.2 55.4 %copy-start.8 = (f32[64,1024]{1,0:T(8,128)S(1)}, f32[64,1024]{1,0:T(8,128)}, u32[]{:S(2)}) copy-start(f32[64,1024]{1,0:T(8,128)} %copy-done.7) | copy-start | bytes 786436
  112.3 3.5 %copy-start.24 = (f32[72,2048]{1,0:T(8,128)S(1)}, f32[72,2048]{1,0:T(8,128)}, u32[]{:S(2)}) copy-start(f32[72,2048]{1,0:T(8,128)} %get-tuple-element.255) | copy-start | bytes 1769476
  114.1 3.4 %copy-start.10 = (f32[64,1024]{1,0:T(8,128)S(1)}, f32[64,1024]{1,0:T(8,128)}, u32[]{:S(2)}) copy-start(f32[64,1024]{1,0:T(8,128)} %copy-done.9) | copy-start | bytes 786436
  114.1 3.4 %copy-start.12 = (f32[64,1024]{1,0:T(8,128)S(1)}, f32[64,1024]{1,0:T(8,128)}, u32[]{:S(2)}) copy-start(f32[64,1024]{1,0:T(8,128)} %copy-done.11) | copy-start | bytes 786436
  114.1 3.4 %copy-start.14 = (f32[64,1024]{1,0:T(8,128)S(1)}, f32[64,1024]{1,0:T(8,128)}, u32[]{:S(2)}) copy-start(f32[64,1024]{1,0:T(8,128)} %copy-done.13) | copy-start | bytes 786436
  114.1 3.4 %copy-start.16 = (f32[64,1024]{1,0:T(8,128)S(1)}, f32[64,1024]{1,0:T(8,128)}, u32[]{:S(2)}) copy-start(f32[64,1024]{1,0:T(8,128)} %copy-done.15) | copy-start | bytes 786436
  128.8 0.7 copy-start.29
  141.6 0.7 copy-start.30
  145.0 0.7 copy-start.31
  154.2 0.7 copy-start.32
  159.4 53.9 %copy-start.17 = (f32[64,2048]{1,0:T(8,128)S(1)}, f32[64,2048]{1,0:T(8,128)}, u32[]{:S(2)}) copy-start(f32[64,2048]{1,0:T(8,128)} %param.48) | copy-start | bytes 1572868
  159.4 53.9 %copy-start.18 = (f32[64,2048]{1,0:T(8,128)S(1)}, f32[64,2048]{1,0:T(8,128)}, u32[]{:S(2)}) copy-start(f32[64,2048]{1,0:T(8,128)} %param.50) | copy-start | bytes 1572868
  159.4 53.9 %copy-start.19 = (f32[64,2048]{1,0:T(8,128)S(1)}, f32[64,2048]{1,0:T(8,128)}, u32[]{:S(2)}) copy-start(f32[64,2048]{1,0:T(8,128)} %param.49) | copy-start | bytes 1572868
  159.4 53.9 %copy-start.20 = (f32[64,2048]{1,0:T(8,128)S(1)}, f32[64,2048]{1,0:T(8,128)}, u32[]{:S(2)}) copy-start(f32[64,2048]{1,0:T(8,128)} %param.47) | copy-start | bytes 1572868
  160.6 55.2 %copy-start.22 = (f32[64,2048]{1,0:T(8,128)S(1)}, f32[64,2048]{1,0:T(8,128)}, u32[]{:S(2)}) copy-start(f32[64,2048]{1,0:T(8,128)} %param.46) | copy-start | bytes 1572868

commit v2 on v1

--- a/solution.py
+++ b/solution.py
@@ -133,18 +133,28 @@
     )(*arrays)
 
 
-def project_block(
-    x_full, matrix_t, inverse_t, image_now, image_gap_dual, input_now, column, block_width
-):
-    image_gap = (image_now - image_gap_dual).astype(jnp.bfloat16)
-    x_column = lax.dynamic_slice_in_dim(x_full, column * block_width, block_width, 1)
-    pulled = lax.dot_general(
-        image_gap, matrix_t, (((1,), (1,)), ((), ())), preferred_element_type=jnp.float32
-    )
-    merged_input = (x_column - input_now + pulled).astype(jnp.bfloat16)
-    x_proj = jnp.dot(merged_input, inverse_t, preferred_element_type=jnp.float32)
-    y_proj = jnp.dot(x_proj.astype(jnp.bfloat16), matrix_t, preferred_element_type=jnp.float32)
-    return (x_proj, y_proj)
+def pick_blocks(full, index, blocks, block_width):
+    parts = full.reshape(full.shape[0], blocks, block_width)
+    chosen = parts[:, 0][None]
+    for b in range(1, blocks):
+        chosen = jnp.where((index == b)[:, None, None], parts[:, b][None], chosen)
+    return chosen
+
+
+def by_tile(stacked, matrices, tiles, contract, slots):
+    results = [
+        lax.dot_general(
+            stacked, matrices[t], (((1,), (contract,)), ((), ())),
+            preferred_element_type=jnp.float32,
+        )
+        for t in range(matrices.shape[0])
+    ]
+    chosen = results[0].reshape(slots, -1, stacked.shape[1])
+    for t in range(1, len(results)):
+        chosen = jnp.where(
+            (tiles == t)[:, None, None], results[t].reshape(slots, -1, stacked.shape[1]), chosen
+        )
+    return chosen
 
 
 def per_device(
@@ -172,7 +182,6 @@
     row_blocks = row_values.shape[1] // block_width
     slot_total = block_rows.shape[2]
     n_row = lax.axis_size("row")
-    n_col = lax.axis_size("col")
     rows_here = block_rows[0, 0]
     cols_here = block_cols[0, 0]
     tiles_here = block_tiles[0, 0]
@@ -181,66 +190,37 @@
     x_dual = column_duals
     y_state = row_values
     y_dual = row_duals
-    x_full = column_values
-    images = [block_image[0, 0, slot_index] for slot_index in range(slot_total)]
-    image_duals = [image_dual[0, 0, slot_index] for slot_index in range(slot_total)]
-    input_duals = [input_dual[0, 0, slot_index] for slot_index in range(slot_total)]
-    zero_block = jnp.zeros((scenarios, block_width), jnp.float32)
+    images = block_image[0, 0]
+    image_duals = image_dual[0, 0]
+    input_duals = input_dual[0, 0]
+    col_mask = [(live_slot & (cols_here == b))[:, None, None] for b in range(col_blocks)]
+    row_mask = [(live_slot & (rows_here == b))[:, None, None] for b in range(row_blocks)]
     col_denom = None
     row_denom = None
     for iteration in range(ITERS):
         x_half = jnp.clip(x_own - x_dual - unit_cost, 0.0, capacity)
         y_half = jnp.clip(y_state - y_dual, row_lower, row_upper)
         y_anchor = y_half + y_dual
-        col_terms = jnp.zeros((scenarios, col_blocks, block_width), jnp.float32)
-        row_terms = jnp.zeros((scenarios, row_blocks, block_width), jnp.float32)
-        col_live = jnp.zeros((col_blocks,), jnp.float32)
-        row_live = jnp.zeros((row_blocks,), jnp.float32)
-        projected = []
-        for slot_index in range(slot_total):
-
-            def active(slot_index=slot_index):
-                matrix_t = lax.dynamic_index_in_dim(
-                    tile_matrix, tiles_here[slot_index], 0, keepdims=False
-                )
-                inverse_t = lax.dynamic_index_in_dim(
-                    tile_inverse, tiles_here[slot_index], 0, keepdims=False
-                )
-                return project_block(
-                    x_full,
-                    matrix_t,
-                    inverse_t,
-                    images[slot_index],
-                    image_duals[slot_index],
-                    input_duals[slot_index],
-                    cols_here[slot_index],
-                    block_width,
-                )
-
-            def skipped():
-                return (zero_block, zero_block)
-
-            x_proj, y_proj = lax.cond(live_slot[slot_index], active, skipped)
-            col_pick = (
-                (jnp.arange(col_blocks, dtype=jnp.int32) == cols_here[slot_index])
-                & live_slot[slot_index]
-            ).astype(jnp.float32)
-            row_pick = (
-                (jnp.arange(row_blocks, dtype=jnp.int32) == rows_here[slot_index])
-                & live_slot[slot_index]
-            ).astype(jnp.float32)
-            col_live = col_live + col_pick
-            row_live = row_live + row_pick
-            col_terms = (
-                col_terms + col_pick[None, :, None] * (x_proj + input_duals[slot_index])[:, None, :]
-            )
-            row_terms = (
-                row_terms + row_pick[None, :, None] * (y_proj + image_duals[slot_index])[:, None, :]
-            )
-            projected.append((x_proj, y_proj))
-        col_terms = col_terms.reshape(scenarios, col_blocks * block_width)
-        row_terms = row_terms.reshape(scenarios, row_blocks * block_width)
+        image_gap = (images - image_duals).astype(jnp.bfloat16).reshape(-1, block_width)
+        pulled = by_tile(image_gap, tile_matrix, tiles_here, 1, slot_total)
+        x_columns = pick_blocks(x_own, cols_here, col_blocks, block_width)
+        merged = (x_columns - input_duals + pulled).astype(jnp.bfloat16).reshape(-1, block_width)
+        x_proj = by_tile(merged, tile_inverse, tiles_here, 0, slot_total)
+        y_proj = by_tile(
+            x_proj.astype(jnp.bfloat16).reshape(-1, block_width), tile_matrix, tiles_here, 0,
+            slot_total,
+        )
+        x_terms = x_proj + input_duals
+        y_terms = y_proj + image_duals
+        col_terms = jnp.concatenate(
+            [jnp.sum(jnp.where(m, x_terms, 0.0), axis=0) for m in col_mask], axis=1
+        )
+        row_terms = jnp.concatenate(
+            [jnp.sum(jnp.where(m, y_terms, 0.0), axis=0) for m in row_mask], axis=1
+        )
         if iteration == 0:
+            col_live = jnp.stack([jnp.sum(m.astype(jnp.float32)) for m in col_mask])
+            row_live = jnp.stack([jnp.sum(m.astype(jnp.float32)) for m in row_mask])
             col_extra = jnp.zeros((8, col_blocks * block_width), jnp.float32).at[0].set(
                 jnp.repeat(col_live, block_width)
             )
@@ -264,22 +244,13 @@
             col_total, row_total = all_reduce([col_terms, row_terms], AXES, n_row, 1)
         x_own = (x_half + x_dual + col_total) / col_denom
         x_dual = x_dual + x_half - x_own
-        x_full = x_own
         shift_full = (row_total - y_anchor) / row_denom
         y_state = y_anchor + shift_full
         y_dual = y_dual + y_half - y_state
-        for slot_index in range(slot_total):
-            x_proj, y_proj = projected[slot_index]
-            x_column = lax.dynamic_slice_in_dim(
-                x_full, cols_here[slot_index] * block_width, block_width, 1
-            )
-            input_duals[slot_index] = input_duals[slot_index] + x_proj - x_column
-            shift_rows = lax.dynamic_slice_in_dim(
-                shift_full, rows_here[slot_index] * block_width, block_width, 1
-            )
-            new_image = y_proj + image_duals[slot_index] - shift_rows
-            image_duals[slot_index] = image_duals[slot_index] + y_proj - new_image
-            images[slot_index] = new_image
+        input_duals = input_duals + x_proj - pick_blocks(x_own, cols_here, col_blocks, block_width)
+        new_images = y_proj + image_duals - pick_blocks(shift_full, rows_here, row_blocks, block_width)
+        image_duals = image_duals + y_proj - new_images
+        images = new_images
     column_final = jnp.clip(x_own - x_dual - unit_cost, 0.0, capacity)
     row_final = jnp.clip(y_state - y_dual, row_lower, row_upper)
     return (column_final, row_final)

time: 220 us -> 136 us (0.62)
  the two profiles are of different devices: /device:TPU:1 before, /device:TPU:2 now
where the time goes in v2:
time: 136 us
  Pallas kernels  83.8 us (62%)
  other arithmetic  22.6 us (17%)
  matrix products  16 us (12%)
  local copies, waits for them, and re-layouts  11.5 us (8%)
  between operations  1.67 us (1%)
    pallas_call x2, Pallas kernels, all_reduce(): pl.pallas_call(functools.partial(reduce_kernel, n, group_axes), out_shape...  83.8 us
    dot_general x12, matrix products, by_tile(): lax.dot_general(stacked, matrices[t], (((1,), (contract,)), ((), ())), pr...  16 us
    reshape x3, local copies, waits for them, and re-layouts, pick_blocks(): parts = full.reshape(full.shape[0], blocks, block_width)  6.11 us
    slice x3, local copies, waits for them, and re-layouts, pick_blocks(): chosen = jnp.where((index == b)[:, None, None], parts[:, b][None], chosen)  3.98 us
    convert_element_type x2, other arithmetic, per_device(): (images - image_duals).astype(jnp.bfloat16).reshape(-1, block_width)  3.92 us
    min x1, other arithmetic, per_device(): column_final = jnp.clip(x_own - x_dual - unit_cost, 0.0, capacity)  2.73 us

profile of v2, /device:TPU:2, one launch (start us, length us, event | category | flops | bytes accessed | tf_op | source)
XLA Modules:
  0.0 135.5 jit_solution(18440177837642050424)
XLA Ops:
  1.3 0.7 compare_bitcast_fusion
  1.9 0.7 compare_bitcast_fusion.1
  2.6 1.4 %convert_reduce_fusion.1 = (f32[]{:T(128)}, pred[4]{0:T(512)(128)(4,1)S(1)}, f32[]{:T(128)}, pred[4]{0:T(512)(128)(4,1)S(1)}, f32[]{:T(128)}, /*index=5*/pred[4]...) fusion(s32[1,1,4]{2,1,0:T(1,128)} %param.23, s32[]{:T(128)} %bitcast.135, s32[1,1,4]{2,1,0:T(1,128)} %param.24), kind=kLoop, calls=%fused_computation.104 | loop fusion | flops 64 | bytes 68 | tf_op jit(solution)/shard_map/reduce_sum | solution.py:223
  4.0 1.4 %pad_maximum_fusion.3 = f32[2]{0:T(128)S(1)} fusion(f32[1]{0:T(128)} %bitcast.22, f32[1]{0:T(128)} %bitcast.21), kind=kLoop, calls=%fused_computation.102 | loop fusion | flops 2 | bytes 16 | tf_op jit(solution)/shard_map/stack | solution.py:223
  5.4 1.3 pad_maximum_fusion.2
  6.7 0.1 broadcast_bitcast_fusion.1
  6.7 0.1 broadcast_bitcast_fusion
  6.8 1.7 %fusion.79 = bf16[4,64,1024]{2,1,0:T(8,128)(2,1)S(1)} fusion(f32[1,1,4,64,1024]{4,3,2,1,0:T(8,128)} %param.35, f32[1,1,4,64,1024]{4,3,2,1,0:T(8,128)} %param.36), kind=kLoop, calls=%fused_computation.75 | loop fusion | flops 524288 | bytes 2621440 | tf_op jit(solution)/shard_map/convert_element_type | solution.py:204
  8.5 0.0 copy-start.1
  8.5 1.6 %reshape.198 = f32[64,2,1024]{2,1,0:T(2,128)S(1)} reshape(f32[64,2048]{1,0:T(8,128)} %param.27) | data formatting | bytes 1048576 | tf_op jit(solution)/shard_map/reshape | solution.py:137
  10.1 0.0 copy-start.10
  10.1 0.4 fusion.90
  10.5 0.1 copy_bitcast_fusion
  10.6 0.0 copy-start.15
  10.6 2.6 %fusion.14 = f32[4,64,1024]{2,1,0:T(8,128)S(1)} fusion(bf16[4,64,1024]{2,1,0:T(8,128)(2,1)S(1)} %fusion.79, bf16[2,1024,1024]{2,1,0:T(8,128)(2,1)} %param.21), kind=kOutput, calls=%fused_computation.14 | convolution fusion | flops 536870912 | bytes 3670016 | tf_op jit(solution)/shard_map/dot_general | solution.py:146
  13.2 0.0 copy-done.1
  13.3 0.0 copy-done.10
  13.3 0.9 fusion.69
  14.2 0.1 copy-done.15
  14.3 0.7 fusion.2
  15.1 1.9 %select_reduce_fusion.7 = (f32[64,1024]{1,0:T(8,128)S(1)}, f32[64,1024]{1,0:T(8,128)S(1)}, f32[4,64,1024]{2,1,0:T(8,128)}, bf16[4,64,1024]{2,1,0:T(8,128)(2,1)S(1)}) fusion(pred[4]{0:T(512)(128)(4,1)S(1)} %get-tuple-element.65, pred[4]{0:T(512)(128)(4,1)S(1)} %get-tuple-element.67, f32[1,1,4,64,1024]{4,3,2,1,0:T(8,128)S(1)} %copy-done.1, ...), kind=kOutput, calls=%fused_computation.62 | convolution fusion | flops 538574848 | bytes 6817280 | tf_op jit(solution)/shard_map/dot_general | solution.py:146
  17.0 0.9 select_maximum_fusion.1.refs_0_
  17.9 0.7 fusion.12
  18.6 0.0 copy-done.17
  18.6 0.0 copy-start.2
  18.6 0.0 copy-start.3
  18.6 0.0 copy-start.4
  18.6 0.0 copy-start.5
  18.6 2.0 %select_reduce_fusion.5 = (f32[64,1024]{1,0:T(8,128)S(1)}, f32[64,1024]{1,0:T(8,128)S(1)}, f32[4,64,1024]{2,1,0:T(8,128)}) fusion(pred[4]{0:T(512)(128)(4,1)S(1)} %get-tuple-element.43, pred[4]{0:T(512)(128)(4,1)S(1)} %get-tuple-element.58, f32[1,1,4,64,1024]{4,3,2,1,0:T(8,128)S(1)} %copy-done.17, f32[4,64,1024]{2,1,0:T(8,128)S(1)} %fusion.12, ...), kind=kOutput, calls=%fused_computation.60 | convolution fusion | flops 538312704 | bytes 6292992 | tf_op jit(solution)/shard_map/dot_general | solution.py:146
  20.6 0.9 select_maximum_fusion.refs_1_
  21.4 43.9 %shard_map.176 = (f32[72,2048]{1,0:T(8,128)}, f32[72,2048]{1,0:T(8,128)}) custom-call(f32[72,2048]{1,0:T(8,128)} %select_maximum_fusion.1.refs_0_, f32[72,2048]{1,0:T(8,128)} %select_maximum_fusion.refs_1_), custom_call_target="tpu_custom_call" | custom-call | tf_op jit(solution)/shard_map/pallas_call | solution.py:126
  65.3 0.8 slice_add_fusion.1
  66.2 0.8 slice_add_fusion
  67.0 0.0 copy-done.2
  67.0 0.0 copy-done.3
  67.1 0.0 copy-done.4
  67.1 0.0 copy-done.5
  67.1 0.0 copy-start
  67.1 0.0 copy-start.6
  67.1 2.1 %subtract_divide_fusion = f32[64,2048]{1,0:T(8,128)} fusion(f32[72,2048]{1,0:T(8,128)} %get-tuple-element.31, f32[2048]{0:T(1024)S(1)} %bitcast.146, f32[64,2048]{1,0:T(8,128)S(1)} %copy-done.2, f32[64,2048]{1,0:T(8,128)S(1)} %copy-done.3, f32[64,2048]{1,0:T(8,128)S(1)} %copy-done.4, f32[64,2048]{1,0:T(8,128)S(1)} %copy-done.5), kind=kLoop, calls=%fused_computation.78 | loop fusion | flops 786432 | bytes 3153920 | tf_op jit(solution)/shard_map/div | solution.py:247
  69.2 2.3 %reshape.202 = f32[64,2,1024]{2,1,0:T(2,128)} reshape(f32[64,2048]{1,0:T(8,128)} %subtract_divide_fusion) | data formatting | bytes 1048576 | tf_op jit(solution)/shard_map/reshape | solution.py:137
  71.5 1.8 %fusion.89 = (f32[64,1,1024]{2,1,0:T(1,128)S(1)}, f32[64,1,1024]{2,1,0:T(1,128)S(1)}) fusion(f32[64,2,1024]{2,1,0:T(2,128)} %reshape.202), kind=kLoop, calls=%fused_computation.111 | loop fusion | bytes 1048576 | tf_op jit(solution)/shard_map/slice | solution.py:140
  73.4 0.0 copy-start.13
  73.4 0.7 copy-done.13
  74.0 2.2 %subtract_convert_fusion = bf16[4,64,1024]{2,1,0:T(8,128)(2,1)} fusion(f32[4,64,1024]{2,1,0:T(8,128)} %get-tuple-element.62, f32[64,1024]{1,0:T(8,128)S(1)} %bitcast.138, f32[64,1024]{1,0:T(8,128)S(1)} %bitcast.136, pred[4]{0:T(512)(128)(4,1)S(1)} %compare_bitcast_fusion), kind=kLoop, calls=%fused_computation.56 | loop fusion | flops 1310720 | bytes 2097156 | tf_op jit(solution)/shard_map/convert_element_type | solution.py:204
  76.3 0.0 copy-done
  76.3 0.0 copy-done.6
  76.3 0.0 copy-done.7
  76.3 0.0 copy-done.8
  76.3 1.0 add_divide_fusion
  77.3 2.3 %reshape.201 = f32[64,2,1024]{2,1,0:T(2,128)} reshape(f32[64,2048]{1,0:T(8,128)} %add_divide_fusion) | data formatting | bytes 1048576 | tf_op jit(solution)/shard_map/reshape | solution.py:137
  79.6 1.8 %fusion.88 = (f32[64,1,1024]{2,1,0:T(1,128)S(1)}, f32[64,1,1024]{2,1,0:T(1,128)S(1)}) fusion(f32[64,2,1024]{2,1,0:T(2,128)} %reshape.201), kind=kLoop, calls=%fused_computation.110 | loop fusion | bytes 1048576 | tf_op jit(solution)/shard_map/slice | solution.py:140
  81.5 0.0 copy-start.16
  81.5 2.6 %fusion.10 = f32[4,64,1024]{2,1,0:T(8,128)S(1)} fusion(bf16[4,64,1024]{2,1,0:T(8,128)(2,1)} %subtract_convert_fusion, bf16[2,1024,1024]{2,1,0:T(8,128)(2,1)} %param.21), kind=kOutput, calls=%fused_computation.10 | convolution fusion | flops 536870912 | bytes 3670016 | tf_op jit(solution)/shard_map/dot_general | solution.py:146
  84.2 0.9 fusion.66
  85.1 0.7 fusion
  85.8 1.2 select_reduce_fusion.3
  87.1 0.8 pad_maximum_fusion.refs_0_
  87.9 0.7 fusion.8
  88.6 1.0 select_reduce_fusion.1
  89.6 0.8 pad_maximum_fusion.1.refs_1_
  90.4 39.9 %shard_map.177 = (f32[64,2048]{1,0:T(8,128)}, f32[64,2048]{1,0:T(8,128)}) custom-call(f32[64,2048]{1,0:T(8,128)} %pad_maximum_fusion.refs_0_, f32[64,2048]{1,0:T(8,128)} %pad_maximum_fusion.1.refs_1_), custom_call_target="tpu_custom_call" | custom-call | tf_op jit(solution)/shard_map/pallas_call | solution.py:126
  130.4 2.4 %fusion.78 = f32[64,2048]{1,0:T(8,128)} fusion(f32[64,2048]{1,0:T(8,128)S(1)} %copy-done.3, f32[64,2048]{1,0:T(8,128)S(1)} %copy-done.4, f32[64,2048]{1,0:T(8,128)} %get-tuple-element.33, f32[2048]{0:T(1024)S(1)} %bitcast.147, f32[64,2048]{1,0:T(8,128)S(1)} %copy-done.2, f32[64,2048]{1,0:T(8,128)S(1)} %copy-done.5, f32[72,2048]{1,0:T(8,128)} %get-tuple-element.31), kind=kLoop, calls=%fused_computation.74 | loop fusion | flops 2490368 | bytes 3678208 | tf_op jit(solution)/shard_map/jit(clip)/min | solution.py:255
  132.8 2.7 %fusion.76 = f32[64,2048]{1,0:T(8,128)} fusion(f32[64,2048]{1,0:T(8,128)S(1)} %copy-done.6, f32[64,2048]{1,0:T(8,128)} %param.29, f32[64,2048]{1,0:T(8,128)} %get-tuple-element.32, f32[2048]{0:T(1024)S(1)} %bitcast.145, f32[64,2048]{1,0:T(8,128)} %param.28, f32[64,2048]{1,0:T(8,128)S(1)} %copy-done, f32[72,2048]{1,0:T(8,128)} %get-tuple-element.30), kind=kLoop, calls=%fused_computation.72 | loop fusion | flops 2621440 | bytes 3678208 | tf_op jit(solution)/shard_map/jit(clip)/min | solution.py:254
  (22 shorter events, 0.2 us)
Async XLA Ops:
  8.5 4.7 %copy-start.1 = (f32[1,1,4,64,1024]{4,3,2,1,0:T(8,128)S(1)}, f32[1,1,4,64,1024]{4,3,2,1,0:T(8,128)}, u32[]{:S(2)}) copy-start(f32[1,1,4,64,1024]{4,3,2,1,0:T(8,128)} %param.37) | copy-start | bytes 3145732
  10.1 3.2 %copy-start.10 = (bf16[2,1024,1024]{2,1,0:T(8,128)(2,1)S(1)}, bf16[2,1024,1024]{2,1,0:T(8,128)(2,1)}, u32[]{:S(2)}) copy-start(bf16[2,1024,1024]{2,1,0:T(8,128)(2,1)} %param.21) | copy-start | bytes 12582916
  10.6 3.7 %copy-start.15 = (bf16[2,1024,1024]{2,1,0:T(8,128)(2,1)S(1)}, bf16[2,1024,1024]{2,1,0:T(8,128)(2,1)}, u32[]{:S(2)}) copy-start(bf16[2,1024,1024]{2,1,0:T(8,128)(2,1)} %param.22) | copy-start | bytes 12582916
  17.0 1.6 %copy-start.17 = (f32[1,1,4,64,1024]{4,3,2,1,0:T(8,128)S(1)}, f32[1,1,4,64,1024]{4,3,2,1,0:T(8,128)}, u32[]{:S(2)}) copy-start(f32[1,1,4,64,1024]{4,3,2,1,0:T(8,128)} %param.36) | copy-start | bytes 3145732
  18.6 48.5 %copy-start.2 = (f32[64,2048]{1,0:T(8,128)S(1)}, f32[64,2048]{1,0:T(8,128)}, u32[]{:S(2)}) copy-start(f32[64,2048]{1,0:T(8,128)} %param.32) | copy-start | bytes 1572868
  18.6 48.5 %copy-start.3 = (f32[64,2048]{1,0:T(8,128)S(1)}, f32[64,2048]{1,0:T(8,128)}, u32[]{:S(2)}) copy-start(f32[64,2048]{1,0:T(8,128)} %param.34) | copy-start | bytes 1572868
  18.6 48.4 %copy-start.4 = (f32[64,2048]{1,0:T(8,128)S(1)}, f32[64,2048]{1,0:T(8,128)}, u32[]{:S(2)}) copy-start(f32[64,2048]{1,0:T(8,128)} %param.33) | copy-start | bytes 1572868
  18.6 48.4 %copy-start.5 = (f32[64,2048]{1,0:T(8,128)S(1)}, f32[64,2048]{1,0:T(8,128)}, u32[]{:S(2)}) copy-start(f32[64,2048]{1,0:T(8,128)} %param.31) | copy-start | bytes 1572868
  67.1 9.2 %copy-start = (f32[64,2048]{1,0:T(8,128)S(1)}, f32[64,2048]{1,0:T(8,128)}, u32[]{:S(2)}) copy-start(f32[64,2048]{1,0:T(8,128)} %param.27) | copy-start | bytes 1572868
  67.1 9.2 %copy-start.6 = (f32[64,2048]{1,0:T(8,128)S(1)}, f32[64,2048]{1,0:T(8,128)}, u32[]{:S(2)}) copy-start(f32[64,2048]{1,0:T(8,128)} %param.30) | copy-start | bytes 1572868
  71.5 4.8 %copy-start.7 = (f32[64,2048]{1,0:T(8,128)S(1)}, f32[64,2048]{1,0:T(8,128)}, u32[]{:S(2)}) copy-start(f32[64,2048]{1,0:T(8,128)} %param.29) | copy-start | bytes 1572868
  71.5 4.8 %copy-start.8 = (f32[64,2048]{1,0:T(8,128)S(1)}, f32[64,2048]{1,0:T(8,128)}, u32[]{:S(2)}) copy-start(f32[64,2048]{1,0:T(8,128)} %param.28) | copy-start | bytes 1572868
  71.5 4.9 %copy-start.9 = (f32[72,2048]{1,0:T(8,128)S(1)}, f32[72,2048]{1,0:T(8,128)}, u32[]{:S(2)}) copy-start(f32[72,2048]{1,0:T(8,128)} %get-tuple-element.30) | copy-start | bytes 1769476
  73.4 0.7 copy-start.13
  79.6 4.6 %copy-start.11 = (bf16[2,1024,1024]{2,1,0:T(8,128)(2,1)S(1)}, bf16[2,1024,1024]{2,1,0:T(8,128)(2,1)}, u32[]{:S(2)}) copy-start(bf16[2,1024,1024]{2,1,0:T(8,128)(2,1)} %param.21) | copy-start | bytes 12582916
  79.6 4.6 %copy-start.18 = (f32[4,64,1024]{2,1,0:T(8,128)S(1)}, f32[4,64,1024]{2,1,0:T(8,128)}, u32[]{:S(2)}) copy-start(f32[4,64,1024]{2,1,0:T(8,128)} %get-tuple-element.46) | copy-start | bytes 3145732
  79.6 4.6 %copy-start.19 = (bf16[4,64,1024]{2,1,0:T(8,128)(2,1)S(1)}, bf16[4,64,1024]{2,1,0:T(8,128)(2,1)}, u32[]{:S(2)}) copy-start(bf16[4,64,1024]{2,1,0:T(8,128)(2,1)} %subtract_convert_fusion) | copy-start | bytes 1572868
  81.5 3.6 %copy-start.16 = (bf16[2,1024,1024]{2,1,0:T(8,128)(2,1)S(1)}, bf16[2,1024,1024]{2,1,0:T(8,128)(2,1)}, u32[]{:S(2)}) copy-start(bf16[2,1024,1024]{2,1,0:T(8,128)(2,1)} %param.22) | copy-start | bytes 12582916
  87.0 1.6 %copy-start.12 = (f32[4,64,1024]{2,1,0:T(8,128)S(1)}, f32[4,64,1024]{2,1,0:T(8,128)}, u32[]{:S(2)}) copy-start(f32[4,64,1024]{2,1,0:T(8,128)} %get-tuple-element.62) | copy-start | bytes 3145732
  87.1 1.6 %copy-start.14 = (f32[64,1,1024]{2,0,1:T(8,128)S(1)}, f32[64,1,1024]{2,0,1:T(8,128)}, u32[]{:S(2)}) copy-start(f32[64,1,1024]{2,0,1:T(8,128)} %copy-done.13) | copy-start | bytes 786436

commit v3 on v2

--- a/solution.py
+++ b/solution.py
@@ -134,10 +134,11 @@
 
 
 def pick_blocks(full, index, blocks, block_width):
-    parts = full.reshape(full.shape[0], blocks, block_width)
-    chosen = parts[:, 0][None]
+    chosen = full[None, :, :block_width]
     for b in range(1, blocks):
-        chosen = jnp.where((index == b)[:, None, None], parts[:, b][None], chosen)
+        chosen = jnp.where(
+            (index == b)[:, None, None], full[None, :, b * block_width : (b + 1) * block_width], chosen
+        )
     return chosen
 
 
@@ -155,6 +156,15 @@
             (tiles == t)[:, None, None], results[t].reshape(slots, -1, stacked.shape[1]), chosen
         )
     return chosen
+
+
+def live_rows(live_slot, index, blocks, block_width):
+    lane_block = lax.broadcasted_iota(jnp.int32, (8, blocks * block_width), 1) // block_width
+    first_row = lax.broadcasted_iota(jnp.int32, (8, blocks * block_width), 0) == 0
+    total = jnp.zeros((8, blocks * block_width), jnp.float32)
+    for k in range(index.shape[0]):
+        total = total + jnp.where(first_row & live_slot[k] & (lane_block == index[k]), 1.0, 0.0)
+    return total
 
 
 def per_device(
@@ -219,14 +229,8 @@
             [jnp.sum(jnp.where(m, y_terms, 0.0), axis=0) for m in row_mask], axis=1
         )
         if iteration == 0:
-            col_live = jnp.stack([jnp.sum(m.astype(jnp.float32)) for m in col_mask])
-            row_live = jnp.stack([jnp.sum(m.astype(jnp.float32)) for m in row_mask])
-            col_extra = jnp.zeros((8, col_blocks * block_width), jnp.float32).at[0].set(
-                jnp.repeat(col_live, block_width)
-            )
-            row_extra = jnp.zeros((8, row_blocks * block_width), jnp.float32).at[0].set(
-                jnp.repeat(row_live, block_width)
-            )
+            col_extra = live_rows(live_slot, cols_here, col_blocks, block_width)
+            row_extra = live_rows(live_slot, rows_here, row_blocks, block_width)
             col_total, row_total = all_reduce(
                 [
                     jnp.concatenate([col_terms, col_extra], axis=0),

time: 136 us -> 131 us (0.963)
  the two profiles are of different devices: /device:TPU:2 before, /device:TPU:1 now
where the time goes in v3:
time: 131 us; the launch traced here: 130 us
  Pallas kernels  82.6 us (63%)
  other arithmetic  24.5 us (19%)
  matrix products  13.8 us (11%)
  local copies, waits for them, and re-layouts  6.94 us (5%)
  between operations  1.82 us (1%)
    pallas_call x2, Pallas kernels, all_reduce(): pl.pallas_call(functools.partial(reduce_kernel, n, group_axes), out_shape...  82.6 us
    dot_general x12, matrix products, by_tile(): lax.dot_general(stacked, matrices[t], (((1,), (contract,)), ((), ())), pr...  13.8 us
    add x1, other arithmetic, live_rows(): total + jnp.where(first_row & live_slot[k] & (lane_block == index[k]), 1....  5.12 us
    slice x2, local copies, waits for them, and re-layouts, live_rows(): index[k]  2.9 us
    min x1, other arithmetic, per_device(): column_final = jnp.clip(x_own - x_dual - unit_cost, 0.0, capacity)  2.73 us

profile of v3, /device:TPU:1, one launch (start us, length us, event | category | flops | bytes accessed | tf_op | source)
XLA Modules:
  0.0 129.6 jit_solution(13139146124566958254)
XLA Ops:
  0.6 0.0 copy-start.10
  0.6 0.0 copy-start.1
  1.4 1.1 compare_bitcast_fusion
  2.5 0.7 compare_bitcast_fusion.1
  3.2 0.7 fusion.96
  3.9 0.7 fusion.95
  4.5 0.7 fusion.101
  5.2 0.7 broadcast_and_fusion.3
  5.8 0.7 broadcast_and_fusion.2
  6.5 0.6 broadcast_and_fusion
  7.1 0.6 broadcast_and_fusion.1
  7.8 1.5 %fusion.100 = (s32[1,1,1]{2,1,0:T(1,128)}, s32[1,1,1]{2,1,0:T(1,128)}, s32[1,1,1]{2,1,0:T(1,128)}, s32[1,1,1]{2,1,0:T(1,128)}) fusion(s32[1,1,4]{2,1,0:T(1,128)} %param.19), kind=kLoop, calls=%fused_computation.128 | loop fusion | bytes 32 | tf_op jit(solution)/shard_map/slice | solution.py:166
  9.2 1.4 %fusion.102 = (s32[1,1,1]{2,1,0:T(1,128)}, s32[1,1,1]{2,1,0:T(1,128)}, s32[1,1,1]{2,1,0:T(1,128)}, s32[1,1,1]{2,1,0:T(1,128)}) fusion(s32[1,1,4]{2,1,0:T(1,128)} %param.20), kind=kLoop, calls=%fused_computation.130 | loop fusion | bytes 32 | tf_op jit(solution)/shard_map/slice | solution.py:166
  10.7 5.1 %select_add_fusion = (f32[8,2048]{1,0:T(8,128)S(1)}, f32[8,2048]{1,0:T(8,128)S(1)}) fusion(s32[]{:T(128)} %bitcast.28, s32[]{:T(128)} %bitcast.27, s32[]{:T(128)} %bitcast.26, s32[]{:T(128)} %bitcast.25, s32[2048]{0:T(1024)S(1)} %get-tuple-element.49, s32[2048]{0:T(1024)S(1)} %get-tuple-element.50, pred[8]{0:T(512)(128)(4,1)S(1)} %broadcast_and_fusion, ...), kind=kLoop, calls=%fused_computation.93 | loop fusion | flops 507904 | bytes 149568 | tf_op jit(solution)/shard_map/add | solution.py:166
  15.8 1.7 %fusion.79 = bf16[4,64,1024]{2,1,0:T(8,128)(2,1)S(1)} fusion(f32[1,1,4,64,1024]{4,3,2,1,0:T(8,128)} %param.31, f32[1,1,4,64,1024]{4,3,2,1,0:T(8,128)} %param.32), kind=kLoop, calls=%fused_computation.74 | loop fusion | flops 524288 | bytes 2621440 | tf_op jit(solution)/shard_map/convert_element_type | solution.py:214
  17.5 1.1 fusion.99
  18.6 0.0 copy-start.13
  18.6 2.5 %fusion.14 = f32[4,64,1024]{2,1,0:T(8,128)S(1)} fusion(bf16[4,64,1024]{2,1,0:T(8,128)(2,1)S(1)} %fusion.79, bf16[2,1024,1024]{2,1,0:T(8,128)(2,1)} %param.17), kind=kOutput, calls=%fused_computation.14 | convolution fusion | flops 536870912 | bytes 3670016 | tf_op jit(solution)/shard_map/dot_general | solution.py:147
  21.1 0.0 copy-done.10
  21.1 0.0 copy-done.1
  21.1 0.9 fusion.69
  22.1 0.0 copy-done.13
  22.1 0.7 fusion.2
  22.8 1.9 %select_reduce_fusion.7 = (f32[64,1024]{1,0:T(8,128)S(1)}, f32[64,1024]{1,0:T(8,128)S(1)}, f32[4,64,1024]{2,1,0:T(8,128)}, bf16[4,64,1024]{2,1,0:T(8,128)(2,1)S(1)}) fusion(pred[4]{0:T(512)(128)(4,1)S(1)} %get-tuple-element.34, pred[4]{0:T(512)(128)(4,1)S(1)} %get-tuple-element.33, f32[1,1,4,64,1024]{4,3,2,1,0:T(8,128)S(1)} %copy-done.1, ...), kind=kOutput, calls=%fused_computation.62 | convolution fusion | flops 538574848 | bytes 6817280 | tf_op jit(solution)/shard_map/dot_general | solution.py:147
  24.7 0.9 pad_maximum_fusion.refs_0_
  25.6 0.7 fusion.12
  26.3 0.0 copy-done.15
  26.3 0.0 copy-start.2
  26.3 0.0 copy-start.3
  26.3 0.0 copy-start.4
  26.3 0.0 copy-start.5
  26.3 1.9 %select_reduce_fusion.5 = (f32[64,1024]{1,0:T(8,128)S(1)}, f32[64,1024]{1,0:T(8,128)S(1)}, f32[4,64,1024]{2,1,0:T(8,128)}) fusion(pred[4]{0:T(512)(128)(4,1)S(1)} %get-tuple-element.28, pred[4]{0:T(512)(128)(4,1)S(1)} %get-tuple-element.27, f32[1,1,4,64,1024]{4,3,2,1,0:T(8,128)S(1)} %copy-done.15, f32[4,64,1024]{2,1,0:T(8,128)S(1)} %fusion.12, ...), kind=kOutput, calls=%fused_computation.60 | convolution fusion | flops 538312704 | bytes 6292992 | tf_op jit(solution)/shard_map/dot_general | solution.py:147
  28.3 0.8 pad_maximum_fusion.1.refs_1_
  29.1 41.7 %shard_map.176 = (f32[72,2048]{1,0:T(8,128)}, f32[72,2048]{1,0:T(8,128)}) custom-call(f32[72,2048]{1,0:T(8,128)} %pad_maximum_fusion.refs_0_, f32[72,2048]{1,0:T(8,128)} %pad_maximum_fusion.1.refs_1_), custom_call_target="tpu_custom_call" | custom-call | tf_op jit(solution)/shard_map/pallas_call | solution.py:126
  70.9 0.0 copy-start.12
  70.9 0.0 copy-start.7
  70.9 0.0 copy-start.8
  70.9 0.0 copy-start.9
  70.9 1.0 slice_add_fusion.1
  71.9 0.8 slice_add_fusion
  72.8 0.0 copy-done.2
  72.8 0.0 copy-done.3
  72.8 0.0 copy-done.4
  72.8 0.0 copy-done.5
  72.8 1.2 subtract_divide_fusion
  74.0 0.0 copy-start.11
  74.1 0.0 copy-done.12
  74.1 0.2 subtract_convert_fusion
  74.4 0.0 copy-done
  74.4 0.2 add_divide_fusion
  74.7 1.6 %copy-done.11 = bf16[2,1024,1024]{2,1,0:T(8,128)(2,1)S(1)} copy-done((bf16[2,1024,1024]{2,1,0:T(8,128)(2,1)S(1)}, bf16[2,1024,1024]{2,1,0:T(8,128)(2,1)}, u32[]{:S(2)}) %copy-start.11) | copy-done | bytes 4194328
  76.2 0.7 fusion.10
  77.0 0.0 copy-done.16
  77.0 0.9 fusion.66
  77.9 0.6 copy-done.14
  78.5 0.7 fusion
  79.2 1.0 select_reduce_fusion.3
  80.2 0.8 pad_maximum_fusion.2.refs_0_
  81.1 0.7 fusion.8
  81.8 1.0 select_reduce_fusion.1
  82.7 0.8 pad_maximum_fusion.3.refs_1_
  83.6 40.8 %shard_map.177 = (f32[64,2048]{1,0:T(8,128)}, f32[64,2048]{1,0:T(8,128)}) custom-call(f32[64,2048]{1,0:T(8,128)} %pad_maximum_fusion.2.refs_0_, f32[64,2048]{1,0:T(8,128)} %pad_maximum_fusion.3.refs_1_), custom_call_target="tpu_custom_call" | custom-call | tf_op jit(solution)/shard_map/pallas_call | solution.py:126
  124.4 2.4 %fusion.78 = f32[64,2048]{1,0:T(8,128)} fusion(f32[64,2048]{1,0:T(8,128)S(1)} %copy-done.3, f32[64,2048]{1,0:T(8,128)S(1)} %copy-done.4, f32[64,2048]{1,0:T(8,128)} %get-tuple-element.9, f32[2048]{0:T(1024)S(1)} %bitcast.120, f32[64,2048]{1,0:T(8,128)S(1)} %copy-done.2, f32[64,2048]{1,0:T(8,128)S(1)} %copy-done.5, f32[72,2048]{1,0:T(8,128)} %get-tuple-element.7), kind=kLoop, calls=%fused_computation.73 | loop fusion | flops 2490368 | bytes 3678208 | tf_op jit(solution)/shard_map/jit(clip)/min | solution.py:259
  126.8 2.7 %fusion.76 = f32[64,2048]{1,0:T(8,128)} fusion(f32[64,2048]{1,0:T(8,128)S(1)} %copy-done.6, f32[64,2048]{1,0:T(8,128)} %param.25, f32[64,2048]{1,0:T(8,128)} %get-tuple-element.8, f32[2048]{0:T(1024)S(1)} %bitcast.118, f32[64,2048]{1,0:T(8,128)} %param.24, f32[64,2048]{1,0:T(8,128)S(1)} %copy-done, f32[72,2048]{1,0:T(8,128)} %get-tuple-element.6), kind=kLoop, calls=%fused_computation.71 | loop fusion | flops 2621440 | bytes 3678208 | tf_op jit(solution)/shard_map/jit(clip)/min | solution.py:258
  (13 shorter events, 0.1 us)
Async XLA Ops:
  0.6 20.5 %copy-start.10 = (bf16[2,1024,1024]{2,1,0:T(8,128)(2,1)S(1)}, bf16[2,1024,1024]{2,1,0:T(8,128)(2,1)}, u32[]{:S(2)}) copy-start(bf16[2,1024,1024]{2,1,0:T(8,128)(2,1)} %param.17) | copy-start | bytes 12582916
  0.6 20.5 %copy-start.1 = (f32[1,1,4,64,1024]{4,3,2,1,0:T(8,128)S(1)}, f32[1,1,4,64,1024]{4,3,2,1,0:T(8,128)}, u32[]{:S(2)}) copy-start(f32[1,1,4,64,1024]{4,3,2,1,0:T(8,128)} %param.33) | copy-start | bytes 3145732
  18.6 3.5 %copy-start.13 = (bf16[2,1024,1024]{2,1,0:T(8,128)(2,1)S(1)}, bf16[2,1024,1024]{2,1,0:T(8,128)(2,1)}, u32[]{:S(2)}) copy-start(bf16[2,1024,1024]{2,1,0:T(8,128)(2,1)} %param.18) | copy-start | bytes 12582916
  24.7 1.6 %copy-start.15 = (f32[1,1,4,64,1024]{4,3,2,1,0:T(8,128)S(1)}, f32[1,1,4,64,1024]{4,3,2,1,0:T(8,128)}, u32[]{:S(2)}) copy-start(f32[1,1,4,64,1024]{4,3,2,1,0:T(8,128)} %param.32) | copy-start | bytes 3145732
  26.3 46.5 %copy-start.2 = (f32[64,2048]{1,0:T(8,128)S(1)}, f32[64,2048]{1,0:T(8,128)}, u32[]{:S(2)}) copy-start(f32[64,2048]{1,0:T(8,128)} %param.28) | copy-start | bytes 1572868
  26.3 46.5 %copy-start.3 = (f32[64,2048]{1,0:T(8,128)S(1)}, f32[64,2048]{1,0:T(8,128)}, u32[]{:S(2)}) copy-start(f32[64,2048]{1,0:T(8,128)} %param.30) | copy-start | bytes 1572868
  26.3 46.5 %copy-start.4 = (f32[64,2048]{1,0:T(8,128)S(1)}, f32[64,2048]{1,0:T(8,128)}, u32[]{:S(2)}) copy-start(f32[64,2048]{1,0:T(8,128)} %param.29) | copy-start | bytes 1572868
  26.3 46.5 %copy-start.5 = (f32[64,2048]{1,0:T(8,128)S(1)}, f32[64,2048]{1,0:T(8,128)}, u32[]{:S(2)}) copy-start(f32[64,2048]{1,0:T(8,128)} %param.27) | copy-start | bytes 1572868
  28.3 46.1 %copy-start = (f32[64,2048]{1,0:T(8,128)S(1)}, f32[64,2048]{1,0:T(8,128)}, u32[]{:S(2)}) copy-start(f32[64,2048]{1,0:T(8,128)} %param.23) | copy-start | bytes 1572868
  28.3 46.1 %copy-start.6 = (f32[64,2048]{1,0:T(8,128)S(1)}, f32[64,2048]{1,0:T(8,128)}, u32[]{:S(2)}) copy-start(f32[64,2048]{1,0:T(8,128)} %param.26) | copy-start | bytes 1572868
  70.9 3.2 %copy-start.12 = (f32[4,64,1024]{2,1,0:T(8,128)S(1)}, f32[4,64,1024]{2,1,0:T(8,128)}, u32[]{:S(2)}) copy-start(f32[4,64,1024]{2,1,0:T(8,128)} %get-tuple-element.44) | copy-start | bytes 3145732
  70.9 3.5 %copy-start.7 = (f32[64,2048]{1,0:T(8,128)S(1)}, f32[64,2048]{1,0:T(8,128)}, u32[]{:S(2)}) copy-start(f32[64,2048]{1,0:T(8,128)} %param.25) | copy-start | bytes 1572868
  70.9 3.5 %copy-start.8 = (f32[64,2048]{1,0:T(8,128)S(1)}, f32[64,2048]{1,0:T(8,128)}, u32[]{:S(2)}) copy-start(f32[64,2048]{1,0:T(8,128)} %param.24) | copy-start | bytes 1572868
  70.9 3.5 %copy-start.9 = (f32[72,2048]{1,0:T(8,128)S(1)}, f32[72,2048]{1,0:T(8,128)}, u32[]{:S(2)}) copy-start(f32[72,2048]{1,0:T(8,128)} %get-tuple-element.6) | copy-start | bytes 1769476
  74.0 2.2 %copy-start.11 = (bf16[2,1024,1024]{2,1,0:T(8,128)(2,1)S(1)}, bf16[2,1024,1024]{2,1,0:T(8,128)(2,1)}, u32[]{:S(2)}) copy-start(bf16[2,1024,1024]{2,1,0:T(8,128)(2,1)} %param.17) | copy-start | bytes 12582916
  74.4 2.6 %copy-start.16 = (f32[4,64,1024]{2,1,0:T(8,128)S(1)}, f32[4,64,1024]{2,1,0:T(8,128)}, u32[]{:S(2)}) copy-start(f32[4,64,1024]{2,1,0:T(8,128)} %get-tuple-element.18) | copy-start | bytes 3145732
  76.2 2.3 %copy-start.14 = (bf16[2,1024,1024]{2,1,0:T(8,128)(2,1)S(1)}, bf16[2,1024,1024]{2,1,0:T(8,128)(2,1)}, u32[]{:S(2)}) copy-start(bf16[2,1024,1024]{2,1,0:T(8,128)(2,1)} %param.18) | copy-start | bytes 12582916

commit v4 on v3

--- a/solution.py
+++ b/solution.py
@@ -32,7 +32,7 @@
             pl.semaphore_signal(barrier, inc=1, device_id=peer_id(axis, peer), device_id_type=MESH)
     pl.semaphore_wait(barrier, groups * (n - 1))
 
-    width = ins[0].shape[1] // n
+    width = ins[0].shape[2]
 
     def cols(index):
         return pl.ds(pl.multiple_of(index * width, width), width)
@@ -45,7 +45,7 @@
         for k in range(1, n):
             peer = lax.rem(me + k, n)
             copy = pltpu.make_async_remote_copy(
-                src_ref=ins[g].at[:, cols(peer)],
+                src_ref=ins[g].at[peer],
                 dst_ref=recv.at[me],
                 send_sem=s1.at[peer],
                 recv_sem=r1.at[me],
@@ -63,14 +63,14 @@
         for k in range(1, n):
             source = lax.rem(me + n - k, n)
             pltpu.make_async_remote_copy(
-                src_ref=ins[g].at[:, cols(source)],
+                src_ref=ins[g].at[source],
                 dst_ref=recv.at[source],
                 send_sem=s1.at[source],
                 recv_sem=r1.at[source],
                 device_id=peer_id(axis, source),
                 device_id_type=MESH,
             ).wait_recv()
-        total = ins[g][:, cols(me)]
+        total = ins[g][me]
         for k in range(1, n):
             total = total + recv[lax.rem(me + k, n)]
         gathered[me] = total
@@ -113,6 +113,7 @@
 def all_reduce(arrays, group_axes, n, collective_id):
     shapes = [a.shape for a in arrays]
     width = shapes[0][1] // n
+    arrays = [a.reshape(a.shape[0], n, width).transpose(1, 0, 2) for a in arrays]
     scratch = []
     for rows, _ in shapes:
         scratch += [

time: 131 us -> 131 us (level)
    transpose x0 -> x4, other arithmetic: none -> 3.4 us  [all_reduce(): a.reshape(a.shape[0], n, width).transpose(1, 0, 2)]
    concatenate x2 -> x0, other arithmetic: 1.66 us -> none  [the longest x1 0.83 us: per_device(): jnp.concatenate([jnp.sum(jnp.where(m, y_terms, 0.0), axis=0) for m in row...]
where the time goes in v4:
time: 131 us; the launch traced here: 129 us
  Pallas kernels  82.2 us (63%)
  other arithmetic  24.6 us (19%)
  matrix products  13.8 us (11%)
  local copies, waits for them, and re-layouts  6.95 us (5%)
  between operations  1.85 us (1%)
    pallas_call x2, Pallas kernels, all_reduce(): pl.pallas_call(functools.partial(reduce_kernel, n, group_axes), out_shape...  82.2 us
    dot_general x12, matrix products, by_tile(): lax.dot_general(stacked, matrices[t], (((1,), (contract,)), ((), ())), pr...  13.8 us
    add x1, other arithmetic, live_rows(): total + jnp.where(first_row & live_slot[k] & (lane_block == index[k]), 1....  5.12 us
    transpose x4, other arithmetic, all_reduce(): a.reshape(a.shape[0], n, width).transpose(1, 0, 2)  3.4 us
    slice x2, local copies, waits for them, and re-layouts, live_rows(): index[k]  2.9 us
    min x1, other arithmetic, per_device(): column_final = jnp.clip(x_own - x_dual - unit_cost, 0.0, capacity)  2.73 us

profile of v4, /device:TPU:1, one launch (start us, length us, event | category | flops | bytes accessed | tf_op | source)
XLA Modules:
  0.0 129.4 jit_solution(5166045341864908532)
XLA Ops:
  0.6 0.0 copy-start.10
  0.6 0.0 copy-start.1
  1.4 1.1 compare_bitcast_fusion
  2.5 0.7 compare_bitcast_fusion.1
  3.2 0.7 fusion.95
  3.9 0.7 fusion.94
  4.5 0.7 fusion.100
  5.2 0.7 broadcast_and_fusion.3
  5.8 0.7 broadcast_and_fusion.2
  6.5 0.6 broadcast_and_fusion
  7.1 0.6 broadcast_and_fusion.1
  7.8 1.5 %fusion.99 = (s32[1,1,1]{2,1,0:T(1,128)}, s32[1,1,1]{2,1,0:T(1,128)}, s32[1,1,1]{2,1,0:T(1,128)}, s32[1,1,1]{2,1,0:T(1,128)}) fusion(s32[1,1,4]{2,1,0:T(1,128)} %param.19), kind=kLoop, calls=%fused_computation.133 | loop fusion | bytes 32 | tf_op jit(solution)/shard_map/slice | solution.py:167
  9.2 1.4 %fusion.101 = (s32[1,1,1]{2,1,0:T(1,128)}, s32[1,1,1]{2,1,0:T(1,128)}, s32[1,1,1]{2,1,0:T(1,128)}, s32[1,1,1]{2,1,0:T(1,128)}) fusion(s32[1,1,4]{2,1,0:T(1,128)} %param.20), kind=kLoop, calls=%fused_computation.135 | loop fusion | bytes 32 | tf_op jit(solution)/shard_map/slice | solution.py:167
  10.7 5.1 %select_add_fusion = (f32[8,16,128]{2,0,1:T(8,128)S(1)}, f32[8,16,128]{2,0,1:T(8,128)S(1)}) fusion(s32[]{:T(128)} %bitcast.29, s32[]{:T(128)} %bitcast.28, s32[]{:T(128)} %bitcast.27, s32[]{:T(128)} %bitcast.26, s32[16,128]{1,0:T(8,128)S(1)} %get-tuple-element.49, s32[16,128]{1,0:T(8,128)S(1)} %get-tuple-element.50, pred[8]{0:T(512)(128)(4,1)S(1)} %broadcast_and_fusion, ...), kind=kLoop, calls=%fused_computation.99 | loop fusion | flops 507904 | bytes 149568 | tf_op jit(solution)/shard_map/add | solution.py:167
  15.8 1.7 %fusion.79 = bf16[4,64,1024]{2,1,0:T(8,128)(2,1)S(1)} fusion(f32[1,1,4,64,1024]{4,3,2,1,0:T(8,128)} %param.31, f32[1,1,4,64,1024]{4,3,2,1,0:T(8,128)} %param.32), kind=kLoop, calls=%fused_computation.74 | loop fusion | flops 524288 | bytes 2621440 | tf_op jit(solution)/shard_map/convert_element_type | solution.py:215
  17.5 1.1 fusion.98
  18.6 0.0 copy-start.13
  18.6 2.5 %fusion.14 = f32[4,64,1024]{2,1,0:T(8,128)S(1)} fusion(bf16[4,64,1024]{2,1,0:T(8,128)(2,1)S(1)} %fusion.79, bf16[2,1024,1024]{2,1,0:T(8,128)(2,1)} %param.17), kind=kOutput, calls=%fused_computation.14 | convolution fusion | flops 536870912 | bytes 3670016 | tf_op jit(solution)/shard_map/dot_general | solution.py:148
  21.1 0.0 copy-done.10
  21.1 0.0 copy-done.1
  21.1 0.9 fusion.69
  22.1 0.0 copy-done.13
  22.1 0.7 fusion.2
  22.8 1.9 %select_reduce_fusion.7 = (f32[64,1024]{1,0:T(8,128)S(1)}, f32[64,1024]{1,0:T(8,128)S(1)}, f32[4,64,1024]{2,1,0:T(8,128)}, bf16[4,64,1024]{2,1,0:T(8,128)(2,1)S(1)}) fusion(pred[4]{0:T(512)(128)(4,1)S(1)} %get-tuple-element.34, pred[4]{0:T(512)(128)(4,1)S(1)} %get-tuple-element.33, f32[1,1,4,64,1024]{4,3,2,1,0:T(8,128)S(1)} %copy-done.1, ...), kind=kOutput, calls=%fused_computation.62 | convolution fusion | flops 538574848 | bytes 6817280 | tf_op jit(solution)/shard_map/dot_general | solution.py:148
  24.8 0.9 maximum_bitcast_fusion.refs_0_
  25.6 0.7 fusion.12
  26.4 0.0 copy-done.15
  26.4 0.0 copy-start.2
  26.4 0.0 copy-start.3
  26.4 0.0 copy-start.4
  26.4 0.0 copy-start.5
  26.4 2.0 %select_reduce_fusion.5 = (f32[64,1024]{1,0:T(8,128)S(1)}, f32[64,1024]{1,0:T(8,128)S(1)}, f32[4,64,1024]{2,1,0:T(8,128)}) fusion(pred[4]{0:T(512)(128)(4,1)S(1)} %get-tuple-element.28, pred[4]{0:T(512)(128)(4,1)S(1)} %get-tuple-element.27, f32[1,1,4,64,1024]{4,3,2,1,0:T(8,128)S(1)} %copy-done.15, f32[4,64,1024]{2,1,0:T(8,128)S(1)} %fusion.12, ...), kind=kOutput, calls=%fused_computation.60 | convolution fusion | flops 538312704 | bytes 6292992 | tf_op jit(solution)/shard_map/dot_general | solution.py:148
  28.4 0.0 copy-start
  28.4 0.0 copy-start.6
  28.4 0.8 maximum_bitcast_fusion.1.refs_1_
  29.3 41.7 %shard_map.176 = (f32[72,2048]{1,0:T(8,128)}, f32[72,2048]{1,0:T(8,128)}) custom-call(f32[16,72,128]{2,1,0:T(8,128)} %maximum_bitcast_fusion.refs_0_, f32[16,72,128]{2,1,0:T(8,128)} %maximum_bitcast_fusion.1.refs_1_), custom_call_target="tpu_custom_call" | custom-call | tf_op jit(solution)/shard_map/pallas_call | solution.py:127
  71.0 0.0 copy-start.12
  71.0 0.0 copy-start.7
  71.0 0.0 copy-start.8
  71.0 0.0 copy-start.9
  71.0 1.0 slice_add_fusion.1
  72.0 0.8 slice_add_fusion
  72.9 0.0 copy-done.2
  72.9 0.0 copy-done.3
  72.9 0.0 copy-done.4
  72.9 0.0 copy-done.5
  72.9 1.2 subtract_divide_fusion
  74.1 0.0 copy-start.11
  74.2 0.0 copy-done.12
  74.2 0.2 subtract_convert_fusion
  74.5 0.2 add_divide_fusion
  74.7 1.6 %copy-done.11 = bf16[2,1024,1024]{2,1,0:T(8,128)(2,1)S(1)} copy-done((bf16[2,1024,1024]{2,1,0:T(8,128)(2,1)S(1)}, bf16[2,1024,1024]{2,1,0:T(8,128)(2,1)}, u32[]{:S(2)}) %copy-start.11) | copy-done | bytes 4194328
  76.3 0.7 fusion.10
  77.1 0.9 fusion.66
  78.0 0.6 copy-done.14
  78.6 0.7 fusion
  79.3 1.0 select_reduce_fusion.3
  80.3 0.8 bitcast_bitcast_fusion.1.refs_0_
  81.2 0.7 fusion.8
  81.9 1.0 select_reduce_fusion.1
  82.9 0.8 bitcast_bitcast_fusion.refs_1_
  83.7 40.5 %shard_map.177 = (f32[64,2048]{1,0:T(8,128)}, f32[64,2048]{1,0:T(8,128)}) custom-call(f32[16,64,128]{2,1,0:T(8,128)} %bitcast_bitcast_fusion.1.refs_0_, f32[16,64,128]{2,1,0:T(8,128)} %bitcast_bitcast_fusion.refs_1_), custom_call_target="tpu_custom_call" | custom-call | tf_op jit(solution)/shard_map/pallas_call | solution.py:127
  124.2 2.4 %fusion.78 = f32[64,2048]{1,0:T(8,128)} fusion(f32[64,2048]{1,0:T(8,128)S(1)} %copy-done.3, f32[64,2048]{1,0:T(8,128)S(1)} %copy-done.4, f32[64,2048]{1,0:T(8,128)} %get-tuple-element.9, f32[2048]{0:T(1024)S(1)} %bitcast.148, f32[64,2048]{1,0:T(8,128)S(1)} %copy-done.2, f32[64,2048]{1,0:T(8,128)S(1)} %copy-done.5, f32[72,2048]{1,0:T(8,128)} %get-tuple-element.7), kind=kLoop, calls=%fused_computation.73 | loop fusion | flops 2490368 | bytes 3678208 | tf_op jit(solution)/shard_map/jit(clip)/min | solution.py:260
  126.7 2.7 %fusion.76 = f32[64,2048]{1,0:T(8,128)} fusion(f32[64,2048]{1,0:T(8,128)S(1)} %copy-done.6, f32[64,2048]{1,0:T(8,128)} %param.25, f32[64,2048]{1,0:T(8,128)} %get-tuple-element.8, f32[2048]{0:T(1024)S(1)} %bitcast.146, f32[64,2048]{1,0:T(8,128)} %param.24, f32[64,2048]{1,0:T(8,128)S(1)} %copy-done, f32[72,2048]{1,0:T(8,128)} %get-tuple-element.6), kind=kLoop, calls=%fused_computation.71 | loop fusion | flops 2621440 | bytes 3678208 | tf_op jit(solution)/shard_map/jit(clip)/min | solution.py:259
  (15 shorter events, 0.2 us)
Async XLA Ops:
  0.6 20.5 %copy-start.10 = (bf16[2,1024,1024]{2,1,0:T(8,128)(2,1)S(1)}, bf16[2,1024,1024]{2,1,0:T(8,128)(2,1)}, u32[]{:S(2)}) copy-start(bf16[2,1024,1024]{2,1,0:T(8,128)(2,1)} %param.17) | copy-start | bytes 12582916
  0.6 20.5 %copy-start.1 = (f32[1,1,4,64,1024]{4,3,2,1,0:T(8,128)S(1)}, f32[1,1,4,64,1024]{4,3,2,1,0:T(8,128)}, u32[]{:S(2)}) copy-start(f32[1,1,4,64,1024]{4,3,2,1,0:T(8,128)} %param.33) | copy-start | bytes 3145732
  18.6 3.5 %copy-start.13 = (bf16[2,1024,1024]{2,1,0:T(8,128)(2,1)S(1)}, bf16[2,1024,1024]{2,1,0:T(8,128)(2,1)}, u32[]{:S(2)}) copy-start(bf16[2,1024,1024]{2,1,0:T(8,128)(2,1)} %param.18) | copy-start | bytes 12582916
  24.7 1.6 %copy-start.15 = (f32[1,1,4,64,1024]{4,3,2,1,0:T(8,128)S(1)}, f32[1,1,4,64,1024]{4,3,2,1,0:T(8,128)}, u32[]{:S(2)}) copy-start(f32[1,1,4,64,1024]{4,3,2,1,0:T(8,128)} %param.32) | copy-start | bytes 3145732
  26.4 46.5 %copy-start.2 = (f32[64,2048]{1,0:T(8,128)S(1)}, f32[64,2048]{1,0:T(8,128)}, u32[]{:S(2)}) copy-start(f32[64,2048]{1,0:T(8,128)} %param.28) | copy-start | bytes 1572868
  26.4 46.5 %copy-start.3 = (f32[64,2048]{1,0:T(8,128)S(1)}, f32[64,2048]{1,0:T(8,128)}, u32[]{:S(2)}) copy-start(f32[64,2048]{1,0:T(8,128)} %param.30) | copy-start | bytes 1572868
  26.4 46.5 %copy-start.4 = (f32[64,2048]{1,0:T(8,128)S(1)}, f32[64,2048]{1,0:T(8,128)}, u32[]{:S(2)}) copy-start(f32[64,2048]{1,0:T(8,128)} %param.29) | copy-start | bytes 1572868
  26.4 46.5 %copy-start.5 = (f32[64,2048]{1,0:T(8,128)S(1)}, f32[64,2048]{1,0:T(8,128)}, u32[]{:S(2)}) copy-start(f32[64,2048]{1,0:T(8,128)} %param.27) | copy-start | bytes 1572868
  28.4 46.0 %copy-start = (f32[64,2048]{1,0:T(8,128)S(1)}, f32[64,2048]{1,0:T(8,128)}, u32[]{:S(2)}) copy-start(f32[64,2048]{1,0:T(8,128)} %param.23) | copy-start | bytes 1572868
  28.4 46.0 %copy-start.6 = (f32[64,2048]{1,0:T(8,128)S(1)}, f32[64,2048]{1,0:T(8,128)}, u32[]{:S(2)}) copy-start(f32[64,2048]{1,0:T(8,128)} %param.26) | copy-start | bytes 1572868
  71.0 3.2 %copy-start.12 = (f32[4,64,1024]{2,1,0:T(8,128)S(1)}, f32[4,64,1024]{2,1,0:T(8,128)}, u32[]{:S(2)}) copy-start(f32[4,64,1024]{2,1,0:T(8,128)} %get-tuple-element.44) | copy-start | bytes 3145732
  71.0 3.5 %copy-start.7 = (f32[64,2048]{1,0:T(8,128)S(1)}, f32[64,2048]{1,0:T(8,128)}, u32[]{:S(2)}) copy-start(f32[64,2048]{1,0:T(8,128)} %param.25) | copy-start | bytes 1572868
  71.0 3.5 %copy-start.8 = (f32[64,2048]{1,0:T(8,128)S(1)}, f32[64,2048]{1,0:T(8,128)}, u32[]{:S(2)}) copy-start(f32[64,2048]{1,0:T(8,128)} %param.24) | copy-start | bytes 1572868
  71.0 3.5 %copy-start.9 = (f32[72,2048]{1,0:T(8,128)S(1)}, f32[72,2048]{1,0:T(8,128)}, u32[]{:S(2)}) copy-start(f32[72,2048]{1,0:T(8,128)} %get-tuple-element.6) | copy-start | bytes 1769476
  74.1 2.2 %copy-start.11 = (bf16[2,1024,1024]{2,1,0:T(8,128)(2,1)S(1)}, bf16[2,1024,1024]{2,1,0:T(8,128)(2,1)}, u32[]{:S(2)}) copy-start(bf16[2,1024,1024]{2,1,0:T(8,128)(2,1)} %param.17) | copy-start | bytes 12582916
  74.5 2.6 %copy-start.16 = (f32[4,64,1024]{2,1,0:T(8,128)S(1)}, f32[4,64,1024]{2,1,0:T(8,128)}, u32[]{:S(2)}) copy-start(f32[4,64,1024]{2,1,0:T(8,128)} %get-tuple-element.18) | copy-start | bytes 3145732
  76.3 2.3 %copy-start.14 = (bf16[2,1024,1024]{2,1,0:T(8,128)(2,1)S(1)}, bf16[2,1024,1024]{2,1,0:T(8,128)(2,1)}, u32[]{:S(2)}) copy-start(bf16[2,1024,1024]{2,1,0:T(8,128)(2,1)} %param.18) | copy-start | bytes 12582916

commit v5 on v4

--- a/solution.py
+++ b/solution.py
@@ -18,12 +18,36 @@
     return (lax.axis_index("row"), peer)
 
 
-def reduce_kernel(n, group_axes, *refs):
+def reduce_kernel(n, group_axes, block_width, with_counts, *refs):
     groups = len(group_axes)
+    if with_counts:
+        info, refs = refs[0], refs[1:]
     ins = refs[:groups]
     outs = refs[groups : 2 * groups]
     scratch = refs[2 * groups :]
-    per = [scratch[6 * g : 6 * g + 6] for g in range(groups)]
+    size = 7 if with_counts else 6
+    per = [scratch[size * g : size * g + 6] for g in range(groups)]
+    width = ins[0].shape[2]
+    sources = list(ins)
+    if with_counts:
+        slots = (info.shape[0] - 1) // groups
+        live = info[groups * slots]
+        for g in range(groups):
+            send = scratch[size * g + 6]
+            data_rows = ins[g].shape[1]
+            extra = send.shape[1] - data_rows
+            for p in range(n):
+                block = (p * width) // block_width
+                count = jnp.int32(0)
+                for k in range(slots):
+                    count = count + jnp.where(
+                        (k < live) & (info[g * slots + k] == block), 1, 0
+                    ).astype(jnp.int32)
+                send[p, :data_rows, :] = ins[g][p]
+                send[p, data_rows:, :] = jnp.full((extra, width), count, jnp.int32).astype(
+                    jnp.float32
+                )
+            sources[g] = send
     barrier = pltpu.get_barrier_semaphore()
     for axis in group_axes:
         me = lax.axis_index(axis)
@@ -31,11 +55,6 @@
             peer = lax.rem(me + k, n)
             pl.semaphore_signal(barrier, inc=1, device_id=peer_id(axis, peer), device_id_type=MESH)
     pl.semaphore_wait(barrier, groups * (n - 1))
-
-    width = ins[0].shape[2]
-
-    def cols(index):
-        return pl.ds(pl.multiple_of(index * width, width), width)
 
     scatter = []
     for g, axis in enumerate(group_axes):
@@ -45,7 +64,7 @@
         for k in range(1, n):
             peer = lax.rem(me + k, n)
             copy = pltpu.make_async_remote_copy(
-                src_ref=ins[g].at[peer],
+                src_ref=sources[g].at[peer],
                 dst_ref=recv.at[me],
                 send_sem=s1.at[peer],
                 recv_sem=r1.at[me],
@@ -63,14 +82,14 @@
         for k in range(1, n):
             source = lax.rem(me + n - k, n)
             pltpu.make_async_remote_copy(
-                src_ref=ins[g].at[source],
+                src_ref=sources[g].at[source],
                 dst_ref=recv.at[source],
                 send_sem=s1.at[source],
                 recv_sem=r1.at[source],
                 device_id=peer_id(axis, source),
                 device_id_type=MESH,
             ).wait_recv()
-        total = ins[g][me]
+        total = sources[g][me]
         for k in range(1, n):
             total = total + recv[lax.rem(me + k, n)]
         gathered[me] = total
@@ -110,8 +129,9 @@
             outs[g][:, index * width : (index + 1) * width] = gathered[index]
 
 
-def all_reduce(arrays, group_axes, n, collective_id):
-    shapes = [a.shape for a in arrays]
+def all_reduce(arrays, group_axes, n, collective_id, block_width, info=None):
+    extra = 0 if info is None else 8
+    shapes = [(a.shape[0] + extra, a.shape[1]) for a in arrays]
     width = shapes[0][1] // n
     arrays = [a.reshape(a.shape[0], n, width).transpose(1, 0, 2) for a in arrays]
     scratch = []
@@ -124,11 +144,17 @@
             pltpu.SemaphoreType.DMA((n,)),
             pltpu.SemaphoreType.DMA((n,)),
         ]
+        if info is not None:
+            scratch.append(pltpu.VMEM((n, rows, width), jnp.float32))
+    in_specs = [pl.BlockSpec(memory_space=pltpu.VMEM)] * len(arrays)
+    if info is not None:
+        in_specs = [pl.BlockSpec(memory_space=pltpu.SMEM)] + in_specs
+        arrays = [info] + arrays
     return pl.pallas_call(
-        functools.partial(reduce_kernel, n, group_axes),
+        functools.partial(reduce_kernel, n, group_axes, block_width, info is not None),
         out_shape=tuple(jax.ShapeDtypeStruct(s, jnp.float32) for s in shapes),
-        in_specs=[pl.BlockSpec(memory_space=pltpu.VMEM)] * len(arrays),
-        out_specs=tuple(pl.BlockSpec(memory_space=pltpu.VMEM) for _ in arrays),
+        in_specs=in_specs,
+        out_specs=tuple(pl.BlockSpec(memory_space=pltpu.VMEM) for _ in shapes),
         scratch_shapes=scratch,
         compiler_params=pltpu.CompilerParams(collective_id=collective_id, has_side_effects=True),
     )(*arrays)
@@ -157,15 +183,6 @@
             (tiles == t)[:, None, None], results[t].reshape(slots, -1, stacked.shape[1]), chosen
         )
     return chosen
-
-
-def live_rows(live_slot, index, blocks, block_width):
-    lane_block = lax.broadcasted_iota(jnp.int32, (8, blocks * block_width), 1) // block_width
-    first_row = lax.broadcasted_iota(jnp.int32, (8, blocks * block_width), 0) == 0
-    total = jnp.zeros((8, blocks * block_width), jnp.float32)
-    for k in range(index.shape[0]):
-        total = total + jnp.where(first_row & live_slot[k] & (lane_block == index[k]), 1.0, 0.0)
-    return total
 
 
 def per_device(
@@ -230,23 +247,16 @@
             [jnp.sum(jnp.where(m, y_terms, 0.0), axis=0) for m in row_mask], axis=1
         )
         if iteration == 0:
-            col_extra = live_rows(live_slot, cols_here, col_blocks, block_width)
-            row_extra = live_rows(live_slot, rows_here, row_blocks, block_width)
+            slot_info = jnp.concatenate([cols_here, rows_here, block_count[0, 0][None]])
             col_total, row_total = all_reduce(
-                [
-                    jnp.concatenate([col_terms, col_extra], axis=0),
-                    jnp.concatenate([row_terms, row_extra], axis=0),
-                ],
-                AXES,
-                n_row,
-                0,
+                [col_terms, row_terms], AXES, n_row, 0, block_width, slot_info
             )
             col_denom = 1.0 + col_total[scenarios : scenarios + 1]
             row_denom = 1.0 + row_total[scenarios : scenarios + 1]
             col_total = col_total[:scenarios]
             row_total = row_total[:scenarios]
         else:
-            col_total, row_total = all_reduce([col_terms, row_terms], AXES, n_row, 1)
+            col_total, row_total = all_reduce([col_terms, row_terms], AXES, n_row, 1, block_width)
         x_own = (x_half + x_dual + col_total) / col_denom
         x_dual = x_dual + x_half - x_own
         shift_full = (row_total - y_anchor) / row_denom

time: 131 us -> 120 us (0.916)
  the two profiles are of different devices: /device:TPU:1 before, /device:TPU:25 now
where the time goes in v5:
time: 120 us; the launch traced here: 119 us
  Pallas kernels  83.7 us (70%)
  other arithmetic  16.8 us (14%)
  matrix products  13.8 us (12%)
  local copies, waits for them, and re-layouts  3.38 us (3%)
  between operations  1.78 us (1%)
    pallas_call x2, Pallas kernels, all_reduce(): pl.pallas_call(functools.partial(reduce_kernel, n, group_axes, block_widt...  83.7 us
    dot_general x12, matrix products, by_tile(): lax.dot_general(stacked, matrices[t], (((1,), (contract,)), ((), ())), pr...  13.8 us
    transpose x4, other arithmetic, all_reduce(): a.reshape(a.shape[0], n, width).transpose(1, 0, 2)  3.39 us
    min x1, other arithmetic, per_device(): column_final = jnp.clip(x_own - x_dual - unit_cost, 0.0, capacity)  2.73 us
    min x1, other arithmetic, per_device(): row_final = jnp.clip(y_state - y_dual, row_lower, row_upper)  2.41 us

profile of v5, /device:TPU:25, one launch (start us, length us, event | category | flops | bytes accessed | tf_op | source)
XLA Modules:
  0.0 119.4 jit_solution(15705987292997615218)
XLA Ops:
  0.6 0.0 copy-start.10
  0.6 0.0 copy-start.1
  1.4 1.1 compare_bitcast_fusion
  2.5 1.3 %pad_add_fusion.refs_0_ = s32[9]{0:T(128)} fusion(s32[1]{0:T(128)} %bitcast.130, s32[4]{0:T(128)} %bitcast.137, s32[4]{0:T(128)} %bitcast.136), kind=kLoop, calls=%fused_computation.94 | loop fusion | flops 18 | bytes 72 | tf_op jit(solution)/shard_map/concatenate | solution.py:250
  3.8 0.7 fusion.85
  4.5 1.7 %fusion.79 = bf16[4,64,1024]{2,1,0:T(8,128)(2,1)S(1)} fusion(f32[1,1,4,64,1024]{4,3,2,1,0:T(8,128)} %param.31, f32[1,1,4,64,1024]{4,3,2,1,0:T(8,128)} %param.32), kind=kLoop, calls=%fused_computation.72 | loop fusion | flops 524288 | bytes 2621440 | tf_op jit(solution)/shard_map/convert_element_type | solution.py:232
  6.2 1.1 fusion.88
  7.3 0.0 copy-start.13
  7.3 2.5 %fusion.14 = f32[4,64,1024]{2,1,0:T(8,128)S(1)} fusion(bf16[4,64,1024]{2,1,0:T(8,128)(2,1)S(1)} %fusion.79, bf16[2,1024,1024]{2,1,0:T(8,128)(2,1)} %param.17), kind=kOutput, calls=%fused_computation.14 | convolution fusion | flops 536870912 | bytes 3670016 | tf_op jit(solution)/shard_map/dot_general | solution.py:174
  9.8 0.0 copy-done.10
  9.8 0.0 copy-done.1
  9.8 0.9 fusion.69
  10.7 0.0 copy-done.13
  10.8 0.7 fusion.2
  11.5 1.9 %select_reduce_fusion.7 = (f32[64,1024]{1,0:T(8,128)S(1)}, f32[64,1024]{1,0:T(8,128)S(1)}, f32[4,64,1024]{2,1,0:T(8,128)}, bf16[4,64,1024]{2,1,0:T(8,128)(2,1)S(1)}) fusion(pred[4]{0:T(512)(128)(4,1)S(1)} %get-tuple-element.30, pred[4]{0:T(512)(128)(4,1)S(1)} %get-tuple-element.28, f32[1,1,4,64,1024]{4,3,2,1,0:T(8,128)S(1)} %copy-done.1, ...), kind=kOutput, calls=%fused_computation.62 | convolution fusion | flops 538574848 | bytes 6817280 | tf_op jit(solution)/shard_map/dot_general | solution.py:174
  13.4 0.0 copy-start.15
  13.4 0.8 bitcast_bitcast_fusion.3.refs_1_
  14.2 0.7 fusion.12
  15.0 0.0 copy-done.15
  15.0 0.0 copy-start.2
  15.0 0.0 copy-start.3
  15.0 0.0 copy-start.4
  15.0 0.0 copy-start.5
  15.0 1.9 %select_reduce_fusion.5 = (f32[64,1024]{1,0:T(8,128)S(1)}, f32[64,1024]{1,0:T(8,128)S(1)}, f32[4,64,1024]{2,1,0:T(8,128)}) fusion(pred[4]{0:T(512)(128)(4,1)S(1)} %get-tuple-element.34, pred[4]{0:T(512)(128)(4,1)S(1)} %get-tuple-element.35, f32[1,1,4,64,1024]{4,3,2,1,0:T(8,128)S(1)} %copy-done.15, f32[4,64,1024]{2,1,0:T(8,128)S(1)} %fusion.12, ...), kind=kOutput, calls=%fused_computation.60 | convolution fusion | flops 538312704 | bytes 6292992 | tf_op jit(solution)/shard_map/dot_general | solution.py:174
  17.0 0.0 copy-start
  17.0 0.0 copy-start.6
  17.0 0.8 bitcast_bitcast_fusion.2.refs_2_
  17.8 43.0 %shard_map.176 = (f32[72,2048]{1,0:T(8,128)}, f32[72,2048]{1,0:T(8,128)}) custom-call(s32[9]{0:T(128)} %pad_add_fusion.refs_0_, f32[16,64,128]{2,1,0:T(8,128)} %bitcast_bitcast_fusion.3.refs_1_, f32[16,64,128]{2,1,0:T(8,128)} %bitcast_bitcast_fusion.2.refs_2_), custom_call_target="tpu_custom_call" | custom-call | tf_op jit(solution)/shard_map/pallas_call | solution.py:153
  60.9 0.0 copy-start.12
  60.9 0.0 copy-start.7
  60.9 0.0 copy-start.8
  60.9 0.0 copy-start.9
  60.9 1.0 slice_add_fusion.1
  61.9 0.8 slice_add_fusion
  62.7 0.0 copy-done.2
  62.8 0.0 copy-done.3
  62.8 0.0 copy-done.4
  62.8 0.0 copy-done.5
  62.8 1.2 %subtract_divide_fusion = f32[64,2048]{1,0:T(8,128)S(1)} fusion(f32[72,2048]{1,0:T(8,128)} %get-tuple-element.7, f32[2048]{0:T(1024)S(1)} %bitcast.134, f32[64,2048]{1,0:T(8,128)S(1)} %copy-done.2, f32[64,2048]{1,0:T(8,128)S(1)} %copy-done.3, f32[64,2048]{1,0:T(8,128)S(1)} %copy-done.4, f32[64,2048]{1,0:T(8,128)S(1)} %copy-done.5), kind=kLoop, calls=%fused_computation.81 | loop fusion | flops 786432 | bytes 3153920 | tf_op jit(solution)/shard_map/div | solution.py:262
  64.0 0.0 copy-start.11
  64.1 0.0 copy-done.12
  64.1 0.2 subtract_convert_fusion
  64.3 0.0 copy-done
  64.3 0.0 copy-done.6
  64.3 0.0 copy-done.7
  64.3 0.0 copy-done.8
  64.4 0.0 copy-done.9
  64.4 0.0 copy-start.16
  64.4 0.2 add_divide_fusion
  64.6 1.6 %copy-done.11 = bf16[2,1024,1024]{2,1,0:T(8,128)(2,1)S(1)} copy-done((bf16[2,1024,1024]{2,1,0:T(8,128)(2,1)S(1)}, bf16[2,1024,1024]{2,1,0:T(8,128)(2,1)}, u32[]{:S(2)}) %copy-start.11) | copy-done | bytes 4194328
  66.2 0.0 copy-start.14
  66.2 0.7 fusion.10
  66.9 0.0 copy-done.16
  67.0 0.9 fusion.66
  67.9 0.6 copy-done.14
  68.5 0.7 fusion
  69.2 1.0 select_reduce_fusion.3
  70.2 0.8 bitcast_bitcast_fusion.1.refs_0_
  71.0 0.7 fusion.8
  71.8 1.0 select_reduce_fusion.1
  72.7 0.8 bitcast_bitcast_fusion.refs_1_
  73.6 40.6 %shard_map.177 = (f32[64,2048]{1,0:T(8,128)}, f32[64,2048]{1,0:T(8,128)}) custom-call(f32[16,64,128]{2,1,0:T(8,128)} %bitcast_bitcast_fusion.1.refs_0_, f32[16,64,128]{2,1,0:T(8,128)} %bitcast_bitcast_fusion.refs_1_), custom_call_target="tpu_custom_call" | custom-call | tf_op jit(solution)/shard_map/pallas_call | solution.py:153
  114.2 2.4 %fusion.78 = f32[64,2048]{1,0:T(8,128)} fusion(f32[64,2048]{1,0:T(8,128)S(1)} %copy-done.3, f32[64,2048]{1,0:T(8,128)S(1)} %copy-done.4, f32[64,2048]{1,0:T(8,128)} %get-tuple-element.9, f32[2048]{0:T(1024)S(1)} %bitcast.135, f32[64,2048]{1,0:T(8,128)S(1)} %copy-done.2, f32[64,2048]{1,0:T(8,128)S(1)} %copy-done.5, f32[72,2048]{1,0:T(8,128)} %get-tuple-element.7), kind=kLoop, calls=%fused_computation.71 | loop fusion | flops 2490368 | bytes 3678208 | tf_op jit(solution)/shard_map/jit(clip)/min | solution.py:270
  116.6 2.7 %fusion.76 = f32[64,2048]{1,0:T(8,128)} fusion(f32[64,2048]{1,0:T(8,128)S(1)} %copy-done.6, f32[64,2048]{1,0:T(8,128)} %param.25, f32[64,2048]{1,0:T(8,128)} %get-tuple-element.8, f32[2048]{0:T(1024)S(1)} %bitcast.133, f32[64,2048]{1,0:T(8,128)} %param.24, f32[64,2048]{1,0:T(8,128)S(1)} %copy-done, f32[72,2048]{1,0:T(8,128)} %get-tuple-element.6), kind=kLoop, calls=%fused_computation.69 | loop fusion | flops 2621440 | bytes 3678208 | tf_op jit(solution)/shard_map/jit(clip)/min | solution.py:269
  (2 shorter events, 0.1 us)
Async XLA Ops:
  0.6 9.2 %copy-start.10 = (bf16[2,1024,1024]{2,1,0:T(8,128)(2,1)S(1)}, bf16[2,1024,1024]{2,1,0:T(8,128)(2,1)}, u32[]{:S(2)}) copy-start(bf16[2,1024,1024]{2,1,0:T(8,128)(2,1)} %param.17) | copy-start | bytes 12582916
  0.6 9.2 %copy-start.1 = (f32[1,1,4,64,1024]{4,3,2,1,0:T(8,128)S(1)}, f32[1,1,4,64,1024]{4,3,2,1,0:T(8,128)}, u32[]{:S(2)}) copy-start(f32[1,1,4,64,1024]{4,3,2,1,0:T(8,128)} %param.33) | copy-start | bytes 3145732
  7.3 3.5 %copy-start.13 = (bf16[2,1024,1024]{2,1,0:T(8,128)(2,1)S(1)}, bf16[2,1024,1024]{2,1,0:T(8,128)(2,1)}, u32[]{:S(2)}) copy-start(bf16[2,1024,1024]{2,1,0:T(8,128)(2,1)} %param.18) | copy-start | bytes 12582916
  13.4 1.6 %copy-start.15 = (f32[1,1,4,64,1024]{4,3,2,1,0:T(8,128)S(1)}, f32[1,1,4,64,1024]{4,3,2,1,0:T(8,128)}, u32[]{:S(2)}) copy-start(f32[1,1,4,64,1024]{4,3,2,1,0:T(8,128)} %param.32) | copy-start | bytes 3145732
  15.0 47.8 %copy-start.2 = (f32[64,2048]{1,0:T(8,128)S(1)}, f32[64,2048]{1,0:T(8,128)}, u32[]{:S(2)}) copy-start(f32[64,2048]{1,0:T(8,128)} %param.28) | copy-start | bytes 1572868
  15.0 47.8 %copy-start.3 = (f32[64,2048]{1,0:T(8,128)S(1)}, f32[64,2048]{1,0:T(8,128)}, u32[]{:S(2)}) copy-start(f32[64,2048]{1,0:T(8,128)} %param.30) | copy-start | bytes 1572868
  15.0 47.8 %copy-start.4 = (f32[64,2048]{1,0:T(8,128)S(1)}, f32[64,2048]{1,0:T(8,128)}, u32[]{:S(2)}) copy-start(f32[64,2048]{1,0:T(8,128)} %param.29) | copy-start | bytes 1572868
  15.0 47.8 %copy-start.5 = (f32[64,2048]{1,0:T(8,128)S(1)}, f32[64,2048]{1,0:T(8,128)}, u32[]{:S(2)}) copy-start(f32[64,2048]{1,0:T(8,128)} %param.27) | copy-start | bytes 1572868
  17.0 47.3 %copy-start = (f32[64,2048]{1,0:T(8,128)S(1)}, f32[64,2048]{1,0:T(8,128)}, u32[]{:S(2)}) copy-start(f32[64,2048]{1,0:T(8,128)} %param.23) | copy-start | bytes 1572868
  17.0 47.4 %copy-start.6 = (f32[64,2048]{1,0:T(8,128)S(1)}, f32[64,2048]{1,0:T(8,128)}, u32[]{:S(2)}) copy-start(f32[64,2048]{1,0:T(8,128)} %param.26) | copy-start | bytes 1572868
  60.9 3.2 %copy-start.12 = (f32[4,64,1024]{2,1,0:T(8,128)S(1)}, f32[4,64,1024]{2,1,0:T(8,128)}, u32[]{:S(2)}) copy-start(f32[4,64,1024]{2,1,0:T(8,128)} %get-tuple-element.32) | copy-start | bytes 3145732
  60.9 3.5 %copy-start.7 = (f32[64,2048]{1,0:T(8,128)S(1)}, f32[64,2048]{1,0:T(8,128)}, u32[]{:S(2)}) copy-start(f32[64,2048]{1,0:T(8,128)} %param.25) | copy-start | bytes 1572868
  60.9 3.5 %copy-start.8 = (f32[64,2048]{1,0:T(8,128)S(1)}, f32[64,2048]{1,0:T(8,128)}, u32[]{:S(2)}) copy-start(f32[64,2048]{1,0:T(8,128)} %param.24) | copy-start | bytes 1572868
  60.9 3.5 %copy-start.9 = (f32[72,2048]{1,0:T(8,128)S(1)}, f32[72,2048]{1,0:T(8,128)}, u32[]{:S(2)}) copy-start(f32[72,2048]{1,0:T(8,128)} %get-tuple-element.6) | copy-start | bytes 1769476
  64.0 2.2 %copy-start.11 = (bf16[2,1024,1024]{2,1,0:T(8,128)(2,1)S(1)}, bf16[2,1024,1024]{2,1,0:T(8,128)(2,1)}, u32[]{:S(2)}) copy-start(bf16[2,1024,1024]{2,1,0:T(8,128)(2,1)} %param.17) | copy-start | bytes 12582916
  64.4 2.6 %copy-start.16 = (f32[4,64,1024]{2,1,0:T(8,128)S(1)}, f32[4,64,1024]{2,1,0:T(8,128)}, u32[]{:S(2)}) copy-start(f32[4,64,1024]{2,1,0:T(8,128)} %get-tuple-element.18) | copy-start | bytes 3145732
  66.2 2.3 %copy-start.14 = (bf16[2,1024,1024]{2,1,0:T(8,128)(2,1)S(1)}, bf16[2,1024,1024]{2,1,0:T(8,128)(2,1)}, u32[]{:S(2)}) copy-start(bf16[2,1024,1024]{2,1,0:T(8,128)(2,1)} %param.18) | copy-start | bytes 12582916

commit v6 on v5

--- a/solution.py
+++ b/solution.py
@@ -27,14 +27,23 @@
     scratch = refs[2 * groups :]
     size = 7 if with_counts else 6
     per = [scratch[size * g : size * g + 6] for g in range(groups)]
-    width = ins[0].shape[2]
+    width = ins[0].shape[1] // n
     sources = list(ins)
+
+    def cols(index):
+        return pl.ds(pl.multiple_of(index * width, width), width)
+
+    def piece(ref, index):
+        if len(ref.shape) == 3:
+            return ref.at[index]
+        return ref.at[:, cols(index)]
+
     if with_counts:
         slots = (info.shape[0] - 1) // groups
         live = info[groups * slots]
         for g in range(groups):
             send = scratch[size * g + 6]
-            data_rows = ins[g].shape[1]
+            data_rows = ins[g].shape[0]
             extra = send.shape[1] - data_rows
             for p in range(n):
                 block = (p * width) // block_width
@@ -43,7 +52,7 @@
                     count = count + jnp.where(
                         (k < live) & (info[g * slots + k] == block), 1, 0
                     ).astype(jnp.int32)
-                send[p, :data_rows, :] = ins[g][p]
+                send[p, :data_rows, :] = ins[g][:, p * width : (p + 1) * width]
                 send[p, data_rows:, :] = jnp.full((extra, width), count, jnp.int32).astype(
                     jnp.float32
                 )
@@ -64,7 +73,7 @@
         for k in range(1, n):
             peer = lax.rem(me + k, n)
             copy = pltpu.make_async_remote_copy(
-                src_ref=sources[g].at[peer],
+                src_ref=piece(sources[g], peer),
                 dst_ref=recv.at[me],
                 send_sem=s1.at[peer],
                 recv_sem=r1.at[me],
@@ -82,14 +91,14 @@
         for k in range(1, n):
             source = lax.rem(me + n - k, n)
             pltpu.make_async_remote_copy(
-                src_ref=sources[g].at[source],
+                src_ref=piece(sources[g], source),
                 dst_ref=recv.at[source],
                 send_sem=s1.at[source],
                 recv_sem=r1.at[source],
                 device_id=peer_id(axis, source),
                 device_id_type=MESH,
             ).wait_recv()
-        total = sources[g][me]
+        total = piece(sources[g], me)[...]
         for k in range(1, n):
             total = total + recv[lax.rem(me + k, n)]
         gathered[me] = total
@@ -133,7 +142,6 @@
     extra = 0 if info is None else 8
     shapes = [(a.shape[0] + extra, a.shape[1]) for a in arrays]
     width = shapes[0][1] // n
-    arrays = [a.reshape(a.shape[0], n, width).transpose(1, 0, 2) for a in arrays]
     scratch = []
     for rows, _ in shapes:
         scratch += [

time: 120 us -> 119 us (level)
  the two profiles are of different devices: /device:TPU:25 before, /device:TPU:2 now
where the time goes in v6:
time: 119 us; the launch traced here: 118 us
  Pallas kernels  82.8 us (70%)
  other arithmetic  16.7 us (14%)
  matrix products  13.8 us (12%)
  local copies, waits for them, and re-layouts  3.38 us (3%)
  between operations  1.78 us (1%)
    pallas_call x2, Pallas kernels, all_reduce(): pl.pallas_call(functools.partial(reduce_kernel, n, group_axes, block_widt...  82.8 us
    dot_general x12, matrix products, by_tile(): lax.dot_general(stacked, matrices[t], (((1,), (contract,)), ((), ())), pr...  13.8 us
    min x1, other arithmetic, per_device(): column_final = jnp.clip(x_own - x_dual - unit_cost, 0.0, capacity)  2.73 us
    min x1, other arithmetic, per_device(): row_final = jnp.clip(y_state - y_dual, row_lower, row_upper)  2.41 us

profile of v6, /device:TPU:2, one launch (start us, length us, event | category | flops | bytes accessed | tf_op | source)
XLA Modules:
  0.0 118.4 jit_solution(8058346342704659415)
XLA Ops:
  0.6 0.0 copy-start.10
  0.6 0.0 copy-start.1
  1.4 1.1 compare_bitcast_fusion
  2.5 1.3 %pad_add_fusion.refs_0_ = s32[9]{0:T(128)} fusion(s32[1]{0:T(128)} %bitcast.102, s32[4]{0:T(128)} %bitcast.109, s32[4]{0:T(128)} %bitcast.108), kind=kLoop, calls=%fused_computation.90 | loop fusion | flops 18 | bytes 72 | tf_op jit(solution)/shard_map/concatenate | solution.py:258
  3.8 0.7 fusion.85
  4.5 1.7 %fusion.79 = bf16[4,64,1024]{2,1,0:T(8,128)(2,1)S(1)} fusion(f32[1,1,4,64,1024]{4,3,2,1,0:T(8,128)} %param.31, f32[1,1,4,64,1024]{4,3,2,1,0:T(8,128)} %param.32), kind=kLoop, calls=%fused_computation.72 | loop fusion | flops 524288 | bytes 2621440 | tf_op jit(solution)/shard_map/convert_element_type | solution.py:240
  6.2 1.1 fusion.88
  7.3 0.0 copy-start.13
  7.3 2.5 %fusion.14 = f32[4,64,1024]{2,1,0:T(8,128)S(1)} fusion(bf16[4,64,1024]{2,1,0:T(8,128)(2,1)S(1)} %fusion.79, bf16[2,1024,1024]{2,1,0:T(8,128)(2,1)} %param.17), kind=kOutput, calls=%fused_computation.14 | convolution fusion | flops 536870912 | bytes 3670016 | tf_op jit(solution)/shard_map/dot_general | solution.py:182
  9.8 0.0 copy-done.10
  9.8 0.0 copy-done.1
  9.8 0.9 fusion.69
  10.8 0.0 copy-done.13
  10.8 0.7 fusion.2
  11.5 1.9 %select_reduce_fusion.7 = (f32[64,1024]{1,0:T(8,128)S(1)}, f32[64,1024]{1,0:T(8,128)S(1)}, f32[4,64,1024]{2,1,0:T(8,128)}, bf16[4,64,1024]{2,1,0:T(8,128)(2,1)S(1)}) fusion(pred[4]{0:T(512)(128)(4,1)S(1)} %get-tuple-element.30, pred[4]{0:T(512)(128)(4,1)S(1)} %get-tuple-element.28, f32[1,1,4,64,1024]{4,3,2,1,0:T(8,128)S(1)} %copy-done.1, ...), kind=kOutput, calls=%fused_computation.62 | convolution fusion | flops 538574848 | bytes 6817280 | tf_op jit(solution)/shard_map/dot_general | solution.py:182
  13.4 0.0 copy-start.15
  13.4 0.8 pad_maximum_fusion.refs_1_
  14.2 0.7 fusion.12
  15.0 0.0 copy-done.15
  15.0 0.0 copy-start.2
  15.0 0.0 copy-start.3
  15.0 0.0 copy-start.4
  15.0 0.0 copy-start.5
  15.0 1.9 %select_reduce_fusion.5 = (f32[64,1024]{1,0:T(8,128)S(1)}, f32[64,1024]{1,0:T(8,128)S(1)}, f32[4,64,1024]{2,1,0:T(8,128)}) fusion(pred[4]{0:T(512)(128)(4,1)S(1)} %get-tuple-element.34, pred[4]{0:T(512)(128)(4,1)S(1)} %get-tuple-element.35, f32[1,1,4,64,1024]{4,3,2,1,0:T(8,128)S(1)} %copy-done.15, f32[4,64,1024]{2,1,0:T(8,128)S(1)} %fusion.12, ...), kind=kOutput, calls=%fused_computation.60 | convolution fusion | flops 538312704 | bytes 6292992 | tf_op jit(solution)/shard_map/dot_general | solution.py:182
  17.0 0.0 copy-start
  17.0 0.0 copy-start.6
  17.0 0.8 pad_maximum_fusion.1.refs_2_
  17.8 43.7 %shard_map.176 = (f32[72,2048]{1,0:T(8,128)}, f32[72,2048]{1,0:T(8,128)}) custom-call(s32[9]{0:T(128)} %pad_add_fusion.refs_0_, f32[64,2048]{1,0:T(8,128)} %pad_maximum_fusion.refs_1_, f32[64,2048]{1,0:T(8,128)} %pad_maximum_fusion.1.refs_2_), custom_call_target="tpu_custom_call" | custom-call | tf_op jit(solution)/shard_map/pallas_call | solution.py:161
  61.5 0.0 copy-start.12
  61.5 0.0 copy-start.7
  61.6 0.0 copy-start.8
  61.6 0.0 copy-start.9
  61.6 1.0 slice_add_fusion.1
  62.6 0.8 slice_add_fusion
  63.4 0.0 copy-done.2
  63.4 0.0 copy-done.3
  63.4 0.0 copy-done.4
  63.4 0.0 copy-done.5
  63.5 1.2 %subtract_divide_fusion = f32[64,2048]{1,0:T(8,128)S(1)} fusion(f32[72,2048]{1,0:T(8,128)} %get-tuple-element.7, f32[2048]{0:T(1024)S(1)} %bitcast.106, f32[64,2048]{1,0:T(8,128)S(1)} %copy-done.2, f32[64,2048]{1,0:T(8,128)S(1)} %copy-done.3, f32[64,2048]{1,0:T(8,128)S(1)} %copy-done.4, f32[64,2048]{1,0:T(8,128)S(1)} %copy-done.5), kind=kLoop, calls=%fused_computation.77 | loop fusion | flops 786432 | bytes 3153920 | tf_op jit(solution)/shard_map/div | solution.py:270
  64.7 0.0 copy-start.11
  64.7 0.0 copy-done.12
  64.7 0.2 subtract_convert_fusion
  65.0 0.0 copy-done
  65.0 0.0 copy-done.6
  65.0 0.0 copy-done.7
  65.0 0.0 copy-done.8
  65.0 0.0 copy-done.9
  65.0 0.0 copy-start.16
  65.0 0.2 add_divide_fusion
  65.3 1.6 %copy-done.11 = bf16[2,1024,1024]{2,1,0:T(8,128)(2,1)S(1)} copy-done((bf16[2,1024,1024]{2,1,0:T(8,128)(2,1)S(1)}, bf16[2,1024,1024]{2,1,0:T(8,128)(2,1)}, u32[]{:S(2)}) %copy-start.11) | copy-done | bytes 4194328
  66.9 0.0 copy-start.14
  66.9 0.7 fusion.10
  67.6 0.0 copy-done.16
  67.6 0.9 fusion.66
  68.5 0.6 copy-done.14
  69.1 0.7 fusion
  69.8 1.0 select_reduce_fusion.3
  70.9 0.8 pad_maximum_fusion.2.refs_0_
  71.7 0.7 fusion.8
  72.4 1.0 select_reduce_fusion.1
  73.4 0.8 pad_maximum_fusion.3.refs_1_
  74.2 39.1 %shard_map.177 = (f32[64,2048]{1,0:T(8,128)}, f32[64,2048]{1,0:T(8,128)}) custom-call(f32[64,2048]{1,0:T(8,128)} %pad_maximum_fusion.2.refs_0_, f32[64,2048]{1,0:T(8,128)} %pad_maximum_fusion.3.refs_1_), custom_call_target="tpu_custom_call" | custom-call | tf_op jit(solution)/shard_map/pallas_call | solution.py:161
  113.3 2.4 %fusion.78 = f32[64,2048]{1,0:T(8,128)} fusion(f32[64,2048]{1,0:T(8,128)S(1)} %copy-done.3, f32[64,2048]{1,0:T(8,128)S(1)} %copy-done.4, f32[64,2048]{1,0:T(8,128)} %get-tuple-element.9, f32[2048]{0:T(1024)S(1)} %bitcast.107, f32[64,2048]{1,0:T(8,128)S(1)} %copy-done.2, f32[64,2048]{1,0:T(8,128)S(1)} %copy-done.5, f32[72,2048]{1,0:T(8,128)} %get-tuple-element.7), kind=kLoop, calls=%fused_computation.71 | loop fusion | flops 2490368 | bytes 3678208 | tf_op jit(solution)/shard_map/jit(clip)/min | solution.py:278
  115.7 2.7 %fusion.76 = f32[64,2048]{1,0:T(8,128)} fusion(f32[64,2048]{1,0:T(8,128)S(1)} %copy-done.6, f32[64,2048]{1,0:T(8,128)} %param.25, f32[64,2048]{1,0:T(8,128)} %get-tuple-element.8, f32[2048]{0:T(1024)S(1)} %bitcast.105, f32[64,2048]{1,0:T(8,128)} %param.24, f32[64,2048]{1,0:T(8,128)S(1)} %copy-done, f32[72,2048]{1,0:T(8,128)} %get-tuple-element.6), kind=kLoop, calls=%fused_computation.69 | loop fusion | flops 2621440 | bytes 3678208 | tf_op jit(solution)/shard_map/jit(clip)/min | solution.py:277
  (2 shorter events, 0.1 us)
Async XLA Ops:
  0.6 9.2 %copy-start.10 = (bf16[2,1024,1024]{2,1,0:T(8,128)(2,1)S(1)}, bf16[2,1024,1024]{2,1,0:T(8,128)(2,1)}, u32[]{:S(2)}) copy-start(bf16[2,1024,1024]{2,1,0:T(8,128)(2,1)} %param.17) | copy-start | bytes 12582916
  0.6 9.2 %copy-start.1 = (f32[1,1,4,64,1024]{4,3,2,1,0:T(8,128)S(1)}, f32[1,1,4,64,1024]{4,3,2,1,0:T(8,128)}, u32[]{:S(2)}) copy-start(f32[1,1,4,64,1024]{4,3,2,1,0:T(8,128)} %param.33) | copy-start | bytes 3145732
  7.3 3.5 %copy-start.13 = (bf16[2,1024,1024]{2,1,0:T(8,128)(2,1)S(1)}, bf16[2,1024,1024]{2,1,0:T(8,128)(2,1)}, u32[]{:S(2)}) copy-start(bf16[2,1024,1024]{2,1,0:T(8,128)(2,1)} %param.18) | copy-start | bytes 12582916
  13.4 1.6 %copy-start.15 = (f32[1,1,4,64,1024]{4,3,2,1,0:T(8,128)S(1)}, f32[1,1,4,64,1024]{4,3,2,1,0:T(8,128)}, u32[]{:S(2)}) copy-start(f32[1,1,4,64,1024]{4,3,2,1,0:T(8,128)} %param.32) | copy-start | bytes 3145732
  15.0 48.5 %copy-start.2 = (f32[64,2048]{1,0:T(8,128)S(1)}, f32[64,2048]{1,0:T(8,128)}, u32[]{:S(2)}) copy-start(f32[64,2048]{1,0:T(8,128)} %param.28) | copy-start | bytes 1572868
  15.0 48.5 %copy-start.3 = (f32[64,2048]{1,0:T(8,128)S(1)}, f32[64,2048]{1,0:T(8,128)}, u32[]{:S(2)}) copy-start(f32[64,2048]{1,0:T(8,128)} %param.30) | copy-start | bytes 1572868
  15.0 48.5 %copy-start.4 = (f32[64,2048]{1,0:T(8,128)S(1)}, f32[64,2048]{1,0:T(8,128)}, u32[]{:S(2)}) copy-start(f32[64,2048]{1,0:T(8,128)} %param.29) | copy-start | bytes 1572868
  15.0 48.4 %copy-start.5 = (f32[64,2048]{1,0:T(8,128)S(1)}, f32[64,2048]{1,0:T(8,128)}, u32[]{:S(2)}) copy-start(f32[64,2048]{1,0:T(8,128)} %param.27) | copy-start | bytes 1572868
  17.0 48.0 %copy-start = (f32[64,2048]{1,0:T(8,128)S(1)}, f32[64,2048]{1,0:T(8,128)}, u32[]{:S(2)}) copy-start(f32[64,2048]{1,0:T(8,128)} %param.23) | copy-start | bytes 1572868
  17.0 48.0 %copy-start.6 = (f32[64,2048]{1,0:T(8,128)S(1)}, f32[64,2048]{1,0:T(8,128)}, u32[]{:S(2)}) copy-start(f32[64,2048]{1,0:T(8,128)} %param.26) | copy-start | bytes 1572868
  61.5 3.2 %copy-start.12 = (f32[4,64,1024]{2,1,0:T(8,128)S(1)}, f32[4,64,1024]{2,1,0:T(8,128)}, u32[]{:S(2)}) copy-start(f32[4,64,1024]{2,1,0:T(8,128)} %get-tuple-element.32) | copy-start | bytes 3145732
  61.5 3.5 %copy-start.7 = (f32[64,2048]{1,0:T(8,128)S(1)}, f32[64,2048]{1,0:T(8,128)}, u32[]{:S(2)}) copy-start(f32[64,2048]{1,0:T(8,128)} %param.25) | copy-start | bytes 1572868
  61.6 3.5 %copy-start.8 = (f32[64,2048]{1,0:T(8,128)S(1)}, f32[64,2048]{1,0:T(8,128)}, u32[]{:S(2)}) copy-start(f32[64,2048]{1,0:T(8,128)} %param.24) | copy-start | bytes 1572868
  61.6 3.5 %copy-start.9 = (f32[72,2048]{1,0:T(8,128)S(1)}, f32[72,2048]{1,0:T(8,128)}, u32[]{:S(2)}) copy-start(f32[72,2048]{1,0:T(8,128)} %get-tuple-element.6) | copy-start | bytes 1769476
  64.7 2.2 %copy-start.11 = (bf16[2,1024,1024]{2,1,0:T(8,128)(2,1)S(1)}, bf16[2,1024,1024]{2,1,0:T(8,128)(2,1)}, u32[]{:S(2)}) copy-start(bf16[2,1024,1024]{2,1,0:T(8,128)(2,1)} %param.17) | copy-start | bytes 12582916
  65.0 2.6 %copy-start.16 = (f32[4,64,1024]{2,1,0:T(8,128)S(1)}, f32[4,64,1024]{2,1,0:T(8,128)}, u32[]{:S(2)}) copy-start(f32[4,64,1024]{2,1,0:T(8,128)} %get-tuple-element.18) | copy-start | bytes 3145732
  66.9 2.3 %copy-start.14 = (bf16[2,1024,1024]{2,1,0:T(8,128)(2,1)S(1)}, bf16[2,1024,1024]{2,1,0:T(8,128)(2,1)}, u32[]{:S(2)}) copy-start(bf16[2,1024,1024]{2,1,0:T(8,128)(2,1)} %param.18) | copy-start | bytes 12582916

commit v7 on v6

--- a/solution.py
+++ b/solution.py
@@ -101,13 +101,13 @@
         total = piece(sources[g], me)[...]
         for k in range(1, n):
             total = total + recv[lax.rem(me + k, n)]
-        gathered[me] = total
+        outs[g][:, cols(me)] = total
         copies = []
         for k in range(1, n):
             peer = lax.rem(me + k, n)
             copy = pltpu.make_async_remote_copy(
-                src_ref=gathered.at[me],
-                dst_ref=gathered.at[me],
+                src_ref=outs[g].at[:, cols(me)],
+                dst_ref=outs[g].at[:, cols(me)],
                 send_sem=s2.at[peer],
                 recv_sem=r2.at[me],
                 device_id=peer_id(axis, peer),
@@ -125,8 +125,8 @@
         for k in range(1, n):
             source = lax.rem(me + n - k, n)
             pltpu.make_async_remote_copy(
-                src_ref=gathered.at[source],
-                dst_ref=gathered.at[source],
+                src_ref=outs[g].at[:, cols(source)],
+                dst_ref=outs[g].at[:, cols(source)],
                 send_sem=s2.at[source],
                 recv_sem=r2.at[source],
                 device_id=peer_id(axis, source),
@@ -134,8 +134,6 @@
             ).wait_recv()
         for copy in gathers[g]:
             copy.wait_send()
-        for index in range(n):
-            outs[g][:, index * width : (index + 1) * width] = gathered[index]
 
 
 def all_reduce(arrays, group_axes, n, collective_id, block_width, info=None):

time: 119 us -> 119 us (level)
  no operation moved by 1% of the time
where the time goes in v7:
time: 119 us; the launch traced here: 118 us
  Pallas kernels  82.8 us (70%)
  other arithmetic  16.7 us (14%)
  matrix products  13.8 us (12%)
  local copies, waits for them, and re-layouts  3.38 us (3%)
  between operations  1.78 us (1%)
    pallas_call x2, Pallas kernels, all_reduce(): pl.pallas_call(functools.partial(reduce_kernel, n, group_axes, block_widt...  82.8 us
    dot_general x12, matrix products, by_tile(): lax.dot_general(stacked, matrices[t], (((1,), (contract,)), ((), ())), pr...  13.8 us
    min x1, other arithmetic, per_device(): column_final = jnp.clip(x_own - x_dual - unit_cost, 0.0, capacity)  2.73 us
    min x1, other arithmetic, per_device(): row_final = jnp.clip(y_state - y_dual, row_lower, row_upper)  2.41 us

profile of v7, /device:TPU:2, one launch (start us, length us, event | category | flops | bytes accessed | tf_op | source)
XLA Modules:
  0.0 118.5 jit_solution(12836665178746389160)
XLA Ops:
  0.6 0.0 copy-start.10
  0.6 0.0 copy-start.1
  1.4 1.1 compare_bitcast_fusion
  2.5 1.3 %pad_add_fusion.refs_0_ = s32[9]{0:T(128)} fusion(s32[1]{0:T(128)} %bitcast.102, s32[4]{0:T(128)} %bitcast.109, s32[4]{0:T(128)} %bitcast.108), kind=kLoop, calls=%fused_computation.90 | loop fusion | flops 18 | bytes 72 | tf_op jit(solution)/shard_map/concatenate | solution.py:256
  3.8 0.7 fusion.85
  4.5 1.7 %fusion.79 = bf16[4,64,1024]{2,1,0:T(8,128)(2,1)S(1)} fusion(f32[1,1,4,64,1024]{4,3,2,1,0:T(8,128)} %param.31, f32[1,1,4,64,1024]{4,3,2,1,0:T(8,128)} %param.32), kind=kLoop, calls=%fused_computation.72 | loop fusion | flops 524288 | bytes 2621440 | tf_op jit(solution)/shard_map/convert_element_type | solution.py:238
  6.2 1.1 fusion.88
  7.3 0.0 copy-start.13
  7.3 2.5 %fusion.14 = f32[4,64,1024]{2,1,0:T(8,128)S(1)} fusion(bf16[4,64,1024]{2,1,0:T(8,128)(2,1)S(1)} %fusion.79, bf16[2,1024,1024]{2,1,0:T(8,128)(2,1)} %param.17), kind=kOutput, calls=%fused_computation.14 | convolution fusion | flops 536870912 | bytes 3670016 | tf_op jit(solution)/shard_map/dot_general | solution.py:180
  9.8 0.0 copy-done.10
  9.8 0.0 copy-done.1
  9.8 0.9 fusion.69
  10.8 0.0 copy-done.13
  10.8 0.7 fusion.2
  11.5 1.9 %select_reduce_fusion.7 = (f32[64,1024]{1,0:T(8,128)S(1)}, f32[64,1024]{1,0:T(8,128)S(1)}, f32[4,64,1024]{2,1,0:T(8,128)}, bf16[4,64,1024]{2,1,0:T(8,128)(2,1)S(1)}) fusion(pred[4]{0:T(512)(128)(4,1)S(1)} %get-tuple-element.30, pred[4]{0:T(512)(128)(4,1)S(1)} %get-tuple-element.28, f32[1,1,4,64,1024]{4,3,2,1,0:T(8,128)S(1)} %copy-done.1, ...), kind=kOutput, calls=%fused_computation.62 | convolution fusion | flops 538574848 | bytes 6817280 | tf_op jit(solution)/shard_map/dot_general | solution.py:180
  13.4 0.0 copy-start.15
  13.4 0.8 pad_maximum_fusion.refs_1_
  14.2 0.7 fusion.12
  15.0 0.0 copy-done.15
  15.0 0.0 copy-start.2
  15.0 0.0 copy-start.3
  15.0 0.0 copy-start.4
  15.0 0.0 copy-start.5
  15.0 1.9 %select_reduce_fusion.5 = (f32[64,1024]{1,0:T(8,128)S(1)}, f32[64,1024]{1,0:T(8,128)S(1)}, f32[4,64,1024]{2,1,0:T(8,128)}) fusion(pred[4]{0:T(512)(128)(4,1)S(1)} %get-tuple-element.34, pred[4]{0:T(512)(128)(4,1)S(1)} %get-tuple-element.35, f32[1,1,4,64,1024]{4,3,2,1,0:T(8,128)S(1)} %copy-done.15, f32[4,64,1024]{2,1,0:T(8,128)S(1)} %fusion.12, ...), kind=kOutput, calls=%fused_computation.60 | convolution fusion | flops 538312704 | bytes 6292992 | tf_op jit(solution)/shard_map/dot_general | solution.py:180
  17.0 0.0 copy-start
  17.0 0.0 copy-start.6
  17.0 0.8 pad_maximum_fusion.1.refs_2_
  17.8 43.7 %shard_map.176 = (f32[72,2048]{1,0:T(8,128)}, f32[72,2048]{1,0:T(8,128)}) custom-call(s32[9]{0:T(128)} %pad_add_fusion.refs_0_, f32[64,2048]{1,0:T(8,128)} %pad_maximum_fusion.refs_1_, f32[64,2048]{1,0:T(8,128)} %pad_maximum_fusion.1.refs_2_), custom_call_target="tpu_custom_call" | custom-call | tf_op jit(solution)/shard_map/pallas_call | solution.py:159
  61.5 0.0 copy-start.12
  61.5 0.0 copy-start.7
  61.6 0.0 copy-start.8
  61.6 0.0 copy-start.9
  61.6 1.0 slice_add_fusion.1
  62.6 0.8 slice_add_fusion
  63.4 0.0 copy-done.2
  63.4 0.0 copy-done.3
  63.4 0.0 copy-done.4
  63.4 0.0 copy-done.5
  63.5 1.2 %subtract_divide_fusion = f32[64,2048]{1,0:T(8,128)S(1)} fusion(f32[72,2048]{1,0:T(8,128)} %get-tuple-element.7, f32[2048]{0:T(1024)S(1)} %bitcast.106, f32[64,2048]{1,0:T(8,128)S(1)} %copy-done.2, f32[64,2048]{1,0:T(8,128)S(1)} %copy-done.3, f32[64,2048]{1,0:T(8,128)S(1)} %copy-done.4, f32[64,2048]{1,0:T(8,128)S(1)} %copy-done.5), kind=kLoop, calls=%fused_computation.77 | loop fusion | flops 786432 | bytes 3153920 | tf_op jit(solution)/shard_map/div | solution.py:268
  64.7 0.0 copy-start.11
  64.7 0.0 copy-done.12
  64.7 0.2 subtract_convert_fusion
  65.0 0.0 copy-done
  65.0 0.0 copy-done.6
  65.0 0.0 copy-done.7
  65.0 0.0 copy-done.8
  65.0 0.0 copy-done.9
  65.0 0.0 copy-start.16
  65.0 0.2 add_divide_fusion
  65.3 1.6 %copy-done.11 = bf16[2,1024,1024]{2,1,0:T(8,128)(2,1)S(1)} copy-done((bf16[2,1024,1024]{2,1,0:T(8,128)(2,1)S(1)}, bf16[2,1024,1024]{2,1,0:T(8,128)(2,1)}, u32[]{:S(2)}) %copy-start.11) | copy-done | bytes 4194328
  66.9 0.0 copy-start.14
  66.9 0.7 fusion.10
  67.6 0.0 copy-done.16
  67.6 0.9 fusion.66
  68.5 0.6 copy-done.14
  69.1 0.7 fusion
  69.8 1.0 select_reduce_fusion.3
  70.9 0.8 pad_maximum_fusion.2.refs_0_
  71.7 0.7 fusion.8
  72.4 1.0 select_reduce_fusion.1
  73.4 0.8 pad_maximum_fusion.3.refs_1_
  74.2 39.1 %shard_map.177 = (f32[64,2048]{1,0:T(8,128)}, f32[64,2048]{1,0:T(8,128)}) custom-call(f32[64,2048]{1,0:T(8,128)} %pad_maximum_fusion.2.refs_0_, f32[64,2048]{1,0:T(8,128)} %pad_maximum_fusion.3.refs_1_), custom_call_target="tpu_custom_call" | custom-call | tf_op jit(solution)/shard_map/pallas_call | solution.py:159
  113.3 2.4 %fusion.78 = f32[64,2048]{1,0:T(8,128)} fusion(f32[64,2048]{1,0:T(8,128)S(1)} %copy-done.3, f32[64,2048]{1,0:T(8,128)S(1)} %copy-done.4, f32[64,2048]{1,0:T(8,128)} %get-tuple-element.9, f32[2048]{0:T(1024)S(1)} %bitcast.107, f32[64,2048]{1,0:T(8,128)S(1)} %copy-done.2, f32[64,2048]{1,0:T(8,128)S(1)} %copy-done.5, f32[72,2048]{1,0:T(8,128)} %get-tuple-element.7), kind=kLoop, calls=%fused_computation.71 | loop fusion | flops 2490368 | bytes 3678208 | tf_op jit(solution)/shard_map/jit(clip)/min | solution.py:276
  115.8 2.7 %fusion.76 = f32[64,2048]{1,0:T(8,128)} fusion(f32[64,2048]{1,0:T(8,128)S(1)} %copy-done.6, f32[64,2048]{1,0:T(8,128)} %param.25, f32[64,2048]{1,0:T(8,128)} %get-tuple-element.8, f32[2048]{0:T(1024)S(1)} %bitcast.105, f32[64,2048]{1,0:T(8,128)} %param.24, f32[64,2048]{1,0:T(8,128)S(1)} %copy-done, f32[72,2048]{1,0:T(8,128)} %get-tuple-element.6), kind=kLoop, calls=%fused_computation.69 | loop fusion | flops 2621440 | bytes 3678208 | tf_op jit(solution)/shard_map/jit(clip)/min | solution.py:275
  (2 shorter events, 0.1 us)
Async XLA Ops:
  0.6 9.2 %copy-start.10 = (bf16[2,1024,1024]{2,1,0:T(8,128)(2,1)S(1)}, bf16[2,1024,1024]{2,1,0:T(8,128)(2,1)}, u32[]{:S(2)}) copy-start(bf16[2,1024,1024]{2,1,0:T(8,128)(2,1)} %param.17) | copy-start | bytes 12582916
  0.6 9.2 %copy-start.1 = (f32[1,1,4,64,1024]{4,3,2,1,0:T(8,128)S(1)}, f32[1,1,4,64,1024]{4,3,2,1,0:T(8,128)}, u32[]{:S(2)}) copy-start(f32[1,1,4,64,1024]{4,3,2,1,0:T(8,128)} %param.33) | copy-start | bytes 3145732
  7.3 3.5 %copy-start.13 = (bf16[2,1024,1024]{2,1,0:T(8,128)(2,1)S(1)}, bf16[2,1024,1024]{2,1,0:T(8,128)(2,1)}, u32[]{:S(2)}) copy-start(bf16[2,1024,1024]{2,1,0:T(8,128)(2,1)} %param.18) | copy-start | bytes 12582916
  13.4 1.6 %copy-start.15 = (f32[1,1,4,64,1024]{4,3,2,1,0:T(8,128)S(1)}, f32[1,1,4,64,1024]{4,3,2,1,0:T(8,128)}, u32[]{:S(2)}) copy-start(f32[1,1,4,64,1024]{4,3,2,1,0:T(8,128)} %param.32) | copy-start | bytes 3145732
  15.0 48.5 %copy-start.2 = (f32[64,2048]{1,0:T(8,128)S(1)}, f32[64,2048]{1,0:T(8,128)}, u32[]{:S(2)}) copy-start(f32[64,2048]{1,0:T(8,128)} %param.28) | copy-start | bytes 1572868
  15.0 48.4 %copy-start.3 = (f32[64,2048]{1,0:T(8,128)S(1)}, f32[64,2048]{1,0:T(8,128)}, u32[]{:S(2)}) copy-start(f32[64,2048]{1,0:T(8,128)} %param.30) | copy-start | bytes 1572868
  15.0 48.4 %copy-start.4 = (f32[64,2048]{1,0:T(8,128)S(1)}, f32[64,2048]{1,0:T(8,128)}, u32[]{:S(2)}) copy-start(f32[64,2048]{1,0:T(8,128)} %param.29) | copy-start | bytes 1572868
  15.0 48.4 %copy-start.5 = (f32[64,2048]{1,0:T(8,128)S(1)}, f32[64,2048]{1,0:T(8,128)}, u32[]{:S(2)}) copy-start(f32[64,2048]{1,0:T(8,128)} %param.27) | copy-start | bytes 1572868
  17.0 48.0 %copy-start = (f32[64,2048]{1,0:T(8,128)S(1)}, f32[64,2048]{1,0:T(8,128)}, u32[]{:S(2)}) copy-start(f32[64,2048]{1,0:T(8,128)} %param.23) | copy-start | bytes 1572868
  17.0 48.0 %copy-start.6 = (f32[64,2048]{1,0:T(8,128)S(1)}, f32[64,2048]{1,0:T(8,128)}, u32[]{:S(2)}) copy-start(f32[64,2048]{1,0:T(8,128)} %param.26) | copy-start | bytes 1572868
  61.5 3.2 %copy-start.12 = (f32[4,64,1024]{2,1,0:T(8,128)S(1)}, f32[4,64,1024]{2,1,0:T(8,128)}, u32[]{:S(2)}) copy-start(f32[4,64,1024]{2,1,0:T(8,128)} %get-tuple-element.32) | copy-start | bytes 3145732
  61.5 3.5 %copy-start.7 = (f32[64,2048]{1,0:T(8,128)S(1)}, f32[64,2048]{1,0:T(8,128)}, u32[]{:S(2)}) copy-start(f32[64,2048]{1,0:T(8,128)} %param.25) | copy-start | bytes 1572868
  61.6 3.5 %copy-start.8 = (f32[64,2048]{1,0:T(8,128)S(1)}, f32[64,2048]{1,0:T(8,128)}, u32[]{:S(2)}) copy-start(f32[64,2048]{1,0:T(8,128)} %param.24) | copy-start | bytes 1572868
  61.6 3.5 %copy-start.9 = (f32[72,2048]{1,0:T(8,128)S(1)}, f32[72,2048]{1,0:T(8,128)}, u32[]{:S(2)}) copy-start(f32[72,2048]{1,0:T(8,128)} %get-tuple-element.6) | copy-start | bytes 1769476
  64.7 2.2 %copy-start.11 = (bf16[2,1024,1024]{2,1,0:T(8,128)(2,1)S(1)}, bf16[2,1024,1024]{2,1,0:T(8,128)(2,1)}, u32[]{:S(2)}) copy-start(bf16[2,1024,1024]{2,1,0:T(8,128)(2,1)} %param.17) | copy-start | bytes 12582916
  65.0 2.6 %copy-start.16 = (f32[4,64,1024]{2,1,0:T(8,128)S(1)}, f32[4,64,1024]{2,1,0:T(8,128)}, u32[]{:S(2)}) copy-start(f32[4,64,1024]{2,1,0:T(8,128)} %get-tuple-element.18) | copy-start | bytes 3145732
  66.9 2.3 %copy-start.14 = (bf16[2,1024,1024]{2,1,0:T(8,128)(2,1)S(1)}, bf16[2,1024,1024]{2,1,0:T(8,128)(2,1)}, u32[]{:S(2)}) copy-start(bf16[2,1024,1024]{2,1,0:T(8,128)(2,1)} %param.18) | copy-start | bytes 12582916

commit v8 on v7

--- a/solution.py
+++ b/solution.py
@@ -18,13 +18,19 @@
     return (lax.axis_index("row"), peer)
 
 
-def reduce_kernel(n, group_axes, block_width, with_counts, *refs):
+def reduce_kernel(n, group_axes, block_width, with_counts, finish, *refs):
     groups = len(group_axes)
     if with_counts:
         info, refs = refs[0], refs[1:]
     ins = refs[:groups]
-    outs = refs[groups : 2 * groups]
-    scratch = refs[2 * groups :]
+    refs = refs[groups:]
+    operands = []
+    if finish is not None:
+        for g in range(groups):
+            operands.append(refs[: finish[g][1]])
+            refs = refs[finish[g][1] :]
+    outs = refs[:groups]
+    scratch = refs[groups:]
     size = 7 if with_counts else 6
     per = [scratch[size * g : size * g + 6] for g in range(groups)]
     width = ins[0].shape[1] // n
@@ -101,6 +107,8 @@
         total = piece(sources[g], me)[...]
         for k in range(1, n):
             total = total + recv[lax.rem(me + k, n)]
+        if finish is not None:
+            total = finish[g][0](total, *[ref[:, cols(me)] for ref in operands[g]])
         outs[g][:, cols(me)] = total
         copies = []
         for k in range(1, n):
@@ -136,7 +144,7 @@
             copy.wait_send()
 
 
-def all_reduce(arrays, group_axes, n, collective_id, block_width, info=None):
+def all_reduce(arrays, group_axes, n, collective_id, block_width, info=None, finish=None):
     extra = 0 if info is None else 8
     shapes = [(a.shape[0] + extra, a.shape[1]) for a in arrays]
     width = shapes[0][1] // n
@@ -152,18 +160,35 @@
         ]
         if info is not None:
             scratch.append(pltpu.VMEM((n, rows, width), jnp.float32))
+    rules = None
+    if finish is not None:
+        rules = tuple((rule, len(extra)) for rule, extra in finish)
+        arrays = arrays + [a for _, extra in finish for a in extra]
     in_specs = [pl.BlockSpec(memory_space=pltpu.VMEM)] * len(arrays)
     if info is not None:
         in_specs = [pl.BlockSpec(memory_space=pltpu.SMEM)] + in_specs
         arrays = [info] + arrays
     return pl.pallas_call(
-        functools.partial(reduce_kernel, n, group_axes, block_width, info is not None),
+        functools.partial(reduce_kernel, n, group_axes, block_width, info is not None, rules),
         out_shape=tuple(jax.ShapeDtypeStruct(s, jnp.float32) for s in shapes),
         in_specs=in_specs,
         out_specs=tuple(pl.BlockSpec(memory_space=pltpu.VMEM) for _ in shapes),
         scratch_shapes=scratch,
         compiler_params=pltpu.CompilerParams(collective_id=collective_id, has_side_effects=True),
     )(*arrays)
+
+
+def column_rule(total, x_half, x_dual, cost, capacity, denom):
+    x_own = (x_half + x_dual + total) / denom
+    x_dual = x_dual + x_half - x_own
+    return jnp.minimum(jnp.maximum(x_own - x_dual - cost, 0.0), capacity)
+
+
+def row_rule(total, y_half, y_dual, lower, upper, denom):
+    y_anchor = y_half + y_dual
+    y_state = y_anchor + (total - y_anchor) / denom
+    y_dual = y_dual + y_half - y_state
+    return jnp.minimum(jnp.maximum(y_state - y_dual, lower), upper)
 
 
 def pick_blocks(full, index, blocks, block_width):
@@ -261,8 +286,20 @@
             row_denom = 1.0 + row_total[scenarios : scenarios + 1]
             col_total = col_total[:scenarios]
             row_total = row_total[:scenarios]
+        elif iteration == ITERS - 1:
+            return all_reduce(
+                [col_terms, row_terms],
+                AXES,
+                n_row,
+                1,
+                block_width,
+                finish=[
+                    (column_rule, [x_half, x_dual, unit_cost, capacity, col_denom]),
+                    (row_rule, [y_half, y_dual, row_lower, row_upper, row_denom]),
+                ],
+            )
         else:
-            col_total, row_total = all_reduce([col_terms, row_terms], AXES, n_row, 1, block_width)
+            col_total, row_total = all_reduce([col_terms, row_terms], AXES, n_row, 2, block_width)
         x_own = (x_half + x_dual + col_total) / col_denom
         x_dual = x_dual + x_half - x_own
         shift_full = (row_total - y_anchor) / row_denom

time: 119 us -> 119 us (level)
  the two profiles are of different devices: /device:TPU:2 before, /device:TPU:25 now
where the time goes in v8:
time: 119 us
  Pallas kernels  84.5 us (71%)
  other arithmetic  13.6 us (11%)
  matrix products  12.7 us (11%)
  local copies, waits for them, and re-layouts  6.45 us (5%)
  between operations  1.78 us (1%)
    pallas_call x2, Pallas kernels, all_reduce(): pl.pallas_call(functools.partial(reduce_kernel, n, group_axes, block_widt...  84.5 us
    dot_general x12, matrix products, by_tile(): lax.dot_general(stacked, matrices[t], (((1,), (contract,)), ((), ())), pr...  12.7 us
    unnamed x38, local copies, waits for them, and re-layouts  5.31 us

profile of v8, /device:TPU:25, one launch (start us, length us, event | category | flops | bytes accessed | tf_op | source)
XLA Modules:
  0.0 119.0 jit_solution(16128988737997636538)
XLA Ops:
  0.6 0.0 copy-start.6
  0.6 0.0 copy-start.2
  1.4 1.1 compare_bitcast_fusion
  2.5 1.3 %pad_add_fusion.refs_0_ = s32[9]{0:T(128)} fusion(s32[1]{0:T(128)} %bitcast.103, s32[4]{0:T(128)} %bitcast.107, s32[4]{0:T(128)} %bitcast.106), kind=kLoop, calls=%fused_computation.85 | loop fusion | flops 18 | bytes 72 | tf_op jit(solution)/shard_map/concatenate | solution.py:281
  3.8 0.7 fusion.80
  4.5 1.7 %fusion.74 = bf16[4,64,1024]{2,1,0:T(8,128)(2,1)S(1)} fusion(f32[1,1,4,64,1024]{4,3,2,1,0:T(8,128)} %param.31, f32[1,1,4,64,1024]{4,3,2,1,0:T(8,128)} %param.32), kind=kLoop, calls=%fused_computation.65 | loop fusion | flops 524288 | bytes 2621440 | tf_op jit(solution)/shard_map/convert_element_type | solution.py:263
  6.1 1.1 fusion.84
  7.2 0.0 copy-start.8
  7.2 2.5 %fusion.14 = f32[4,64,1024]{2,1,0:T(8,128)S(1)} fusion(bf16[4,64,1024]{2,1,0:T(8,128)(2,1)S(1)} %fusion.74, bf16[2,1024,1024]{2,1,0:T(8,128)(2,1)} %param.17), kind=kOutput, calls=%fused_computation.14 | convolution fusion | flops 536870912 | bytes 3670016 | tf_op jit(solution)/shard_map/dot_general | solution.py:205
  9.7 0.0 copy-done.6
  9.7 0.0 copy-done.2
  9.7 0.9 fusion.69
  10.7 0.0 copy-done.8
  10.7 0.7 fusion.2
  11.4 1.9 %select_reduce_fusion.7 = (f32[64,1024]{1,0:T(8,128)S(1)}, f32[64,1024]{1,0:T(8,128)S(1)}, f32[4,64,1024]{2,1,0:T(8,128)}, bf16[4,64,1024]{2,1,0:T(8,128)(2,1)S(1)}) fusion(pred[4]{0:T(512)(128)(4,1)S(1)} %get-tuple-element.34, pred[4]{0:T(512)(128)(4,1)S(1)} %get-tuple-element.32, f32[1,1,4,64,1024]{4,3,2,1,0:T(8,128)S(1)} %copy-done.2, ...), kind=kOutput, calls=%fused_computation.62 | convolution fusion | flops 538574848 | bytes 6817280 | tf_op jit(solution)/shard_map/dot_general | solution.py:205
  13.3 0.0 copy-start.10
  13.3 0.8 pad_maximum_fusion.refs_1_
  14.2 0.7 fusion.12
  14.9 0.0 copy-done.10
  14.9 0.0 copy-start
  14.9 0.0 copy-start.1
  14.9 0.0 copy-start.12
  14.9 0.0 copy-start.13
  14.9 0.9 select_reduce_fusion.5
  15.8 0.8 pad_maximum_fusion.1.refs_2_
  16.6 42.8 %shard_map.176 = (f32[72,2048]{1,0:T(8,128)}, f32[72,2048]{1,0:T(8,128)}) custom-call(s32[9]{0:T(128)} %pad_add_fusion.refs_0_, f32[64,2048]{1,0:T(8,128)} %pad_maximum_fusion.refs_1_, f32[64,2048]{1,0:T(8,128)} %pad_maximum_fusion.1.refs_2_), custom_call_target="tpu_custom_call" | custom-call | tf_op jit(solution)/shard_map/pallas_call | solution.py:171
  59.5 0.8 slice_add_fusion.1.refs_6_
  60.3 0.0 copy-start.16
  60.3 0.8 slice_add_fusion.refs_11_
  61.2 0.0 copy-start.17
  61.2 0.0 copy-done
  61.2 0.0 copy-done.1
  61.2 0.0 copy-done.12
  61.2 0.0 copy-done.13
  61.2 1.2 %fusion.81 = (f32[64,2048]{1,0:T(8,128)S(1)}, f32[64,2048]{1,0:T(8,128)S(1)}, f32[64,2048]{1,0:T(8,128)S(1)}) fusion(f32[2048]{0:T(1024)S(1)} %bitcast.105, f32[72,2048]{1,0:T(8,128)} %get-tuple-element.5, f32[64,2048]{1,0:T(8,128)S(1)} %copy-done.12, f32[64,2048]{1,0:T(8,128)S(1)} %copy-done, f32[64,2048]{1,0:T(8,128)S(1)} %copy-done.1, ...), kind=kLoop, calls=%fused_computation.91 | loop fusion | flops 917504 | bytes 4202496 | tf_op jit(solution)/shard_map/add | solution.py:306
  62.5 0.0 copy-start.3
  62.5 0.0 copy-start.4
  62.5 0.0 copy-start.5
  62.5 0.0 copy-start.14
  62.5 0.0 copy-start.15
  62.5 1.2 maximum_minimum_fusion
  63.8 0.0 copy-done.17
  63.8 0.2 subtract_convert_fusion
  64.0 0.0 copy-done.16
  64.0 0.0 copy-done.3
  64.0 0.0 copy-done.4
  64.0 0.2 copy-done.5
  64.2 0.2 copy-done.14
  64.4 0.2 copy-done.15
  64.6 1.2 %maximum_minimum_fusion.1 = (f32[64,2048]{1,0:T(8,128)}, f32[64,2048]{1,0:T(8,128)}, f32[64,2048]{1,0:T(8,128)S(1)}) fusion(f32[64,2048]{1,0:T(8,128)S(1)} %copy-done.3, f32[64,2048]{1,0:T(8,128)S(1)} %copy-done.4, f32[2048]{0:T(1024)S(1)} %bitcast.104, f32[72,2048]{1,0:T(8,128)S(1)} %copy-done.15, f32[64,2048]{1,0:T(8,128)S(1)} %copy-done.14, ...), kind=kLoop, calls=%fused_computation.71 | loop fusion | flops 1572864 | bytes 4202496 | tf_op jit(solution)/shard_map/jit(clip)/min | solution.py:260
  65.8 0.4 copy-done.7
  66.2 0.7 fusion.10
  67.0 0.0 copy-done.11
  67.0 0.9 fusion.66
  67.9 0.6 copy-done.9
  68.5 0.7 fusion
  69.2 1.0 select_reduce_fusion.3
  70.2 0.8 pad_maximum_fusion.2.refs_0_
  71.1 0.7 fusion.8
  71.8 1.0 select_reduce_fusion.1
  72.8 0.8 pad_maximum_fusion.3.refs_1_
  73.6 41.6 %shard_map.177 = (f32[64,2048]{1,0:T(8,128)}, f32[64,2048]{1,0:T(8,128)}) custom-call(f32[64,2048]{1,0:T(8,128)} %pad_maximum_fusion.2.refs_0_, f32[64,2048]{1,0:T(8,128)} %pad_maximum_fusion.3.refs_1_, f32[64,2048]{1,0:T(8,128)} %get-tuple-element.19.refs_2_, f32[64,2048]{1,0:T(8,128)} %get-tuple-element.20.refs_3_, f32[64,2048]{1,0:T(8,128)} %refs_4_.1, ...), custom_call_target="tpu_custom_call" | custom-call | tf_op jit(solution)/shard_map/pallas_call | solution.py:171
  115.2 1.9 %copy.22 = f32[64,2048]{1,0:T(8,128)} copy(f32[64,2048]{1,0:T(8,128)} %get-tuple-element.50) | data formatting | bytes 1048576
  117.1 1.9 %copy.23 = f32[64,2048]{1,0:T(8,128)} copy(f32[64,2048]{1,0:T(8,128)} %get-tuple-element.51) | data formatting | bytes 1048576
  (5 shorter events, 0.1 us)
Async XLA Ops:
  0.6 9.1 %copy-start.6 = (bf16[2,1024,1024]{2,1,0:T(8,128)(2,1)S(1)}, bf16[2,1024,1024]{2,1,0:T(8,128)(2,1)}, u32[]{:S(2)}) copy-start(bf16[2,1024,1024]{2,1,0:T(8,128)(2,1)} %param.17) | copy-start | bytes 12582916
  0.6 9.1 %copy-start.2 = (f32[1,1,4,64,1024]{4,3,2,1,0:T(8,128)S(1)}, f32[1,1,4,64,1024]{4,3,2,1,0:T(8,128)}, u32[]{:S(2)}) copy-start(f32[1,1,4,64,1024]{4,3,2,1,0:T(8,128)} %param.33) | copy-start | bytes 3145732
  7.2 3.5 %copy-start.8 = (bf16[2,1024,1024]{2,1,0:T(8,128)(2,1)S(1)}, bf16[2,1024,1024]{2,1,0:T(8,128)(2,1)}, u32[]{:S(2)}) copy-start(bf16[2,1024,1024]{2,1,0:T(8,128)(2,1)} %param.18) | copy-start | bytes 12582916
  13.3 1.6 %copy-start.10 = (f32[1,1,4,64,1024]{4,3,2,1,0:T(8,128)S(1)}, f32[1,1,4,64,1024]{4,3,2,1,0:T(8,128)}, u32[]{:S(2)}) copy-start(f32[1,1,4,64,1024]{4,3,2,1,0:T(8,128)} %param.32) | copy-start | bytes 3145732
  14.9 46.3 %copy-start = (f32[64,2048]{1,0:T(8,128)S(1)}, f32[64,2048]{1,0:T(8,128)}, u32[]{:S(2)}) copy-start(f32[64,2048]{1,0:T(8,128)} %refs_10_.1) | copy-start | bytes 1572868
  14.9 46.3 %copy-start.1 = (f32[64,2048]{1,0:T(8,128)S(1)}, f32[64,2048]{1,0:T(8,128)}, u32[]{:S(2)}) copy-start(f32[64,2048]{1,0:T(8,128)} %refs_9_.1) | copy-start | bytes 1572868
  14.9 46.3 %copy-start.12 = (f32[64,2048]{1,0:T(8,128)S(1)}, f32[64,2048]{1,0:T(8,128)}, u32[]{:S(2)}) copy-start(f32[64,2048]{1,0:T(8,128)} %param.28) | copy-start | bytes 1572868
  14.9 46.3 %copy-start.13 = (f32[64,2048]{1,0:T(8,128)S(1)}, f32[64,2048]{1,0:T(8,128)}, u32[]{:S(2)}) copy-start(f32[64,2048]{1,0:T(8,128)} %param.27) | copy-start | bytes 1572868
  60.3 3.7 %copy-start.16 = (f32[1,2048]{1,0:T(1,128)}, f32[1,2048]{1,0:T(1,128)S(1)}, u32[]{:S(2)}) copy-start(f32[1,2048]{1,0:T(1,128)S(1)} %slice_add_fusion.1.refs_6_) | copy-start | bytes 24580
  61.2 2.6 %copy-start.17 = (f32[1,2048]{1,0:T(1,128)}, f32[1,2048]{1,0:T(1,128)S(1)}, u32[]{:S(2)}) copy-start(f32[1,2048]{1,0:T(1,128)S(1)} %slice_add_fusion.refs_11_) | copy-start | bytes 24580
  62.5 1.6 %copy-start.3 = (f32[64,2048]{1,0:T(8,128)S(1)}, f32[64,2048]{1,0:T(8,128)}, u32[]{:S(2)}) copy-start(f32[64,2048]{1,0:T(8,128)} %refs_5_.1) | copy-start | bytes 1572868
  62.5 1.6 %copy-start.4 = (f32[64,2048]{1,0:T(8,128)S(1)}, f32[64,2048]{1,0:T(8,128)}, u32[]{:S(2)}) copy-start(f32[64,2048]{1,0:T(8,128)} %refs_4_.1) | copy-start | bytes 1572868
  62.5 1.7 %copy-start.5 = (f32[64,2048]{1,0:T(8,128)S(1)}, f32[64,2048]{1,0:T(8,128)}, u32[]{:S(2)}) copy-start(f32[64,2048]{1,0:T(8,128)} %param.23) | copy-start | bytes 1572868
  62.5 1.9 %copy-start.14 = (f32[64,2048]{1,0:T(8,128)S(1)}, f32[64,2048]{1,0:T(8,128)}, u32[]{:S(2)}) copy-start(f32[64,2048]{1,0:T(8,128)} %param.24) | copy-start | bytes 1572868
  62.5 2.0 %copy-start.15 = (f32[72,2048]{1,0:T(8,128)S(1)}, f32[72,2048]{1,0:T(8,128)}, u32[]{:S(2)}) copy-start(f32[72,2048]{1,0:T(8,128)} %get-tuple-element.4) | copy-start | bytes 1769476
  63.7 2.5 %copy-start.7 = (bf16[2,1024,1024]{2,1,0:T(8,128)(2,1)S(1)}, bf16[2,1024,1024]{2,1,0:T(8,128)(2,1)}, u32[]{:S(2)}) copy-start(bf16[2,1024,1024]{2,1,0:T(8,128)(2,1)} %param.17) | copy-start | bytes 12582916
  64.6 2.4 %copy-start.11 = (f32[4,64,1024]{2,1,0:T(8,128)S(1)}, f32[4,64,1024]{2,1,0:T(8,128)}, u32[]{:S(2)}) copy-start(f32[4,64,1024]{2,1,0:T(8,128)} %get-tuple-element.22) | copy-start | bytes 3145732
  66.2 2.3 %copy-start.9 = (bf16[2,1024,1024]{2,1,0:T(8,128)(2,1)S(1)}, bf16[2,1024,1024]{2,1,0:T(8,128)(2,1)}, u32[]{:S(2)}) copy-start(bf16[2,1024,1024]{2,1,0:T(8,128)(2,1)} %param.18) | copy-start | bytes 12582916

commit v9 on v7

--- a/solution.py
+++ b/solution.py
@@ -57,16 +57,18 @@
                     jnp.float32
                 )
             sources[g] = send
+    issue_order = sorted(range(groups), key=lambda g: group_axes[g] != "col")
     barrier = pltpu.get_barrier_semaphore()
-    for axis in group_axes:
+    for axis in [group_axes[g] for g in issue_order]:
         me = lax.axis_index(axis)
         for k in range(1, n):
             peer = lax.rem(me + k, n)
             pl.semaphore_signal(barrier, inc=1, device_id=peer_id(axis, peer), device_id_type=MESH)
     pl.semaphore_wait(barrier, groups * (n - 1))
 
-    scatter = []
-    for g, axis in enumerate(group_axes):
+    scatter = [None] * groups
+    for g in issue_order:
+        axis = group_axes[g]
         recv, gathered, s1, r1, s2, r2 = per[g]
         me = lax.axis_index(axis)
         copies = []
@@ -82,7 +84,7 @@
             )
             copy.start()
             copies.append(copy)
-        scatter.append(copies)
+        scatter[g] = copies
 
     gathers = []
     for g, axis in enumerate(group_axes):

time: 119 us -> 117 us (0.983)
  the two profiles are of different devices: /device:TPU:2 before, /device:TPU:1 now
where the time goes in v9:
time: 117 us; the launch traced here: 115 us
  Pallas kernels  79.3 us (68%)
  other arithmetic  16.7 us (14%)
  matrix products  13.8 us (12%)
  local copies, waits for them, and re-layouts  3.38 us (3%)
  between operations  1.78 us (2%)
    pallas_call x2, Pallas kernels, all_reduce(): pl.pallas_call(functools.partial(reduce_kernel, n, group_axes, block_widt...  79.3 us
    dot_general x12, matrix products, by_tile(): lax.dot_general(stacked, matrices[t], (((1,), (contract,)), ((), ())), pr...  13.8 us
    min x1, other arithmetic, per_device(): column_final = jnp.clip(x_own - x_dual - unit_cost, 0.0, capacity)  2.73 us
    min x1, other arithmetic, per_device(): row_final = jnp.clip(y_state - y_dual, row_lower, row_upper)  2.41 us

profile of v9, /device:TPU:1, one launch (start us, length us, event | category | flops | bytes accessed | tf_op | source)
XLA Modules:
  0.0 115.0 jit_solution(5388986120047161502)
XLA Ops:
  0.6 0.0 copy-start.10
  0.6 0.0 copy-start.1
  1.4 1.1 compare_bitcast_fusion
  2.5 1.3 %pad_add_fusion.refs_0_ = s32[9]{0:T(128)} fusion(s32[1]{0:T(128)} %bitcast.102, s32[4]{0:T(128)} %bitcast.109, s32[4]{0:T(128)} %bitcast.108), kind=kLoop, calls=%fused_computation.90 | loop fusion | flops 18 | bytes 72 | tf_op jit(solution)/shard_map/concatenate | solution.py:258
  3.8 0.7 fusion.85
  4.5 1.7 %fusion.79 = bf16[4,64,1024]{2,1,0:T(8,128)(2,1)S(1)} fusion(f32[1,1,4,64,1024]{4,3,2,1,0:T(8,128)} %param.31, f32[1,1,4,64,1024]{4,3,2,1,0:T(8,128)} %param.32), kind=kLoop, calls=%fused_computation.72 | loop fusion | flops 524288 | bytes 2621440 | tf_op jit(solution)/shard_map/convert_element_type | solution.py:240
  6.2 1.1 fusion.88
  7.3 0.0 copy-start.13
  7.3 2.5 %fusion.14 = f32[4,64,1024]{2,1,0:T(8,128)S(1)} fusion(bf16[4,64,1024]{2,1,0:T(8,128)(2,1)S(1)} %fusion.79, bf16[2,1024,1024]{2,1,0:T(8,128)(2,1)} %param.17), kind=kOutput, calls=%fused_computation.14 | convolution fusion | flops 536870912 | bytes 3670016 | tf_op jit(solution)/shard_map/dot_general | solution.py:182
  9.8 0.0 copy-done.10
  9.8 0.0 copy-done.1
  9.8 0.9 fusion.69
  10.8 0.0 copy-done.13
  10.8 0.7 fusion.2
  11.5 1.9 %select_reduce_fusion.7 = (f32[64,1024]{1,0:T(8,128)S(1)}, f32[64,1024]{1,0:T(8,128)S(1)}, f32[4,64,1024]{2,1,0:T(8,128)}, bf16[4,64,1024]{2,1,0:T(8,128)(2,1)S(1)}) fusion(pred[4]{0:T(512)(128)(4,1)S(1)} %get-tuple-element.30, pred[4]{0:T(512)(128)(4,1)S(1)} %get-tuple-element.28, f32[1,1,4,64,1024]{4,3,2,1,0:T(8,128)S(1)} %copy-done.1, ...), kind=kOutput, calls=%fused_computation.62 | convolution fusion | flops 538574848 | bytes 6817280 | tf_op jit(solution)/shard_map/dot_general | solution.py:182
  13.4 0.0 copy-start.15
  13.4 0.8 pad_maximum_fusion.refs_1_
  14.2 0.7 fusion.12
  15.0 0.0 copy-done.15
  15.0 0.0 copy-start.2
  15.0 0.0 copy-start.3
  15.0 0.0 copy-start.4
  15.0 0.0 copy-start.5
  15.0 1.9 %select_reduce_fusion.5 = (f32[64,1024]{1,0:T(8,128)S(1)}, f32[64,1024]{1,0:T(8,128)S(1)}, f32[4,64,1024]{2,1,0:T(8,128)}) fusion(pred[4]{0:T(512)(128)(4,1)S(1)} %get-tuple-element.34, pred[4]{0:T(512)(128)(4,1)S(1)} %get-tuple-element.35, f32[1,1,4,64,1024]{4,3,2,1,0:T(8,128)S(1)} %copy-done.15, f32[4,64,1024]{2,1,0:T(8,128)S(1)} %fusion.12, ...), kind=kOutput, calls=%fused_computation.60 | convolution fusion | flops 538312704 | bytes 6292992 | tf_op jit(solution)/shard_map/dot_general | solution.py:182
  17.0 0.0 copy-start
  17.0 0.0 copy-start.6
  17.0 0.8 pad_maximum_fusion.1.refs_2_
  17.8 42.3 %shard_map.176 = (f32[72,2048]{1,0:T(8,128)}, f32[72,2048]{1,0:T(8,128)}) custom-call(s32[9]{0:T(128)} %pad_add_fusion.refs_0_, f32[64,2048]{1,0:T(8,128)} %pad_maximum_fusion.refs_1_, f32[64,2048]{1,0:T(8,128)} %pad_maximum_fusion.1.refs_2_), custom_call_target="tpu_custom_call" | custom-call | tf_op jit(solution)/shard_map/pallas_call | solution.py:161
  60.1 0.0 copy-start.12
  60.1 0.0 copy-start.7
  60.2 0.0 copy-start.8
  60.2 0.0 copy-start.9
  60.2 1.0 slice_add_fusion.1
  61.2 0.8 slice_add_fusion
  62.0 0.0 copy-done.2
  62.0 0.0 copy-done.3
  62.0 0.0 copy-done.4
  62.1 0.0 copy-done.5
  62.1 1.2 %subtract_divide_fusion = f32[64,2048]{1,0:T(8,128)S(1)} fusion(f32[72,2048]{1,0:T(8,128)} %get-tuple-element.7, f32[2048]{0:T(1024)S(1)} %bitcast.106, f32[64,2048]{1,0:T(8,128)S(1)} %copy-done.2, f32[64,2048]{1,0:T(8,128)S(1)} %copy-done.3, f32[64,2048]{1,0:T(8,128)S(1)} %copy-done.4, f32[64,2048]{1,0:T(8,128)S(1)} %copy-done.5), kind=kLoop, calls=%fused_computation.77 | loop fusion | flops 786432 | bytes 3153920 | tf_op jit(solution)/shard_map/div | solution.py:270
  63.3 0.0 copy-start.11
  63.3 0.0 copy-done.12
  63.3 0.2 subtract_convert_fusion
  63.6 0.0 copy-done
  63.6 0.0 copy-done.6
  63.6 0.0 copy-done.7
  63.6 0.0 copy-done.8
  63.6 0.0 copy-done.9
  63.6 0.0 copy-start.16
  63.6 0.2 add_divide_fusion
  63.9 1.6 %copy-done.11 = bf16[2,1024,1024]{2,1,0:T(8,128)(2,1)S(1)} copy-done((bf16[2,1024,1024]{2,1,0:T(8,128)(2,1)S(1)}, bf16[2,1024,1024]{2,1,0:T(8,128)(2,1)}, u32[]{:S(2)}) %copy-start.11) | copy-done | bytes 4194328
  65.5 0.0 copy-start.14
  65.5 0.7 fusion.10
  66.2 0.0 copy-done.16
  66.2 0.9 fusion.66
  67.1 0.6 copy-done.14
  67.7 0.7 fusion
  68.5 1.0 select_reduce_fusion.3
  69.5 0.8 pad_maximum_fusion.2.refs_0_
  70.3 0.7 fusion.8
  71.0 1.0 select_reduce_fusion.1
  72.0 0.8 pad_maximum_fusion.3.refs_1_
  72.8 37.0 %shard_map.177 = (f32[64,2048]{1,0:T(8,128)}, f32[64,2048]{1,0:T(8,128)}) custom-call(f32[64,2048]{1,0:T(8,128)} %pad_maximum_fusion.2.refs_0_, f32[64,2048]{1,0:T(8,128)} %pad_maximum_fusion.3.refs_1_), custom_call_target="tpu_custom_call" | custom-call | tf_op jit(solution)/shard_map/pallas_call | solution.py:161
  109.8 2.4 %fusion.78 = f32[64,2048]{1,0:T(8,128)} fusion(f32[64,2048]{1,0:T(8,128)S(1)} %copy-done.3, f32[64,2048]{1,0:T(8,128)S(1)} %copy-done.4, f32[64,2048]{1,0:T(8,128)} %get-tuple-element.9, f32[2048]{0:T(1024)S(1)} %bitcast.107, f32[64,2048]{1,0:T(8,128)S(1)} %copy-done.2, f32[64,2048]{1,0:T(8,128)S(1)} %copy-done.5, f32[72,2048]{1,0:T(8,128)} %get-tuple-element.7), kind=kLoop, calls=%fused_computation.71 | loop fusion | flops 2490368 | bytes 3678208 | tf_op jit(solution)/shard_map/jit(clip)/min | solution.py:278
  112.2 2.7 %fusion.76 = f32[64,2048]{1,0:T(8,128)} fusion(f32[64,2048]{1,0:T(8,128)S(1)} %copy-done.6, f32[64,2048]{1,0:T(8,128)} %param.25, f32[64,2048]{1,0:T(8,128)} %get-tuple-element.8, f32[2048]{0:T(1024)S(1)} %bitcast.105, f32[64,2048]{1,0:T(8,128)} %param.24, f32[64,2048]{1,0:T(8,128)S(1)} %copy-done, f32[72,2048]{1,0:T(8,128)} %get-tuple-element.6), kind=kLoop, calls=%fused_computation.69 | loop fusion | flops 2621440 | bytes 3678208 | tf_op jit(solution)/shard_map/jit(clip)/min | solution.py:277
  (2 shorter events, 0.1 us)
Async XLA Ops:
  0.6 9.2 %copy-start.10 = (bf16[2,1024,1024]{2,1,0:T(8,128)(2,1)S(1)}, bf16[2,1024,1024]{2,1,0:T(8,128)(2,1)}, u32[]{:S(2)}) copy-start(bf16[2,1024,1024]{2,1,0:T(8,128)(2,1)} %param.17) | copy-start | bytes 12582916
  0.6 9.2 %copy-start.1 = (f32[1,1,4,64,1024]{4,3,2,1,0:T(8,128)S(1)}, f32[1,1,4,64,1024]{4,3,2,1,0:T(8,128)}, u32[]{:S(2)}) copy-start(f32[1,1,4,64,1024]{4,3,2,1,0:T(8,128)} %param.33) | copy-start | bytes 3145732
  7.3 3.5 %copy-start.13 = (bf16[2,1024,1024]{2,1,0:T(8,128)(2,1)S(1)}, bf16[2,1024,1024]{2,1,0:T(8,128)(2,1)}, u32[]{:S(2)}) copy-start(bf16[2,1024,1024]{2,1,0:T(8,128)(2,1)} %param.18) | copy-start | bytes 12582916
  13.4 1.6 %copy-start.15 = (f32[1,1,4,64,1024]{4,3,2,1,0:T(8,128)S(1)}, f32[1,1,4,64,1024]{4,3,2,1,0:T(8,128)}, u32[]{:S(2)}) copy-start(f32[1,1,4,64,1024]{4,3,2,1,0:T(8,128)} %param.32) | copy-start | bytes 3145732
  15.0 47.1 %copy-start.2 = (f32[64,2048]{1,0:T(8,128)S(1)}, f32[64,2048]{1,0:T(8,128)}, u32[]{:S(2)}) copy-start(f32[64,2048]{1,0:T(8,128)} %param.28) | copy-start | bytes 1572868
  15.0 47.1 %copy-start.3 = (f32[64,2048]{1,0:T(8,128)S(1)}, f32[64,2048]{1,0:T(8,128)}, u32[]{:S(2)}) copy-start(f32[64,2048]{1,0:T(8,128)} %param.30) | copy-start | bytes 1572868
  15.0 47.1 %copy-start.4 = (f32[64,2048]{1,0:T(8,128)S(1)}, f32[64,2048]{1,0:T(8,128)}, u32[]{:S(2)}) copy-start(f32[64,2048]{1,0:T(8,128)} %param.29) | copy-start | bytes 1572868
  15.0 47.1 %copy-start.5 = (f32[64,2048]{1,0:T(8,128)S(1)}, f32[64,2048]{1,0:T(8,128)}, u32[]{:S(2)}) copy-start(f32[64,2048]{1,0:T(8,128)} %param.27) | copy-start | bytes 1572868
  17.0 46.6 %copy-start = (f32[64,2048]{1,0:T(8,128)S(1)}, f32[64,2048]{1,0:T(8,128)}, u32[]{:S(2)}) copy-start(f32[64,2048]{1,0:T(8,128)} %param.23) | copy-start | bytes 1572868
  17.0 46.6 %copy-start.6 = (f32[64,2048]{1,0:T(8,128)S(1)}, f32[64,2048]{1,0:T(8,128)}, u32[]{:S(2)}) copy-start(f32[64,2048]{1,0:T(8,128)} %param.26) | copy-start | bytes 1572868
  60.1 3.2 %copy-start.12 = (f32[4,64,1024]{2,1,0:T(8,128)S(1)}, f32[4,64,1024]{2,1,0:T(8,128)}, u32[]{:S(2)}) copy-start(f32[4,64,1024]{2,1,0:T(8,128)} %get-tuple-element.32) | copy-start | bytes 3145732
  60.1 3.5 %copy-start.7 = (f32[64,2048]{1,0:T(8,128)S(1)}, f32[64,2048]{1,0:T(8,128)}, u32[]{:S(2)}) copy-start(f32[64,2048]{1,0:T(8,128)} %param.25) | copy-start | bytes 1572868
  60.2 3.5 %copy-start.8 = (f32[64,2048]{1,0:T(8,128)S(1)}, f32[64,2048]{1,0:T(8,128)}, u32[]{:S(2)}) copy-start(f32[64,2048]{1,0:T(8,128)} %param.24) | copy-start | bytes 1572868
  60.2 3.5 %copy-start.9 = (f32[72,2048]{1,0:T(8,128)S(1)}, f32[72,2048]{1,0:T(8,128)}, u32[]{:S(2)}) copy-start(f32[72,2048]{1,0:T(8,128)} %get-tuple-element.6) | copy-start | bytes 1769476
  63.3 2.2 %copy-start.11 = (bf16[2,1024,1024]{2,1,0:T(8,128)(2,1)S(1)}, bf16[2,1024,1024]{2,1,0:T(8,128)(2,1)}, u32[]{:S(2)}) copy-start(bf16[2,1024,1024]{2,1,0:T(8,128)(2,1)} %param.17) | copy-start | bytes 12582916
  63.6 2.6 %copy-start.16 = (f32[4,64,1024]{2,1,0:T(8,128)S(1)}, f32[4,64,1024]{2,1,0:T(8,128)}, u32[]{:S(2)}) copy-start(f32[4,64,1024]{2,1,0:T(8,128)} %get-tuple-element.18) | copy-start | bytes 3145732
  65.5 2.3 %copy-start.14 = (bf16[2,1024,1024]{2,1,0:T(8,128)(2,1)S(1)}, bf16[2,1024,1024]{2,1,0:T(8,128)(2,1)}, u32[]{:S(2)}) copy-start(bf16[2,1024,1024]{2,1,0:T(8,128)(2,1)} %param.18) | copy-start | bytes 12582916

commit v10 on v9

--- a/solution.py
+++ b/solution.py
@@ -18,32 +18,53 @@
     return (lax.axis_index("row"), peer)
 
 
-def reduce_kernel(n, group_axes, block_width, with_counts, *refs):
+def reduce_kernel(n, group_axes, block_width, with_counts, blocks, *refs):
     groups = len(group_axes)
     if with_counts:
         info, refs = refs[0], refs[1:]
-    ins = refs[:groups]
-    outs = refs[groups : 2 * groups]
-    scratch = refs[2 * groups :]
+    ins = [refs[g * blocks : (g + 1) * blocks] for g in range(groups)]
+    refs = refs[groups * blocks :]
+    outs = refs[:groups]
+    scratch = refs[groups:]
     size = 7 if with_counts else 6
     per = [scratch[size * g : size * g + 6] for g in range(groups)]
-    width = ins[0].shape[1] // n
-    sources = list(ins)
+    width = blocks * block_width // n
+    per_block = block_width // width
+    chunked = [False] * groups
 
     def cols(index):
         return pl.ds(pl.multiple_of(index * width, width), width)
 
-    def piece(ref, index):
-        if len(ref.shape) == 3:
-            return ref.at[index]
-        return ref.at[:, cols(index)]
+    def piece(g, index, b=0):
+        if chunked[g]:
+            return scratch[size * g + 6].at[index]
+        offset = pl.multiple_of(lax.rem(index, per_block) * width, width)
+        return ins[g][b].at[:, pl.ds(offset, width)]
+
+    def start_from(g, index, make):
+        if chunked[g]:
+            make(piece(g, index)).start()
+            return
+        for b in range(blocks):
+
+            @pl.when(index // per_block == b)
+            def _():
+                make(piece(g, index, b)).start()
+
+    def load(g, index):
+        if chunked[g]:
+            return piece(g, index)[...]
+        value = piece(g, index, 0)[...]
+        for b in range(1, blocks):
+            value = jnp.where(index // per_block == b, piece(g, index, b)[...], value)
+        return value
 
     if with_counts:
         slots = (info.shape[0] - 1) // groups
         live = info[groups * slots]
         for g in range(groups):
             send = scratch[size * g + 6]
-            data_rows = ins[g].shape[0]
+            data_rows = ins[g][0].shape[0]
             extra = send.shape[1] - data_rows
             for p in range(n):
                 block = (p * width) // block_width
@@ -52,11 +73,12 @@
                     count = count + jnp.where(
                         (k < live) & (info[g * slots + k] == block), 1, 0
                     ).astype(jnp.int32)
-                send[p, :data_rows, :] = ins[g][:, p * width : (p + 1) * width]
+                part, offset = divmod(p, per_block)
+                send[p, :data_rows, :] = ins[g][part][:, offset * width : (offset + 1) * width]
                 send[p, data_rows:, :] = jnp.full((extra, width), count, jnp.int32).astype(
                     jnp.float32
                 )
-            sources[g] = send
+            chunked[g] = True
     issue_order = sorted(range(groups), key=lambda g: group_axes[g] != "col")
     barrier = pltpu.get_barrier_semaphore()
     for axis in [group_axes[g] for g in issue_order]:
@@ -74,16 +96,18 @@
         copies = []
         for k in range(1, n):
             peer = lax.rem(me + k, n)
-            copy = pltpu.make_async_remote_copy(
-                src_ref=piece(sources[g], peer),
-                dst_ref=recv.at[me],
-                send_sem=s1.at[peer],
-                recv_sem=r1.at[me],
-                device_id=peer_id(axis, peer),
-                device_id_type=MESH,
-            )
-            copy.start()
-            copies.append(copy)
+            def make(src, peer=peer, recv=recv, s1=s1, r1=r1, me=me, axis=axis):
+                return pltpu.make_async_remote_copy(
+                    src_ref=src,
+                    dst_ref=recv.at[me],
+                    send_sem=s1.at[peer],
+                    recv_sem=r1.at[me],
+                    device_id=peer_id(axis, peer),
+                    device_id_type=MESH,
+                )
+
+            start_from(g, peer, make)
+            copies.append(make(piece(g, peer)))
         scatter[g] = copies
 
     gathers = []
@@ -93,14 +117,14 @@
         for k in range(1, n):
             source = lax.rem(me + n - k, n)
             pltpu.make_async_remote_copy(
-                src_ref=piece(sources[g], source),
+                src_ref=piece(g, source),
                 dst_ref=recv.at[source],
                 send_sem=s1.at[source],
                 recv_sem=r1.at[source],
                 device_id=peer_id(axis, source),
                 device_id_type=MESH,
             ).wait_recv()
-        total = piece(sources[g], me)[...]
+        total = load(g, me)
         for k in range(1, n):
             total = total + recv[lax.rem(me + k, n)]
         outs[g][:, cols(me)] = total
@@ -140,7 +164,8 @@
 
 def all_reduce(arrays, group_axes, n, collective_id, block_width, info=None):
     extra = 0 if info is None else 8
-    shapes = [(a.shape[0] + extra, a.shape[1]) for a in arrays]
+    blocks = len(arrays[0])
+    shapes = [(a[0].shape[0] + extra, blocks * a[0].shape[1]) for a in arrays]
     width = shapes[0][1] // n
     scratch = []
     for rows, _ in shapes:
@@ -154,12 +179,13 @@
         ]
         if info is not None:
             scratch.append(pltpu.VMEM((n, rows, width), jnp.float32))
+    arrays = [block for group in arrays for block in group]
     in_specs = [pl.BlockSpec(memory_space=pltpu.VMEM)] * len(arrays)
     if info is not None:
         in_specs = [pl.BlockSpec(memory_space=pltpu.SMEM)] + in_specs
         arrays = [info] + arrays
     return pl.pallas_call(
-        functools.partial(reduce_kernel, n, group_axes, block_width, info is not None),
+        functools.partial(reduce_kernel, n, group_axes, block_width, info is not None, blocks),
         out_shape=tuple(jax.ShapeDtypeStruct(s, jnp.float32) for s in shapes),
         in_specs=in_specs,
         out_specs=tuple(pl.BlockSpec(memory_space=pltpu.VMEM) for _ in shapes),
@@ -248,12 +274,8 @@
         )
         x_terms = x_proj + input_duals
         y_terms = y_proj + image_duals
-        col_terms = jnp.concatenate(
-            [jnp.sum(jnp.where(m, x_terms, 0.0), axis=0) for m in col_mask], axis=1
-        )
-        row_terms = jnp.concatenate(
-            [jnp.sum(jnp.where(m, y_terms, 0.0), axis=0) for m in row_mask], axis=1
-        )
+        col_terms = [jnp.sum(jnp.where(m, x_terms, 0.0), axis=0) for m in col_mask]
+        row_terms = [jnp.sum(jnp.where(m, y_terms, 0.0), axis=0) for m in row_mask]
         if iteration == 0:
             slot_info = jnp.concatenate([cols_here, rows_here, block_count[0, 0][None]])
             col_total, row_total = all_reduce(

time: 117 us -> 120 us (1.026)
  the two profiles are of different devices: /device:TPU:1 before, /device:TPU:16 now
where the time goes in v10:
time: 120 us; the launch traced here: 119 us
  Pallas kernels  83.7 us (70%)
  matrix products  16.9 us (14%)
  other arithmetic  13.3 us (11%)
  local copies, waits for them, and re-layouts  3.39 us (3%)
  between operations  1.78 us (1%)
    pallas_call x2, Pallas kernels, all_reduce(): pl.pallas_call(functools.partial(reduce_kernel, n, group_axes, block_widt...  83.7 us
    dot_general x12, matrix products, by_tile(): lax.dot_general(stacked, matrices[t], (((1,), (contract,)), ((), ())), pr...  16.9 us
    min x1, other arithmetic, per_device(): column_final = jnp.clip(x_own - x_dual - unit_cost, 0.0, capacity)  2.73 us
    min x1, other arithmetic, per_device(): row_final = jnp.clip(y_state - y_dual, row_lower, row_upper)  2.41 us

profile of v10, /device:TPU:16, one launch (start us, length us, event | category | flops | bytes accessed | tf_op | source)
XLA Modules:
  0.0 119.2 jit_solution(17047319833815682714)
XLA Ops:
  0.6 0.0 copy-start.10
  0.6 0.0 copy-start.1
  1.4 1.1 compare_bitcast_fusion
  2.5 1.3 %pad_add_fusion.refs_0_ = s32[9]{0:T(128)} fusion(s32[1]{0:T(128)} %bitcast.102, s32[4]{0:T(128)} %bitcast.109, s32[4]{0:T(128)} %bitcast.108), kind=kLoop, calls=%fused_computation.86 | loop fusion | flops 18 | bytes 72 | tf_op jit(solution)/shard_map/concatenate | solution.py:280
  3.8 0.7 compare_and_fusion.1
  4.5 1.7 %fusion.79 = bf16[4,64,1024]{2,1,0:T(8,128)(2,1)S(1)} fusion(f32[1,1,4,64,1024]{4,3,2,1,0:T(8,128)} %param.31, f32[1,1,4,64,1024]{4,3,2,1,0:T(8,128)} %param.32), kind=kLoop, calls=%fused_computation.72 | loop fusion | flops 524288 | bytes 2621440 | tf_op jit(solution)/shard_map/convert_element_type | solution.py:266
  6.2 1.1 fusion.88
  7.2 0.0 copy-start.13
  7.3 2.5 %fusion.14 = f32[4,64,1024]{2,1,0:T(8,128)S(1)} fusion(bf16[4,64,1024]{2,1,0:T(8,128)(2,1)S(1)} %fusion.79, bf16[2,1024,1024]{2,1,0:T(8,128)(2,1)} %param.17), kind=kOutput, calls=%fused_computation.14 | convolution fusion | flops 536870912 | bytes 3670016 | tf_op jit(solution)/shard_map/dot_general | solution.py:208
  9.8 0.0 copy-done.10
  9.8 0.0 copy-done.1
  9.8 0.9 fusion.69
  10.7 0.0 copy-done.13
  10.7 0.7 fusion.2
  11.4 0.0 copy-start.15
  11.5 2.7 %select_reduce_fusion.6 = (f32[64,1024]{1,0:T(8,128)}, f32[64,1024]{1,0:T(8,128)}, f32[4,64,1024]{2,1,0:T(8,128)}, bf16[4,64,1024]{2,1,0:T(8,128)(2,1)S(1)}) fusion(pred[4]{0:T(512)(128)(4,1)S(1)} %get-tuple-element.30, pred[4]{0:T(512)(128)(4,1)S(1)} %get-tuple-element.28, f32[1,1,4,64,1024]{4,3,2,1,0:T(8,128)S(1)} %copy-done.1, ...), kind=kOutput, calls=%fused_computation.61 | convolution fusion | flops 538574848 | bytes 6817280 | tf_op jit(solution)/shard_map/dot_general | solution.py:208
  14.1 0.7 fusion.12
  14.8 0.0 copy-done.15
  14.9 0.0 copy-start.2
  14.9 0.0 copy-start.3
  14.9 0.0 copy-start.4
  14.9 0.0 copy-start.5
  14.9 2.7 %select_reduce_fusion.4 = (f32[64,1024]{1,0:T(8,128)}, f32[64,1024]{1,0:T(8,128)}, f32[4,64,1024]{2,1,0:T(8,128)}) fusion(pred[4]{0:T(512)(128)(4,1)S(1)} %get-tuple-element.35, pred[4]{0:T(512)(128)(4,1)S(1)} %get-tuple-element.34, f32[1,1,4,64,1024]{4,3,2,1,0:T(8,128)S(1)} %copy-done.15, f32[4,64,1024]{2,1,0:T(8,128)S(1)} %fusion.12, ...), kind=kOutput, calls=%fused_computation.59 | convolution fusion | flops 538312704 | bytes 6292992 | tf_op jit(solution)/shard_map/dot_general | solution.py:208
  17.6 0.0 copy-start
  17.6 0.0 copy-start.6
  17.7 42.0 %shard_map.176 = (f32[72,2048]{1,0:T(8,128)}, f32[72,2048]{1,0:T(8,128)}) custom-call(s32[9]{0:T(128)} %pad_add_fusion.refs_0_, f32[64,1024]{1,0:T(8,128)} %get-tuple-element.17.refs_1_, f32[64,1024]{1,0:T(8,128)} %get-tuple-element.16.refs_2_, f32[64,1024]{1,0:T(8,128)} %get-tuple-element.15.refs_3_, f32[64,1024]{1,0:T(8,128)} %get-tuple-element.14.refs_4_), custom_call_target="tpu_custom_call" | custom-call | tf_op jit(solution)/shard_map/pallas_call | solution.py:187
  59.6 0.0 copy-start.12
  59.6 0.0 copy-start.7
  59.6 0.0 copy-start.8
  59.6 0.0 copy-start.9
  59.7 1.0 slice_add_fusion.1
  60.7 0.8 slice_add_fusion
  61.5 0.0 copy-done.2
  61.5 0.0 copy-done.3
  61.5 0.0 copy-done.4
  61.5 0.0 copy-done.5
  61.5 1.2 %subtract_divide_fusion = f32[64,2048]{1,0:T(8,128)S(1)} fusion(f32[72,2048]{1,0:T(8,128)} %get-tuple-element.7, f32[2048]{0:T(1024)S(1)} %bitcast.106, f32[64,2048]{1,0:T(8,128)S(1)} %copy-done.2, f32[64,2048]{1,0:T(8,128)S(1)} %copy-done.3, f32[64,2048]{1,0:T(8,128)S(1)} %copy-done.4, f32[64,2048]{1,0:T(8,128)S(1)} %copy-done.5), kind=kLoop, calls=%fused_computation.73 | loop fusion | flops 786432 | bytes 3153920 | tf_op jit(solution)/shard_map/div | solution.py:292
  62.8 0.0 copy-start.11
  62.8 0.0 copy-done.12
  62.8 0.2 subtract_convert_fusion
  63.1 0.0 copy-done
  63.1 0.0 copy-done.6
  63.1 0.0 copy-done.7
  63.1 0.0 copy-done.8
  63.1 0.0 copy-done.9
  63.1 0.0 copy-start.16
  63.1 0.2 add_divide_fusion
  63.4 1.6 %copy-done.11 = bf16[2,1024,1024]{2,1,0:T(8,128)(2,1)S(1)} copy-done((bf16[2,1024,1024]{2,1,0:T(8,128)(2,1)S(1)}, bf16[2,1024,1024]{2,1,0:T(8,128)(2,1)}, u32[]{:S(2)}) %copy-start.11) | copy-done | bytes 4194328
  64.9 0.0 copy-start.14
  64.9 0.7 fusion.10
  65.7 0.0 copy-done.16
  65.7 0.9 fusion.66
  66.6 0.6 copy-done.14
  67.2 0.7 fusion
  67.9 1.8 %select_reduce_fusion.2 = (f32[64,1024]{1,0:T(8,128)}, f32[64,1024]{1,0:T(8,128)}, bf16[4,64,1024]{2,1,0:T(8,128)(2,1)S(1)}) fusion(pred[4]{0:T(512)(128)(4,1)S(1)} %get-tuple-element.30, f32[4,64,1024]{2,1,0:T(8,128)S(1)} %copy-done.16, f32[64,1024]{1,0:T(8,128)S(1)} %get-tuple-element.20, f32[64,1024]{1,0:T(8,128)S(1)} %get-tuple-element.19, ...), kind=kOutput, calls=%fused_computation.54 | convolution fusion | flops 539099136 | bytes 6293504 | tf_op jit(solution)/shard_map/dot_general | solution.py:208
  69.8 0.7 fusion.8
  70.5 1.8 %select_reduce_fusion = (f32[64,1024]{1,0:T(8,128)}, f32[64,1024]{1,0:T(8,128)}) fusion(pred[4]{0:T(512)(128)(4,1)S(1)} %get-tuple-element.35, pred[4]{0:T(512)(128)(4,1)S(1)} %get-tuple-element.34, f32[4,64,1024]{2,1,0:T(8,128)S(1)} %copy-done.12, f32[64,1024]{1,0:T(8,128)S(1)} %get-tuple-element.22, f32[64,1024]{1,0:T(8,128)S(1)} %get-tuple-element.21, ...), kind=kOutput, calls=%fused_computation.52 | convolution fusion | flops 539099136 | bytes 5769216 | tf_op jit(solution)/shard_map/dot_general | solution.py:208
  72.3 41.8 %shard_map.177 = (f32[64,2048]{1,0:T(8,128)}, f32[64,2048]{1,0:T(8,128)}) custom-call(f32[64,1024]{1,0:T(8,128)} %get-tuple-element.11.refs_0_, f32[64,1024]{1,0:T(8,128)} %get-tuple-element.10.refs_1_, f32[64,1024]{1,0:T(8,128)} %get-tuple-element.13.refs_2_, f32[64,1024]{1,0:T(8,128)} %get-tuple-element.12.refs_3_), custom_call_target="tpu_custom_call" | custom-call | tf_op jit(solution)/shard_map/pallas_call | solution.py:187
  114.0 2.4 %fusion.78 = f32[64,2048]{1,0:T(8,128)} fusion(f32[64,2048]{1,0:T(8,128)S(1)} %copy-done.3, f32[64,2048]{1,0:T(8,128)S(1)} %copy-done.4, f32[64,2048]{1,0:T(8,128)} %get-tuple-element.9, f32[2048]{0:T(1024)S(1)} %bitcast.107, f32[64,2048]{1,0:T(8,128)S(1)} %copy-done.2, f32[64,2048]{1,0:T(8,128)S(1)} %copy-done.5, f32[72,2048]{1,0:T(8,128)} %get-tuple-element.7), kind=kLoop, calls=%fused_computation.71 | loop fusion | flops 2490368 | bytes 3678208 | tf_op jit(solution)/shard_map/jit(clip)/min | solution.py:300
  116.5 2.7 %fusion.76 = f32[64,2048]{1,0:T(8,128)} fusion(f32[64,2048]{1,0:T(8,128)S(1)} %copy-done.6, f32[64,2048]{1,0:T(8,128)} %param.25, f32[64,2048]{1,0:T(8,128)} %get-tuple-element.8, f32[2048]{0:T(1024)S(1)} %bitcast.105, f32[64,2048]{1,0:T(8,128)} %param.24, f32[64,2048]{1,0:T(8,128)S(1)} %copy-done, f32[72,2048]{1,0:T(8,128)} %get-tuple-element.6), kind=kLoop, calls=%fused_computation.69 | loop fusion | flops 2621440 | bytes 3678208 | tf_op jit(solution)/shard_map/jit(clip)/min | solution.py:299
  (2 shorter events, 0.1 us)
Async XLA Ops:
  0.6 9.1 %copy-start.10 = (bf16[2,1024,1024]{2,1,0:T(8,128)(2,1)S(1)}, bf16[2,1024,1024]{2,1,0:T(8,128)(2,1)}, u32[]{:S(2)}) copy-start(bf16[2,1024,1024]{2,1,0:T(8,128)(2,1)} %param.17) | copy-start | bytes 12582916
  0.6 9.1 %copy-start.1 = (f32[1,1,4,64,1024]{4,3,2,1,0:T(8,128)S(1)}, f32[1,1,4,64,1024]{4,3,2,1,0:T(8,128)}, u32[]{:S(2)}) copy-start(f32[1,1,4,64,1024]{4,3,2,1,0:T(8,128)} %param.33) | copy-start | bytes 3145732
  7.2 3.5 %copy-start.13 = (bf16[2,1024,1024]{2,1,0:T(8,128)(2,1)S(1)}, bf16[2,1024,1024]{2,1,0:T(8,128)(2,1)}, u32[]{:S(2)}) copy-start(bf16[2,1024,1024]{2,1,0:T(8,128)(2,1)} %param.18) | copy-start | bytes 12582916
  11.4 3.4 %copy-start.15 = (f32[1,1,4,64,1024]{4,3,2,1,0:T(8,128)S(1)}, f32[1,1,4,64,1024]{4,3,2,1,0:T(8,128)}, u32[]{:S(2)}) copy-start(f32[1,1,4,64,1024]{4,3,2,1,0:T(8,128)} %param.32) | copy-start | bytes 3145732
  14.9 46.6 %copy-start.2 = (f32[64,2048]{1,0:T(8,128)S(1)}, f32[64,2048]{1,0:T(8,128)}, u32[]{:S(2)}) copy-start(f32[64,2048]{1,0:T(8,128)} %param.28) | copy-start | bytes 1572868
  14.9 46.6 %copy-start.3 = (f32[64,2048]{1,0:T(8,128)S(1)}, f32[64,2048]{1,0:T(8,128)}, u32[]{:S(2)}) copy-start(f32[64,2048]{1,0:T(8,128)} %param.30) | copy-start | bytes 1572868
  14.9 46.6 %copy-start.4 = (f32[64,2048]{1,0:T(8,128)S(1)}, f32[64,2048]{1,0:T(8,128)}, u32[]{:S(2)}) copy-start(f32[64,2048]{1,0:T(8,128)} %param.29) | copy-start | bytes 1572868
  14.9 46.6 %copy-start.5 = (f32[64,2048]{1,0:T(8,128)S(1)}, f32[64,2048]{1,0:T(8,128)}, u32[]{:S(2)}) copy-start(f32[64,2048]{1,0:T(8,128)} %param.27) | copy-start | bytes 1572868
  17.6 45.4 %copy-start = (f32[64,2048]{1,0:T(8,128)S(1)}, f32[64,2048]{1,0:T(8,128)}, u32[]{:S(2)}) copy-start(f32[64,2048]{1,0:T(8,128)} %param.23) | copy-start | bytes 1572868
  17.6 45.4 %copy-start.6 = (f32[64,2048]{1,0:T(8,128)S(1)}, f32[64,2048]{1,0:T(8,128)}, u32[]{:S(2)}) copy-start(f32[64,2048]{1,0:T(8,128)} %param.26) | copy-start | bytes 1572868
  59.6 3.2 %copy-start.12 = (f32[4,64,1024]{2,1,0:T(8,128)S(1)}, f32[4,64,1024]{2,1,0:T(8,128)}, u32[]{:S(2)}) copy-start(f32[4,64,1024]{2,1,0:T(8,128)} %get-tuple-element.32) | copy-start | bytes 3145732
  59.6 3.5 %copy-start.7 = (f32[64,2048]{1,0:T(8,128)S(1)}, f32[64,2048]{1,0:T(8,128)}, u32[]{:S(2)}) copy-start(f32[64,2048]{1,0:T(8,128)} %param.25) | copy-start | bytes 1572868
  59.6 3.5 %copy-start.8 = (f32[64,2048]{1,0:T(8,128)S(1)}, f32[64,2048]{1,0:T(8,128)}, u32[]{:S(2)}) copy-start(f32[64,2048]{1,0:T(8,128)} %param.24) | copy-start | bytes 1572868
  59.6 3.5 %copy-start.9 = (f32[72,2048]{1,0:T(8,128)S(1)}, f32[72,2048]{1,0:T(8,128)}, u32[]{:S(2)}) copy-start(f32[72,2048]{1,0:T(8,128)} %get-tuple-element.6) | copy-start | bytes 1769476
  62.8 2.2 %copy-start.11 = (bf16[2,1024,1024]{2,1,0:T(8,128)(2,1)S(1)}, bf16[2,1024,1024]{2,1,0:T(8,128)(2,1)}, u32[]{:S(2)}) copy-start(bf16[2,1024,1024]{2,1,0:T(8,128)(2,1)} %param.17) | copy-start | bytes 12582916
  63.1 2.6 %copy-start.16 = (f32[4,64,1024]{2,1,0:T(8,128)S(1)}, f32[4,64,1024]{2,1,0:T(8,128)}, u32[]{:S(2)}) copy-start(f32[4,64,1024]{2,1,0:T(8,128)} %get-tuple-element.18) | copy-start | bytes 3145732
  64.9 2.3 %copy-start.14 = (bf16[2,1024,1024]{2,1,0:T(8,128)(2,1)S(1)}, bf16[2,1024,1024]{2,1,0:T(8,128)(2,1)}, u32[]{:S(2)}) copy-start(bf16[2,1024,1024]{2,1,0:T(8,128)(2,1)} %param.18) | copy-start | bytes 12582916

commit v11 on v9

--- a/solution.py
+++ b/solution.py
@@ -86,8 +86,9 @@
             copies.append(copy)
         scatter[g] = copies
 
-    gathers = []
-    for g, axis in enumerate(group_axes):
+    gathers = [None] * groups
+    for g in issue_order:
+        axis = group_axes[g]
         recv, gathered, s1, r1, s2, r2 = per[g]
         me = lax.axis_index(axis)
         for k in range(1, n):
@@ -117,7 +118,7 @@
             )
             copy.start()
             copies.append(copy)
-        gathers.append(copies)
+        gathers[g] = copies
 
     for g, axis in enumerate(group_axes):
         recv, gathered, s1, r1, s2, r2 = per[g]

time: 117 us -> 115 us (0.983); the launches traced: 115 us -> 114 us
  no operation moved by 1% of the time
where the time goes in v11:
time: 115 us; the launch traced here: 114 us
  Pallas kernels  78.8 us (69%)
  other arithmetic  16.7 us (15%)
  matrix products  13.8 us (12%)
  local copies, waits for them, and re-layouts  3.38 us (3%)
  between operations  1.78 us (2%)
    pallas_call x2, Pallas kernels, all_reduce(): pl.pallas_call(functools.partial(reduce_kernel, n, group_axes, block_widt...  78.8 us
    dot_general x12, matrix products, by_tile(): lax.dot_general(stacked, matrices[t], (((1,), (contract,)), ((), ())), pr...  13.8 us
    min x1, other arithmetic, per_device(): column_final = jnp.clip(x_own - x_dual - unit_cost, 0.0, capacity)  2.73 us
    min x1, other arithmetic, per_device(): row_final = jnp.clip(y_state - y_dual, row_lower, row_upper)  2.41 us

profile of v11, /device:TPU:1, one launch (start us, length us, event | category | flops | bytes accessed | tf_op | source)
XLA Modules:
  0.0 114.4 jit_solution(1205718486365001892)
XLA Ops:
  0.6 0.0 copy-start.10
  0.6 0.0 copy-start.1
  1.4 1.1 compare_bitcast_fusion
  2.5 1.3 %pad_add_fusion.refs_0_ = s32[9]{0:T(128)} fusion(s32[1]{0:T(128)} %bitcast.102, s32[4]{0:T(128)} %bitcast.109, s32[4]{0:T(128)} %bitcast.108), kind=kLoop, calls=%fused_computation.90 | loop fusion | flops 18 | bytes 72 | tf_op jit(solution)/shard_map/concatenate | solution.py:259
  3.8 0.7 fusion.85
  4.5 1.7 %fusion.79 = bf16[4,64,1024]{2,1,0:T(8,128)(2,1)S(1)} fusion(f32[1,1,4,64,1024]{4,3,2,1,0:T(8,128)} %param.31, f32[1,1,4,64,1024]{4,3,2,1,0:T(8,128)} %param.32), kind=kLoop, calls=%fused_computation.72 | loop fusion | flops 524288 | bytes 2621440 | tf_op jit(solution)/shard_map/convert_element_type | solution.py:241
  6.2 1.1 fusion.88
  7.3 0.0 copy-start.13
  7.3 2.5 %fusion.14 = f32[4,64,1024]{2,1,0:T(8,128)S(1)} fusion(bf16[4,64,1024]{2,1,0:T(8,128)(2,1)S(1)} %fusion.79, bf16[2,1024,1024]{2,1,0:T(8,128)(2,1)} %param.17), kind=kOutput, calls=%fused_computation.14 | convolution fusion | flops 536870912 | bytes 3670016 | tf_op jit(solution)/shard_map/dot_general | solution.py:183
  9.8 0.0 copy-done.10
  9.8 0.0 copy-done.1
  9.8 0.9 fusion.69
  10.8 0.0 copy-done.13
  10.8 0.7 fusion.2
  11.5 1.9 %select_reduce_fusion.7 = (f32[64,1024]{1,0:T(8,128)S(1)}, f32[64,1024]{1,0:T(8,128)S(1)}, f32[4,64,1024]{2,1,0:T(8,128)}, bf16[4,64,1024]{2,1,0:T(8,128)(2,1)S(1)}) fusion(pred[4]{0:T(512)(128)(4,1)S(1)} %get-tuple-element.30, pred[4]{0:T(512)(128)(4,1)S(1)} %get-tuple-element.28, f32[1,1,4,64,1024]{4,3,2,1,0:T(8,128)S(1)} %copy-done.1, ...), kind=kOutput, calls=%fused_computation.62 | convolution fusion | flops 538574848 | bytes 6817280 | tf_op jit(solution)/shard_map/dot_general | solution.py:183
  13.4 0.0 copy-start.15
  13.4 0.8 pad_maximum_fusion.refs_1_
  14.2 0.7 fusion.12
  15.0 0.0 copy-done.15
  15.0 0.0 copy-start.2
  15.0 0.0 copy-start.3
  15.0 0.0 copy-start.4
  15.0 0.0 copy-start.5
  15.0 1.9 %select_reduce_fusion.5 = (f32[64,1024]{1,0:T(8,128)S(1)}, f32[64,1024]{1,0:T(8,128)S(1)}, f32[4,64,1024]{2,1,0:T(8,128)}) fusion(pred[4]{0:T(512)(128)(4,1)S(1)} %get-tuple-element.34, pred[4]{0:T(512)(128)(4,1)S(1)} %get-tuple-element.35, f32[1,1,4,64,1024]{4,3,2,1,0:T(8,128)S(1)} %copy-done.15, f32[4,64,1024]{2,1,0:T(8,128)S(1)} %fusion.12, ...), kind=kOutput, calls=%fused_computation.60 | convolution fusion | flops 538312704 | bytes 6292992 | tf_op jit(solution)/shard_map/dot_general | solution.py:183
  17.0 0.0 copy-start
  17.0 0.0 copy-start.6
  17.0 0.8 pad_maximum_fusion.1.refs_2_
  17.8 42.0 %shard_map.176 = (f32[72,2048]{1,0:T(8,128)}, f32[72,2048]{1,0:T(8,128)}) custom-call(s32[9]{0:T(128)} %pad_add_fusion.refs_0_, f32[64,2048]{1,0:T(8,128)} %pad_maximum_fusion.refs_1_, f32[64,2048]{1,0:T(8,128)} %pad_maximum_fusion.1.refs_2_), custom_call_target="tpu_custom_call" | custom-call | tf_op jit(solution)/shard_map/pallas_call | solution.py:162
  59.8 0.0 copy-start.12
  59.8 0.0 copy-start.7
  59.8 0.0 copy-start.8
  59.8 0.0 copy-start.9
  59.9 1.0 slice_add_fusion.1
  60.9 0.8 slice_add_fusion
  61.7 0.0 copy-done.2
  61.7 0.0 copy-done.3
  61.7 0.0 copy-done.4
  61.7 0.0 copy-done.5
  61.7 1.2 %subtract_divide_fusion = f32[64,2048]{1,0:T(8,128)S(1)} fusion(f32[72,2048]{1,0:T(8,128)} %get-tuple-element.7, f32[2048]{0:T(1024)S(1)} %bitcast.106, f32[64,2048]{1,0:T(8,128)S(1)} %copy-done.2, f32[64,2048]{1,0:T(8,128)S(1)} %copy-done.3, f32[64,2048]{1,0:T(8,128)S(1)} %copy-done.4, f32[64,2048]{1,0:T(8,128)S(1)} %copy-done.5), kind=kLoop, calls=%fused_computation.77 | loop fusion | flops 786432 | bytes 3153920 | tf_op jit(solution)/shard_map/div | solution.py:271
  62.9 0.0 copy-start.11
  63.0 0.0 copy-done.12
  63.0 0.2 subtract_convert_fusion
  63.3 0.0 copy-done
  63.3 0.0 copy-done.6
  63.3 0.0 copy-done.7
  63.3 0.0 copy-done.8
  63.3 0.0 copy-done.9
  63.3 0.0 copy-start.16
  63.3 0.2 add_divide_fusion
  63.6 1.6 %copy-done.11 = bf16[2,1024,1024]{2,1,0:T(8,128)(2,1)S(1)} copy-done((bf16[2,1024,1024]{2,1,0:T(8,128)(2,1)S(1)}, bf16[2,1024,1024]{2,1,0:T(8,128)(2,1)}, u32[]{:S(2)}) %copy-start.11) | copy-done | bytes 4194328
  65.1 0.0 copy-start.14
  65.1 0.7 fusion.10
  65.9 0.0 copy-done.16
  65.9 0.9 fusion.66
  66.8 0.6 copy-done.14
  67.4 0.7 fusion
  68.1 1.0 select_reduce_fusion.3
  69.2 0.8 pad_maximum_fusion.2.refs_0_
  70.0 0.7 fusion.8
  70.7 1.0 select_reduce_fusion.1
  71.7 0.8 pad_maximum_fusion.3.refs_1_
  72.5 36.8 %shard_map.177 = (f32[64,2048]{1,0:T(8,128)}, f32[64,2048]{1,0:T(8,128)}) custom-call(f32[64,2048]{1,0:T(8,128)} %pad_maximum_fusion.2.refs_0_, f32[64,2048]{1,0:T(8,128)} %pad_maximum_fusion.3.refs_1_), custom_call_target="tpu_custom_call" | custom-call | tf_op jit(solution)/shard_map/pallas_call | solution.py:162
  109.3 2.4 %fusion.78 = f32[64,2048]{1,0:T(8,128)} fusion(f32[64,2048]{1,0:T(8,128)S(1)} %copy-done.3, f32[64,2048]{1,0:T(8,128)S(1)} %copy-done.4, f32[64,2048]{1,0:T(8,128)} %get-tuple-element.9, f32[2048]{0:T(1024)S(1)} %bitcast.107, f32[64,2048]{1,0:T(8,128)S(1)} %copy-done.2, f32[64,2048]{1,0:T(8,128)S(1)} %copy-done.5, f32[72,2048]{1,0:T(8,128)} %get-tuple-element.7), kind=kLoop, calls=%fused_computation.71 | loop fusion | flops 2490368 | bytes 3678208 | tf_op jit(solution)/shard_map/jit(clip)/min | solution.py:279
  111.7 2.7 %fusion.76 = f32[64,2048]{1,0:T(8,128)} fusion(f32[64,2048]{1,0:T(8,128)S(1)} %copy-done.6, f32[64,2048]{1,0:T(8,128)} %param.25, f32[64,2048]{1,0:T(8,128)} %get-tuple-element.8, f32[2048]{0:T(1024)S(1)} %bitcast.105, f32[64,2048]{1,0:T(8,128)} %param.24, f32[64,2048]{1,0:T(8,128)S(1)} %copy-done, f32[72,2048]{1,0:T(8,128)} %get-tuple-element.6), kind=kLoop, calls=%fused_computation.69 | loop fusion | flops 2621440 | bytes 3678208 | tf_op jit(solution)/shard_map/jit(clip)/min | solution.py:278
  (2 shorter events, 0.1 us)
Async XLA Ops:
  0.6 9.2 %copy-start.10 = (bf16[2,1024,1024]{2,1,0:T(8,128)(2,1)S(1)}, bf16[2,1024,1024]{2,1,0:T(8,128)(2,1)}, u32[]{:S(2)}) copy-start(bf16[2,1024,1024]{2,1,0:T(8,128)(2,1)} %param.17) | copy-start | bytes 12582916
  0.6 9.2 %copy-start.1 = (f32[1,1,4,64,1024]{4,3,2,1,0:T(8,128)S(1)}, f32[1,1,4,64,1024]{4,3,2,1,0:T(8,128)}, u32[]{:S(2)}) copy-start(f32[1,1,4,64,1024]{4,3,2,1,0:T(8,128)} %param.33) | copy-start | bytes 3145732
  7.3 3.5 %copy-start.13 = (bf16[2,1024,1024]{2,1,0:T(8,128)(2,1)S(1)}, bf16[2,1024,1024]{2,1,0:T(8,128)(2,1)}, u32[]{:S(2)}) copy-start(bf16[2,1024,1024]{2,1,0:T(8,128)(2,1)} %param.18) | copy-start | bytes 12582916
  13.4 1.6 %copy-start.15 = (f32[1,1,4,64,1024]{4,3,2,1,0:T(8,128)S(1)}, f32[1,1,4,64,1024]{4,3,2,1,0:T(8,128)}, u32[]{:S(2)}) copy-start(f32[1,1,4,64,1024]{4,3,2,1,0:T(8,128)} %param.32) | copy-start | bytes 3145732
  15.0 46.7 %copy-start.2 = (f32[64,2048]{1,0:T(8,128)S(1)}, f32[64,2048]{1,0:T(8,128)}, u32[]{:S(2)}) copy-start(f32[64,2048]{1,0:T(8,128)} %param.28) | copy-start | bytes 1572868
  15.0 46.7 %copy-start.3 = (f32[64,2048]{1,0:T(8,128)S(1)}, f32[64,2048]{1,0:T(8,128)}, u32[]{:S(2)}) copy-start(f32[64,2048]{1,0:T(8,128)} %param.30) | copy-start | bytes 1572868
  15.0 46.7 %copy-start.4 = (f32[64,2048]{1,0:T(8,128)S(1)}, f32[64,2048]{1,0:T(8,128)}, u32[]{:S(2)}) copy-start(f32[64,2048]{1,0:T(8,128)} %param.29) | copy-start | bytes 1572868
  15.0 46.7 %copy-start.5 = (f32[64,2048]{1,0:T(8,128)S(1)}, f32[64,2048]{1,0:T(8,128)}, u32[]{:S(2)}) copy-start(f32[64,2048]{1,0:T(8,128)} %param.27) | copy-start | bytes 1572868
  17.0 46.3 %copy-start = (f32[64,2048]{1,0:T(8,128)S(1)}, f32[64,2048]{1,0:T(8,128)}, u32[]{:S(2)}) copy-start(f32[64,2048]{1,0:T(8,128)} %param.23) | copy-start | bytes 1572868
  17.0 46.3 %copy-start.6 = (f32[64,2048]{1,0:T(8,128)S(1)}, f32[64,2048]{1,0:T(8,128)}, u32[]{:S(2)}) copy-start(f32[64,2048]{1,0:T(8,128)} %param.26) | copy-start | bytes 1572868
  59.8 3.2 %copy-start.12 = (f32[4,64,1024]{2,1,0:T(8,128)S(1)}, f32[4,64,1024]{2,1,0:T(8,128)}, u32[]{:S(2)}) copy-start(f32[4,64,1024]{2,1,0:T(8,128)} %get-tuple-element.32) | copy-start | bytes 3145732
  59.8 3.5 %copy-start.7 = (f32[64,2048]{1,0:T(8,128)S(1)}, f32[64,2048]{1,0:T(8,128)}, u32[]{:S(2)}) copy-start(f32[64,2048]{1,0:T(8,128)} %param.25) | copy-start | bytes 1572868
  59.8 3.5 %copy-start.8 = (f32[64,2048]{1,0:T(8,128)S(1)}, f32[64,2048]{1,0:T(8,128)}, u32[]{:S(2)}) copy-start(f32[64,2048]{1,0:T(8,128)} %param.24) | copy-start | bytes 1572868
  59.8 3.5 %copy-start.9 = (f32[72,2048]{1,0:T(8,128)S(1)}, f32[72,2048]{1,0:T(8,128)}, u32[]{:S(2)}) copy-start(f32[72,2048]{1,0:T(8,128)} %get-tuple-element.6) | copy-start | bytes 1769476
  62.9 2.2 %copy-start.11 = (bf16[2,1024,1024]{2,1,0:T(8,128)(2,1)S(1)}, bf16[2,1024,1024]{2,1,0:T(8,128)(2,1)}, u32[]{:S(2)}) copy-start(bf16[2,1024,1024]{2,1,0:T(8,128)(2,1)} %param.17) | copy-start | bytes 12582916
  63.3 2.6 %copy-start.16 = (f32[4,64,1024]{2,1,0:T(8,128)S(1)}, f32[4,64,1024]{2,1,0:T(8,128)}, u32[]{:S(2)}) copy-start(f32[4,64,1024]{2,1,0:T(8,128)} %get-tuple-element.18) | copy-start | bytes 3145732
  65.1 2.3 %copy-start.14 = (bf16[2,1024,1024]{2,1,0:T(8,128)(2,1)S(1)}, bf16[2,1024,1024]{2,1,0:T(8,128)(2,1)}, u32[]{:S(2)}) copy-start(bf16[2,1024,1024]{2,1,0:T(8,128)(2,1)} %param.18) | copy-start | bytes 12582916

commit v12 on v11

--- a/solution.py
+++ b/solution.py
@@ -66,13 +66,14 @@
             pl.semaphore_signal(barrier, inc=1, device_id=peer_id(axis, peer), device_id_type=MESH)
     pl.semaphore_wait(barrier, groups * (n - 1))
 
+    far_first = sorted(range(1, n), key=lambda k: (-min(k, n - k), k))
     scatter = [None] * groups
     for g in issue_order:
         axis = group_axes[g]
         recv, gathered, s1, r1, s2, r2 = per[g]
         me = lax.axis_index(axis)
         copies = []
-        for k in range(1, n):
+        for k in far_first:
             peer = lax.rem(me + k, n)
             copy = pltpu.make_async_remote_copy(
                 src_ref=piece(sources[g], peer),
@@ -106,7 +107,7 @@
             total = total + recv[lax.rem(me + k, n)]
         outs[g][:, cols(me)] = total
         copies = []
-        for k in range(1, n):
+        for k in far_first:
             peer = lax.rem(me + k, n)
             copy = pltpu.make_async_remote_copy(
                 src_ref=outs[g].at[:, cols(me)],

time: 115 us -> 115 us (level)
  no operation moved by 1% of the time
where the time goes in v12:
time: 115 us
  Pallas kernels  79.4 us (69%)
  other arithmetic  16.7 us (15%)
  matrix products  13.8 us (12%)
  local copies, waits for them, and re-layouts  3.38 us (3%)
  between operations  1.78 us (2%)
    pallas_call x2, Pallas kernels, all_reduce(): pl.pallas_call(functools.partial(reduce_kernel, n, group_axes, block_widt...  79.4 us
    dot_general x12, matrix products, by_tile(): lax.dot_general(stacked, matrices[t], (((1,), (contract,)), ((), ())), pr...  13.8 us
    min x1, other arithmetic, per_device(): column_final = jnp.clip(x_own - x_dual - unit_cost, 0.0, capacity)  2.73 us
    min x1, other arithmetic, per_device(): row_final = jnp.clip(y_state - y_dual, row_lower, row_upper)  2.41 us

profile of v12, /device:TPU:1, one launch (start us, length us, event | category | flops | bytes accessed | tf_op | source)
XLA Modules:
  0.0 115.0 jit_solution(656584831185257664)
XLA Ops:
  0.6 0.0 copy-start.10
  0.6 0.0 copy-start.1
  1.4 1.1 compare_bitcast_fusion
  2.5 1.3 %pad_add_fusion.refs_0_ = s32[9]{0:T(128)} fusion(s32[1]{0:T(128)} %bitcast.102, s32[4]{0:T(128)} %bitcast.109, s32[4]{0:T(128)} %bitcast.108), kind=kLoop, calls=%fused_computation.90 | loop fusion | flops 18 | bytes 72 | tf_op jit(solution)/shard_map/concatenate | solution.py:260
  3.8 0.7 fusion.85
  4.5 1.7 %fusion.79 = bf16[4,64,1024]{2,1,0:T(8,128)(2,1)S(1)} fusion(f32[1,1,4,64,1024]{4,3,2,1,0:T(8,128)} %param.31, f32[1,1,4,64,1024]{4,3,2,1,0:T(8,128)} %param.32), kind=kLoop, calls=%fused_computation.72 | loop fusion | flops 524288 | bytes 2621440 | tf_op jit(solution)/shard_map/convert_element_type | solution.py:242
  6.2 1.1 fusion.88
  7.3 0.0 copy-start.13
  7.3 2.5 %fusion.14 = f32[4,64,1024]{2,1,0:T(8,128)S(1)} fusion(bf16[4,64,1024]{2,1,0:T(8,128)(2,1)S(1)} %fusion.79, bf16[2,1024,1024]{2,1,0:T(8,128)(2,1)} %param.17), kind=kOutput, calls=%fused_computation.14 | convolution fusion | flops 536870912 | bytes 3670016 | tf_op jit(solution)/shard_map/dot_general | solution.py:184
  9.8 0.0 copy-done.10
  9.8 0.0 copy-done.1
  9.8 0.9 fusion.69
  10.8 0.0 copy-done.13
  10.8 0.7 fusion.2
  11.5 1.9 %select_reduce_fusion.7 = (f32[64,1024]{1,0:T(8,128)S(1)}, f32[64,1024]{1,0:T(8,128)S(1)}, f32[4,64,1024]{2,1,0:T(8,128)}, bf16[4,64,1024]{2,1,0:T(8,128)(2,1)S(1)}) fusion(pred[4]{0:T(512)(128)(4,1)S(1)} %get-tuple-element.30, pred[4]{0:T(512)(128)(4,1)S(1)} %get-tuple-element.28, f32[1,1,4,64,1024]{4,3,2,1,0:T(8,128)S(1)} %copy-done.1, ...), kind=kOutput, calls=%fused_computation.62 | convolution fusion | flops 538574848 | bytes 6817280 | tf_op jit(solution)/shard_map/dot_general | solution.py:184
  13.4 0.0 copy-start.15
  13.4 0.8 pad_maximum_fusion.refs_1_
  14.2 0.7 fusion.12
  15.0 0.0 copy-done.15
  15.0 0.0 copy-start.2
  15.0 0.0 copy-start.3
  15.0 0.0 copy-start.4
  15.0 0.0 copy-start.5
  15.0 1.9 %select_reduce_fusion.5 = (f32[64,1024]{1,0:T(8,128)S(1)}, f32[64,1024]{1,0:T(8,128)S(1)}, f32[4,64,1024]{2,1,0:T(8,128)}) fusion(pred[4]{0:T(512)(128)(4,1)S(1)} %get-tuple-element.34, pred[4]{0:T(512)(128)(4,1)S(1)} %get-tuple-element.35, f32[1,1,4,64,1024]{4,3,2,1,0:T(8,128)S(1)} %copy-done.15, f32[4,64,1024]{2,1,0:T(8,128)S(1)} %fusion.12, ...), kind=kOutput, calls=%fused_computation.60 | convolution fusion | flops 538312704 | bytes 6292992 | tf_op jit(solution)/shard_map/dot_general | solution.py:184
  17.0 0.0 copy-start
  17.0 0.0 copy-start.6
  17.0 0.8 pad_maximum_fusion.1.refs_2_
  17.8 44.3 %shard_map.176 = (f32[72,2048]{1,0:T(8,128)}, f32[72,2048]{1,0:T(8,128)}) custom-call(s32[9]{0:T(128)} %pad_add_fusion.refs_0_, f32[64,2048]{1,0:T(8,128)} %pad_maximum_fusion.refs_1_, f32[64,2048]{1,0:T(8,128)} %pad_maximum_fusion.1.refs_2_), custom_call_target="tpu_custom_call" | custom-call | tf_op jit(solution)/shard_map/pallas_call | solution.py:163
  62.1 0.0 copy-start.12
  62.1 0.0 copy-start.7
  62.2 0.0 copy-start.8
  62.2 0.0 copy-start.9
  62.2 1.0 slice_add_fusion.1
  63.2 0.8 slice_add_fusion
  64.0 0.0 copy-done.2
  64.0 0.0 copy-done.3
  64.0 0.0 copy-done.4
  64.0 0.0 copy-done.5
  64.1 1.2 %subtract_divide_fusion = f32[64,2048]{1,0:T(8,128)S(1)} fusion(f32[72,2048]{1,0:T(8,128)} %get-tuple-element.7, f32[2048]{0:T(1024)S(1)} %bitcast.106, f32[64,2048]{1,0:T(8,128)S(1)} %copy-done.2, f32[64,2048]{1,0:T(8,128)S(1)} %copy-done.3, f32[64,2048]{1,0:T(8,128)S(1)} %copy-done.4, f32[64,2048]{1,0:T(8,128)S(1)} %copy-done.5), kind=kLoop, calls=%fused_computation.77 | loop fusion | flops 786432 | bytes 3153920 | tf_op jit(solution)/shard_map/div | solution.py:272
  65.3 0.0 copy-start.11
  65.3 0.0 copy-done.12
  65.3 0.2 subtract_convert_fusion
  65.6 0.0 copy-done
  65.6 0.0 copy-done.6
  65.6 0.0 copy-done.7
  65.6 0.0 copy-done.8
  65.6 0.0 copy-done.9
  65.6 0.0 copy-start.16
  65.6 0.2 add_divide_fusion
  65.9 1.6 %copy-done.11 = bf16[2,1024,1024]{2,1,0:T(8,128)(2,1)S(1)} copy-done((bf16[2,1024,1024]{2,1,0:T(8,128)(2,1)S(1)}, bf16[2,1024,1024]{2,1,0:T(8,128)(2,1)}, u32[]{:S(2)}) %copy-start.11) | copy-done | bytes 4194328
  67.5 0.0 copy-start.14
  67.5 0.7 fusion.10
  68.2 0.0 copy-done.16
  68.2 0.9 fusion.66
  69.1 0.6 copy-done.14
  69.7 0.7 fusion
  70.4 1.0 select_reduce_fusion.3
  71.5 0.8 pad_maximum_fusion.2.refs_0_
  72.3 0.7 fusion.8
  73.0 1.0 select_reduce_fusion.1
  74.0 0.8 pad_maximum_fusion.3.refs_1_
  74.8 35.1 %shard_map.177 = (f32[64,2048]{1,0:T(8,128)}, f32[64,2048]{1,0:T(8,128)}) custom-call(f32[64,2048]{1,0:T(8,128)} %pad_maximum_fusion.2.refs_0_, f32[64,2048]{1,0:T(8,128)} %pad_maximum_fusion.3.refs_1_), custom_call_target="tpu_custom_call" | custom-call | tf_op jit(solution)/shard_map/pallas_call | solution.py:163
  109.9 2.4 %fusion.78 = f32[64,2048]{1,0:T(8,128)} fusion(f32[64,2048]{1,0:T(8,128)S(1)} %copy-done.3, f32[64,2048]{1,0:T(8,128)S(1)} %copy-done.4, f32[64,2048]{1,0:T(8,128)} %get-tuple-element.9, f32[2048]{0:T(1024)S(1)} %bitcast.107, f32[64,2048]{1,0:T(8,128)S(1)} %copy-done.2, f32[64,2048]{1,0:T(8,128)S(1)} %copy-done.5, f32[72,2048]{1,0:T(8,128)} %get-tuple-element.7), kind=kLoop, calls=%fused_computation.71 | loop fusion | flops 2490368 | bytes 3678208 | tf_op jit(solution)/shard_map/jit(clip)/min | solution.py:280
  112.3 2.7 %fusion.76 = f32[64,2048]{1,0:T(8,128)} fusion(f32[64,2048]{1,0:T(8,128)S(1)} %copy-done.6, f32[64,2048]{1,0:T(8,128)} %param.25, f32[64,2048]{1,0:T(8,128)} %get-tuple-element.8, f32[2048]{0:T(1024)S(1)} %bitcast.105, f32[64,2048]{1,0:T(8,128)} %param.24, f32[64,2048]{1,0:T(8,128)S(1)} %copy-done, f32[72,2048]{1,0:T(8,128)} %get-tuple-element.6), kind=kLoop, calls=%fused_computation.69 | loop fusion | flops 2621440 | bytes 3678208 | tf_op jit(solution)/shard_map/jit(clip)/min | solution.py:279
  (2 shorter events, 0.1 us)
Async XLA Ops:
  0.6 9.2 %copy-start.10 = (bf16[2,1024,1024]{2,1,0:T(8,128)(2,1)S(1)}, bf16[2,1024,1024]{2,1,0:T(8,128)(2,1)}, u32[]{:S(2)}) copy-start(bf16[2,1024,1024]{2,1,0:T(8,128)(2,1)} %param.17) | copy-start | bytes 12582916
  0.6 9.2 %copy-start.1 = (f32[1,1,4,64,1024]{4,3,2,1,0:T(8,128)S(1)}, f32[1,1,4,64,1024]{4,3,2,1,0:T(8,128)}, u32[]{:S(2)}) copy-start(f32[1,1,4,64,1024]{4,3,2,1,0:T(8,128)} %param.33) | copy-start | bytes 3145732
  7.3 3.5 %copy-start.13 = (bf16[2,1024,1024]{2,1,0:T(8,128)(2,1)S(1)}, bf16[2,1024,1024]{2,1,0:T(8,128)(2,1)}, u32[]{:S(2)}) copy-start(bf16[2,1024,1024]{2,1,0:T(8,128)(2,1)} %param.18) | copy-start | bytes 12582916
  13.4 1.6 %copy-start.15 = (f32[1,1,4,64,1024]{4,3,2,1,0:T(8,128)S(1)}, f32[1,1,4,64,1024]{4,3,2,1,0:T(8,128)}, u32[]{:S(2)}) copy-start(f32[1,1,4,64,1024]{4,3,2,1,0:T(8,128)} %param.32) | copy-start | bytes 3145732
  15.0 49.1 %copy-start.2 = (f32[64,2048]{1,0:T(8,128)S(1)}, f32[64,2048]{1,0:T(8,128)}, u32[]{:S(2)}) copy-start(f32[64,2048]{1,0:T(8,128)} %param.28) | copy-start | bytes 1572868
  15.0 49.1 %copy-start.3 = (f32[64,2048]{1,0:T(8,128)S(1)}, f32[64,2048]{1,0:T(8,128)}, u32[]{:S(2)}) copy-start(f32[64,2048]{1,0:T(8,128)} %param.30) | copy-start | bytes 1572868
  15.0 49.1 %copy-start.4 = (f32[64,2048]{1,0:T(8,128)S(1)}, f32[64,2048]{1,0:T(8,128)}, u32[]{:S(2)}) copy-start(f32[64,2048]{1,0:T(8,128)} %param.29) | copy-start | bytes 1572868
  15.0 49.0 %copy-start.5 = (f32[64,2048]{1,0:T(8,128)S(1)}, f32[64,2048]{1,0:T(8,128)}, u32[]{:S(2)}) copy-start(f32[64,2048]{1,0:T(8,128)} %param.27) | copy-start | bytes 1572868
  17.0 48.6 %copy-start = (f32[64,2048]{1,0:T(8,128)S(1)}, f32[64,2048]{1,0:T(8,128)}, u32[]{:S(2)}) copy-start(f32[64,2048]{1,0:T(8,128)} %param.23) | copy-start | bytes 1572868
  17.0 48.6 %copy-start.6 = (f32[64,2048]{1,0:T(8,128)S(1)}, f32[64,2048]{1,0:T(8,128)}, u32[]{:S(2)}) copy-start(f32[64,2048]{1,0:T(8,128)} %param.26) | copy-start | bytes 1572868
  62.1 3.2 %copy-start.12 = (f32[4,64,1024]{2,1,0:T(8,128)S(1)}, f32[4,64,1024]{2,1,0:T(8,128)}, u32[]{:S(2)}) copy-start(f32[4,64,1024]{2,1,0:T(8,128)} %get-tuple-element.32) | copy-start | bytes 3145732
  62.1 3.5 %copy-start.7 = (f32[64,2048]{1,0:T(8,128)S(1)}, f32[64,2048]{1,0:T(8,128)}, u32[]{:S(2)}) copy-start(f32[64,2048]{1,0:T(8,128)} %param.25) | copy-start | bytes 1572868
  62.2 3.5 %copy-start.8 = (f32[64,2048]{1,0:T(8,128)S(1)}, f32[64,2048]{1,0:T(8,128)}, u32[]{:S(2)}) copy-start(f32[64,2048]{1,0:T(8,128)} %param.24) | copy-start | bytes 1572868
  62.2 3.5 %copy-start.9 = (f32[72,2048]{1,0:T(8,128)S(1)}, f32[72,2048]{1,0:T(8,128)}, u32[]{:S(2)}) copy-start(f32[72,2048]{1,0:T(8,128)} %get-tuple-element.6) | copy-start | bytes 1769476
  65.3 2.2 %copy-start.11 = (bf16[2,1024,1024]{2,1,0:T(8,128)(2,1)S(1)}, bf16[2,1024,1024]{2,1,0:T(8,128)(2,1)}, u32[]{:S(2)}) copy-start(bf16[2,1024,1024]{2,1,0:T(8,128)(2,1)} %param.17) | copy-start | bytes 12582916
  65.6 2.6 %copy-start.16 = (f32[4,64,1024]{2,1,0:T(8,128)S(1)}, f32[4,64,1024]{2,1,0:T(8,128)}, u32[]{:S(2)}) copy-start(f32[4,64,1024]{2,1,0:T(8,128)} %get-tuple-element.18) | copy-start | bytes 3145732
  67.5 2.3 %copy-start.14 = (bf16[2,1024,1024]{2,1,0:T(8,128)(2,1)S(1)}, bf16[2,1024,1024]{2,1,0:T(8,128)(2,1)}, u32[]{:S(2)}) copy-start(bf16[2,1024,1024]{2,1,0:T(8,128)(2,1)} %param.18) | copy-start | bytes 12582916

commit v13 on v11

--- a/solution.py
+++ b/solution.py
@@ -66,24 +66,35 @@
             pl.semaphore_signal(barrier, inc=1, device_id=peer_id(axis, peer), device_id_type=MESH)
     pl.semaphore_wait(barrier, groups * (n - 1))
 
+    def rows_of(g):
+        total_rows = outs[g].shape[0]
+        first = ((total_rows // 2 + 7) // 8) * 8
+        return [(0, first), (first, total_rows - first)]
+
+    def part(ref, index, start, count):
+        if len(ref.shape) == 3:
+            return ref.at[index, pl.ds(start, count)]
+        return ref.at[pl.ds(start, count), cols(index)]
+
     scatter = [None] * groups
     for g in issue_order:
         axis = group_axes[g]
         recv, gathered, s1, r1, s2, r2 = per[g]
         me = lax.axis_index(axis)
         copies = []
-        for k in range(1, n):
-            peer = lax.rem(me + k, n)
-            copy = pltpu.make_async_remote_copy(
-                src_ref=piece(sources[g], peer),
-                dst_ref=recv.at[me],
-                send_sem=s1.at[peer],
-                recv_sem=r1.at[me],
-                device_id=peer_id(axis, peer),
-                device_id_type=MESH,
-            )
-            copy.start()
-            copies.append(copy)
+        for h, (start, count) in enumerate(rows_of(g)):
+            for k in range(1, n):
+                peer = lax.rem(me + k, n)
+                copy = pltpu.make_async_remote_copy(
+                    src_ref=part(sources[g], peer, start, count),
+                    dst_ref=recv.at[me, pl.ds(start, count)],
+                    send_sem=s1.at[h, peer],
+                    recv_sem=r1.at[h, me],
+                    device_id=peer_id(axis, peer),
+                    device_id_type=MESH,
+                )
+                copy.start()
+                copies.append(copy)
         scatter[g] = copies
 
     gathers = [None] * groups
@@ -91,33 +102,34 @@
         axis = group_axes[g]
         recv, gathered, s1, r1, s2, r2 = per[g]
         me = lax.axis_index(axis)
-        for k in range(1, n):
-            source = lax.rem(me + n - k, n)
-            pltpu.make_async_remote_copy(
-                src_ref=piece(sources[g], source),
-                dst_ref=recv.at[source],
-                send_sem=s1.at[source],
-                recv_sem=r1.at[source],
-                device_id=peer_id(axis, source),
-                device_id_type=MESH,
-            ).wait_recv()
-        total = piece(sources[g], me)[...]
-        for k in range(1, n):
-            total = total + recv[lax.rem(me + k, n)]
-        outs[g][:, cols(me)] = total
         copies = []
-        for k in range(1, n):
-            peer = lax.rem(me + k, n)
-            copy = pltpu.make_async_remote_copy(
-                src_ref=outs[g].at[:, cols(me)],
-                dst_ref=outs[g].at[:, cols(me)],
-                send_sem=s2.at[peer],
-                recv_sem=r2.at[me],
-                device_id=peer_id(axis, peer),
-                device_id_type=MESH,
-            )
-            copy.start()
-            copies.append(copy)
+        for h, (start, count) in enumerate(rows_of(g)):
+            for k in range(1, n):
+                source = lax.rem(me + n - k, n)
+                pltpu.make_async_remote_copy(
+                    src_ref=part(sources[g], source, start, count),
+                    dst_ref=recv.at[source, pl.ds(start, count)],
+                    send_sem=s1.at[h, source],
+                    recv_sem=r1.at[h, source],
+                    device_id=peer_id(axis, source),
+                    device_id_type=MESH,
+                ).wait_recv()
+            total = part(sources[g], me, start, count)[...]
+            for k in range(1, n):
+                total = total + recv[lax.rem(me + k, n), start : start + count, :]
+            outs[g][start : start + count, cols(me)] = total
+            for k in range(1, n):
+                peer = lax.rem(me + k, n)
+                copy = pltpu.make_async_remote_copy(
+                    src_ref=part(outs[g], me, start, count),
+                    dst_ref=part(outs[g], me, start, count),
+                    send_sem=s2.at[h, peer],
+                    recv_sem=r2.at[h, me],
+                    device_id=peer_id(axis, peer),
+                    device_id_type=MESH,
+                )
+                copy.start()
+                copies.append(copy)
         gathers[g] = copies
 
     for g, axis in enumerate(group_axes):
@@ -125,16 +137,17 @@
         me = lax.axis_index(axis)
         for copy in scatter[g]:
             copy.wait_send()
-        for k in range(1, n):
-            source = lax.rem(me + n - k, n)
-            pltpu.make_async_remote_copy(
-                src_ref=outs[g].at[:, cols(source)],
-                dst_ref=outs[g].at[:, cols(source)],
-                send_sem=s2.at[source],
-                recv_sem=r2.at[source],
-                device_id=peer_id(axis, source),
-                device_id_type=MESH,
-            ).wait_recv()
+        for h, (start, count) in enumerate(rows_of(g)):
+            for k in range(1, n):
+                source = lax.rem(me + n - k, n)
+                pltpu.make_async_remote_copy(
+                    src_ref=part(outs[g], source, start, count),
+                    dst_ref=part(outs[g], source, start, count),
+                    send_sem=s2.at[h, source],
+                    recv_sem=r2.at[h, source],
+                    device_id=peer_id(axis, source),
+                    device_id_type=MESH,
+                ).wait_recv()
         for copy in gathers[g]:
             copy.wait_send()
 
@@ -148,10 +161,10 @@
         scratch += [
             pltpu.VMEM((n, rows, width), jnp.float32),
             pltpu.VMEM((n, rows, width), jnp.float32),
-            pltpu.SemaphoreType.DMA((n,)),
-            pltpu.SemaphoreType.DMA((n,)),
-            pltpu.SemaphoreType.DMA((n,)),
-            pltpu.SemaphoreType.DMA((n,)),
+            pltpu.SemaphoreType.DMA((2, n)),
+            pltpu.SemaphoreType.DMA((2, n)),
+            pltpu.SemaphoreType.DMA((2, n)),
+            pltpu.SemaphoreType.DMA((2, n)),
         ]
         if info is not None:
             scratch.append(pltpu.VMEM((n, rows, width), jnp.float32))

time: 115 us -> 115 us (level)
  no operation moved by 1% of the time
where the time goes in v13:
time: 115 us
  Pallas kernels  79 us (69%)
  other arithmetic  16.7 us (15%)
  matrix products  13.8 us (12%)
  local copies, waits for them, and re-layouts  3.38 us (3%)
  between operations  1.78 us (2%)
    pallas_call x2, Pallas kernels, all_reduce(): pl.pallas_call(functools.partial(reduce_kernel, n, group_axes, block_widt...  79 us
    dot_general x12, matrix products, by_tile(): lax.dot_general(stacked, matrices[t], (((1,), (contract,)), ((), ())), pr...  13.8 us
    min x1, other arithmetic, per_device(): column_final = jnp.clip(x_own - x_dual - unit_cost, 0.0, capacity)  2.73 us
    min x1, other arithmetic, per_device(): row_final = jnp.clip(y_state - y_dual, row_lower, row_upper)  2.41 us

profile of v13, /device:TPU:1, one launch (start us, length us, event | category | flops | bytes accessed | tf_op | source)
XLA Modules:
  0.0 114.6 jit_solution(12171415787590548286)
XLA Ops:
  0.6 0.0 copy-start.10
  0.6 0.0 copy-start.1
  1.4 1.1 compare_bitcast_fusion
  2.5 1.3 %pad_add_fusion.refs_0_ = s32[9]{0:T(128)} fusion(s32[1]{0:T(128)} %bitcast.102, s32[4]{0:T(128)} %bitcast.109, s32[4]{0:T(128)} %bitcast.108), kind=kLoop, calls=%fused_computation.90 | loop fusion | flops 18 | bytes 72 | tf_op jit(solution)/shard_map/concatenate | solution.py:272
  3.8 0.7 fusion.85
  4.5 1.7 %fusion.79 = bf16[4,64,1024]{2,1,0:T(8,128)(2,1)S(1)} fusion(f32[1,1,4,64,1024]{4,3,2,1,0:T(8,128)} %param.31, f32[1,1,4,64,1024]{4,3,2,1,0:T(8,128)} %param.32), kind=kLoop, calls=%fused_computation.72 | loop fusion | flops 524288 | bytes 2621440 | tf_op jit(solution)/shard_map/convert_element_type | solution.py:254
  6.2 1.1 fusion.88
  7.3 0.0 copy-start.13
  7.3 2.5 %fusion.14 = f32[4,64,1024]{2,1,0:T(8,128)S(1)} fusion(bf16[4,64,1024]{2,1,0:T(8,128)(2,1)S(1)} %fusion.79, bf16[2,1024,1024]{2,1,0:T(8,128)(2,1)} %param.17), kind=kOutput, calls=%fused_computation.14 | convolution fusion | flops 536870912 | bytes 3670016 | tf_op jit(solution)/shard_map/dot_general | solution.py:196
  9.8 0.0 copy-done.10
  9.8 0.0 copy-done.1
  9.8 0.9 fusion.69
  10.7 0.0 copy-done.13
  10.8 0.7 fusion.2
  11.5 1.9 %select_reduce_fusion.7 = (f32[64,1024]{1,0:T(8,128)S(1)}, f32[64,1024]{1,0:T(8,128)S(1)}, f32[4,64,1024]{2,1,0:T(8,128)}, bf16[4,64,1024]{2,1,0:T(8,128)(2,1)S(1)}) fusion(pred[4]{0:T(512)(128)(4,1)S(1)} %get-tuple-element.30, pred[4]{0:T(512)(128)(4,1)S(1)} %get-tuple-element.28, f32[1,1,4,64,1024]{4,3,2,1,0:T(8,128)S(1)} %copy-done.1, ...), kind=kOutput, calls=%fused_computation.62 | convolution fusion | flops 538574848 | bytes 6817280 | tf_op jit(solution)/shard_map/dot_general | solution.py:196
  13.4 0.0 copy-start.15
  13.4 0.8 pad_maximum_fusion.refs_1_
  14.2 0.7 fusion.12
  14.9 0.0 copy-done.15
  15.0 0.0 copy-start.2
  15.0 0.0 copy-start.3
  15.0 0.0 copy-start.4
  15.0 0.0 copy-start.5
  15.0 1.9 %select_reduce_fusion.5 = (f32[64,1024]{1,0:T(8,128)S(1)}, f32[64,1024]{1,0:T(8,128)S(1)}, f32[4,64,1024]{2,1,0:T(8,128)}) fusion(pred[4]{0:T(512)(128)(4,1)S(1)} %get-tuple-element.34, pred[4]{0:T(512)(128)(4,1)S(1)} %get-tuple-element.35, f32[1,1,4,64,1024]{4,3,2,1,0:T(8,128)S(1)} %copy-done.15, f32[4,64,1024]{2,1,0:T(8,128)S(1)} %fusion.12, ...), kind=kOutput, calls=%fused_computation.60 | convolution fusion | flops 538312704 | bytes 6292992 | tf_op jit(solution)/shard_map/dot_general | solution.py:196
  16.9 0.0 copy-start
  16.9 0.0 copy-start.6
  16.9 0.8 pad_maximum_fusion.1.refs_2_
  17.8 44.7 %shard_map.176 = (f32[72,2048]{1,0:T(8,128)}, f32[72,2048]{1,0:T(8,128)}) custom-call(s32[9]{0:T(128)} %pad_add_fusion.refs_0_, f32[64,2048]{1,0:T(8,128)} %pad_maximum_fusion.refs_1_, f32[64,2048]{1,0:T(8,128)} %pad_maximum_fusion.1.refs_2_), custom_call_target="tpu_custom_call" | custom-call | tf_op jit(solution)/shard_map/pallas_call | solution.py:175
  62.5 0.0 copy-start.12
  62.5 0.0 copy-start.7
  62.5 0.0 copy-start.8
  62.5 0.0 copy-start.9
  62.6 1.0 slice_add_fusion.1
  63.6 0.8 slice_add_fusion
  64.4 0.0 copy-done.2
  64.4 0.0 copy-done.3
  64.4 0.0 copy-done.4
  64.4 0.0 copy-done.5
  64.4 1.2 %subtract_divide_fusion = f32[64,2048]{1,0:T(8,128)S(1)} fusion(f32[72,2048]{1,0:T(8,128)} %get-tuple-element.7, f32[2048]{0:T(1024)S(1)} %bitcast.106, f32[64,2048]{1,0:T(8,128)S(1)} %copy-done.2, f32[64,2048]{1,0:T(8,128)S(1)} %copy-done.3, f32[64,2048]{1,0:T(8,128)S(1)} %copy-done.4, f32[64,2048]{1,0:T(8,128)S(1)} %copy-done.5), kind=kLoop, calls=%fused_computation.77 | loop fusion | flops 786432 | bytes 3153920 | tf_op jit(solution)/shard_map/div | solution.py:284
  65.6 0.0 copy-start.11
  65.7 0.0 copy-done.12
  65.7 0.2 subtract_convert_fusion
  66.0 0.0 copy-done
  66.0 0.0 copy-done.6
  66.0 0.0 copy-done.7
  66.0 0.0 copy-done.8
  66.0 0.0 copy-done.9
  66.0 0.0 copy-start.16
  66.0 0.2 add_divide_fusion
  66.3 1.6 %copy-done.11 = bf16[2,1024,1024]{2,1,0:T(8,128)(2,1)S(1)} copy-done((bf16[2,1024,1024]{2,1,0:T(8,128)(2,1)S(1)}, bf16[2,1024,1024]{2,1,0:T(8,128)(2,1)}, u32[]{:S(2)}) %copy-start.11) | copy-done | bytes 4194328
  67.8 0.0 copy-start.14
  67.8 0.7 fusion.10
  68.6 0.0 copy-done.16
  68.6 0.9 fusion.66
  69.5 0.6 copy-done.14
  70.1 0.7 fusion
  70.8 1.0 select_reduce_fusion.3
  71.9 0.8 pad_maximum_fusion.2.refs_0_
  72.7 0.7 fusion.8
  73.4 1.0 select_reduce_fusion.1
  74.4 0.8 pad_maximum_fusion.3.refs_1_
  75.2 34.2 %shard_map.177 = (f32[64,2048]{1,0:T(8,128)}, f32[64,2048]{1,0:T(8,128)}) custom-call(f32[64,2048]{1,0:T(8,128)} %pad_maximum_fusion.2.refs_0_, f32[64,2048]{1,0:T(8,128)} %pad_maximum_fusion.3.refs_1_), custom_call_target="tpu_custom_call" | custom-call | tf_op jit(solution)/shard_map/pallas_call | solution.py:175
  109.5 2.4 %fusion.78 = f32[64,2048]{1,0:T(8,128)} fusion(f32[64,2048]{1,0:T(8,128)S(1)} %copy-done.3, f32[64,2048]{1,0:T(8,128)S(1)} %copy-done.4, f32[64,2048]{1,0:T(8,128)} %get-tuple-element.9, f32[2048]{0:T(1024)S(1)} %bitcast.107, f32[64,2048]{1,0:T(8,128)S(1)} %copy-done.2, f32[64,2048]{1,0:T(8,128)S(1)} %copy-done.5, f32[72,2048]{1,0:T(8,128)} %get-tuple-element.7), kind=kLoop, calls=%fused_computation.71 | loop fusion | flops 2490368 | bytes 3678208 | tf_op jit(solution)/shard_map/jit(clip)/min | solution.py:292
  111.9 2.7 %fusion.76 = f32[64,2048]{1,0:T(8,128)} fusion(f32[64,2048]{1,0:T(8,128)S(1)} %copy-done.6, f32[64,2048]{1,0:T(8,128)} %param.25, f32[64,2048]{1,0:T(8,128)} %get-tuple-element.8, f32[2048]{0:T(1024)S(1)} %bitcast.105, f32[64,2048]{1,0:T(8,128)} %param.24, f32[64,2048]{1,0:T(8,128)S(1)} %copy-done, f32[72,2048]{1,0:T(8,128)} %get-tuple-element.6), kind=kLoop, calls=%fused_computation.69 | loop fusion | flops 2621440 | bytes 3678208 | tf_op jit(solution)/shard_map/jit(clip)/min | solution.py:291
  (2 shorter events, 0.1 us)
Async XLA Ops:
  0.6 9.2 %copy-start.10 = (bf16[2,1024,1024]{2,1,0:T(8,128)(2,1)S(1)}, bf16[2,1024,1024]{2,1,0:T(8,128)(2,1)}, u32[]{:S(2)}) copy-start(bf16[2,1024,1024]{2,1,0:T(8,128)(2,1)} %param.17) | copy-start | bytes 12582916
  0.6 9.2 %copy-start.1 = (f32[1,1,4,64,1024]{4,3,2,1,0:T(8,128)S(1)}, f32[1,1,4,64,1024]{4,3,2,1,0:T(8,128)}, u32[]{:S(2)}) copy-start(f32[1,1,4,64,1024]{4,3,2,1,0:T(8,128)} %param.33) | copy-start | bytes 3145732
  7.3 3.5 %copy-start.13 = (bf16[2,1024,1024]{2,1,0:T(8,128)(2,1)S(1)}, bf16[2,1024,1024]{2,1,0:T(8,128)(2,1)}, u32[]{:S(2)}) copy-start(bf16[2,1024,1024]{2,1,0:T(8,128)(2,1)} %param.18) | copy-start | bytes 12582916
  13.4 1.6 %copy-start.15 = (f32[1,1,4,64,1024]{4,3,2,1,0:T(8,128)S(1)}, f32[1,1,4,64,1024]{4,3,2,1,0:T(8,128)}, u32[]{:S(2)}) copy-start(f32[1,1,4,64,1024]{4,3,2,1,0:T(8,128)} %param.32) | copy-start | bytes 3145732
  15.0 49.4 %copy-start.2 = (f32[64,2048]{1,0:T(8,128)S(1)}, f32[64,2048]{1,0:T(8,128)}, u32[]{:S(2)}) copy-start(f32[64,2048]{1,0:T(8,128)} %param.28) | copy-start | bytes 1572868
  15.0 49.4 %copy-start.3 = (f32[64,2048]{1,0:T(8,128)S(1)}, f32[64,2048]{1,0:T(8,128)}, u32[]{:S(2)}) copy-start(f32[64,2048]{1,0:T(8,128)} %param.30) | copy-start | bytes 1572868
  15.0 49.4 %copy-start.4 = (f32[64,2048]{1,0:T(8,128)S(1)}, f32[64,2048]{1,0:T(8,128)}, u32[]{:S(2)}) copy-start(f32[64,2048]{1,0:T(8,128)} %param.29) | copy-start | bytes 1572868
  15.0 49.4 %copy-start.5 = (f32[64,2048]{1,0:T(8,128)S(1)}, f32[64,2048]{1,0:T(8,128)}, u32[]{:S(2)}) copy-start(f32[64,2048]{1,0:T(8,128)} %param.27) | copy-start | bytes 1572868
  16.9 49.0 %copy-start = (f32[64,2048]{1,0:T(8,128)S(1)}, f32[64,2048]{1,0:T(8,128)}, u32[]{:S(2)}) copy-start(f32[64,2048]{1,0:T(8,128)} %param.23) | copy-start | bytes 1572868
  16.9 49.0 %copy-start.6 = (f32[64,2048]{1,0:T(8,128)S(1)}, f32[64,2048]{1,0:T(8,128)}, u32[]{:S(2)}) copy-start(f32[64,2048]{1,0:T(8,128)} %param.26) | copy-start | bytes 1572868
  62.5 3.2 %copy-start.12 = (f32[4,64,1024]{2,1,0:T(8,128)S(1)}, f32[4,64,1024]{2,1,0:T(8,128)}, u32[]{:S(2)}) copy-start(f32[4,64,1024]{2,1,0:T(8,128)} %get-tuple-element.32) | copy-start | bytes 3145732
  62.5 3.5 %copy-start.7 = (f32[64,2048]{1,0:T(8,128)S(1)}, f32[64,2048]{1,0:T(8,128)}, u32[]{:S(2)}) copy-start(f32[64,2048]{1,0:T(8,128)} %param.25) | copy-start | bytes 1572868
  62.5 3.5 %copy-start.8 = (f32[64,2048]{1,0:T(8,128)S(1)}, f32[64,2048]{1,0:T(8,128)}, u32[]{:S(2)}) copy-start(f32[64,2048]{1,0:T(8,128)} %param.24) | copy-start | bytes 1572868
  62.5 3.5 %copy-start.9 = (f32[72,2048]{1,0:T(8,128)S(1)}, f32[72,2048]{1,0:T(8,128)}, u32[]{:S(2)}) copy-start(f32[72,2048]{1,0:T(8,128)} %get-tuple-element.6) | copy-start | bytes 1769476
  65.6 2.2 %copy-start.11 = (bf16[2,1024,1024]{2,1,0:T(8,128)(2,1)S(1)}, bf16[2,1024,1024]{2,1,0:T(8,128)(2,1)}, u32[]{:S(2)}) copy-start(bf16[2,1024,1024]{2,1,0:T(8,128)(2,1)} %param.17) | copy-start | bytes 12582916
  66.0 2.6 %copy-start.16 = (f32[4,64,1024]{2,1,0:T(8,128)S(1)}, f32[4,64,1024]{2,1,0:T(8,128)}, u32[]{:S(2)}) copy-start(f32[4,64,1024]{2,1,0:T(8,128)} %get-tuple-element.18) | copy-start | bytes 3145732
  67.8 2.3 %copy-start.14 = (bf16[2,1024,1024]{2,1,0:T(8,128)(2,1)S(1)}, bf16[2,1024,1024]{2,1,0:T(8,128)(2,1)}, u32[]{:S(2)}) copy-start(bf16[2,1024,1024]{2,1,0:T(8,128)(2,1)} %param.18) | copy-start | bytes 12582916

commit v14 on v11

--- a/solution.py
+++ b/solution.py
@@ -21,7 +21,7 @@
 def reduce_kernel(n, group_axes, block_width, with_counts, *refs):
     groups = len(group_axes)
     if with_counts:
-        info, refs = refs[0], refs[1:]
+        info, live_ref, refs = refs[:groups], refs[groups], refs[groups + 1 :]
     ins = refs[:groups]
     outs = refs[groups : 2 * groups]
     scratch = refs[2 * groups :]
@@ -39,8 +39,8 @@
         return ref.at[:, cols(index)]
 
     if with_counts:
-        slots = (info.shape[0] - 1) // groups
-        live = info[groups * slots]
+        slots = info[0].shape[0]
+        live = live_ref[0]
         for g in range(groups):
             send = scratch[size * g + 6]
             data_rows = ins[g].shape[0]
@@ -50,7 +50,7 @@
                 count = jnp.int32(0)
                 for k in range(slots):
                     count = count + jnp.where(
-                        (k < live) & (info[g * slots + k] == block), 1, 0
+                        (k < live) & (info[g][k] == block), 1, 0
                     ).astype(jnp.int32)
                 send[p, :data_rows, :] = ins[g][:, p * width : (p + 1) * width]
                 send[p, data_rows:, :] = jnp.full((extra, width), count, jnp.int32).astype(
@@ -157,8 +157,8 @@
             scratch.append(pltpu.VMEM((n, rows, width), jnp.float32))
     in_specs = [pl.BlockSpec(memory_space=pltpu.VMEM)] * len(arrays)
     if info is not None:
-        in_specs = [pl.BlockSpec(memory_space=pltpu.SMEM)] + in_specs
-        arrays = [info] + arrays
+        in_specs = [pl.BlockSpec(memory_space=pltpu.SMEM)] * len(info) + in_specs
+        arrays = list(info) + arrays
     return pl.pallas_call(
         functools.partial(reduce_kernel, n, group_axes, block_width, info is not None),
         out_shape=tuple(jax.ShapeDtypeStruct(s, jnp.float32) for s in shapes),
@@ -256,7 +256,7 @@
             [jnp.sum(jnp.where(m, y_terms, 0.0), axis=0) for m in row_mask], axis=1
         )
         if iteration == 0:
-            slot_info = jnp.concatenate([cols_here, rows_here, block_count[0, 0][None]])
+            slot_info = [cols_here, rows_here, block_count.reshape(1)]
             col_total, row_total = all_reduce(
                 [col_terms, row_terms], AXES, n_row, 0, block_width, slot_info
             )

time: 115 us -> 114 us (level)
  other arithmetic: 16.7 us -> 15.4 us
    concatenate x1 -> x0, other arithmetic: 1.32 us -> none  [per_device(): slot_info = jnp.concatenate([cols_here, rows_here, block_count[0, 0][None]])]
where the time goes in v14:
time: 114 us; the launch traced here: 113 us
  Pallas kernels  78.9 us (69%)
  other arithmetic  15.4 us (14%)
  matrix products  13.8 us (12%)
  local copies, waits for them, and re-layouts  3.39 us (3%)
  between operations  1.78 us (2%)
    pallas_call x2, Pallas kernels, all_reduce(): pl.pallas_call(functools.partial(reduce_kernel, n, group_axes, block_widt...  78.9 us
    dot_general x12, matrix products, by_tile(): lax.dot_general(stacked, matrices[t], (((1,), (contract,)), ((), ())), pr...  13.8 us
    min x1, other arithmetic, per_device(): column_final = jnp.clip(x_own - x_dual - unit_cost, 0.0, capacity)  2.73 us
    min x1, other arithmetic, per_device(): row_final = jnp.clip(y_state - y_dual, row_lower, row_upper)  2.41 us

profile of v14, /device:TPU:1, one launch (start us, length us, event | category | flops | bytes accessed | tf_op | source)
XLA Modules:
  0.0 113.2 jit_solution(12128825714989292365)
XLA Ops:
  0.6 0.0 copy-start.10
  0.6 0.0 copy-start.1
  1.4 1.1 compare_bitcast_fusion
  2.5 0.7 fusion.85
  3.2 1.7 %fusion.79 = bf16[4,64,1024]{2,1,0:T(8,128)(2,1)S(1)} fusion(f32[1,1,4,64,1024]{4,3,2,1,0:T(8,128)} %param.31, f32[1,1,4,64,1024]{4,3,2,1,0:T(8,128)} %param.32), kind=kLoop, calls=%fused_computation.72 | loop fusion | flops 524288 | bytes 2621440 | tf_op jit(solution)/shard_map/convert_element_type | solution.py:241
  4.9 1.1 fusion.88
  6.0 0.0 copy-start.13
  6.0 2.5 %fusion.14 = f32[4,64,1024]{2,1,0:T(8,128)S(1)} fusion(bf16[4,64,1024]{2,1,0:T(8,128)(2,1)S(1)} %fusion.79, bf16[2,1024,1024]{2,1,0:T(8,128)(2,1)} %param.17), kind=kOutput, calls=%fused_computation.14 | convolution fusion | flops 536870912 | bytes 3670016 | tf_op jit(solution)/shard_map/dot_general | solution.py:183
  8.5 0.0 copy-done.10
  8.5 0.0 copy-done.1
  8.5 0.9 fusion.69
  9.4 0.0 copy-done.13
  9.4 0.7 fusion.2
  10.2 1.9 %select_reduce_fusion.7 = (f32[64,1024]{1,0:T(8,128)S(1)}, f32[64,1024]{1,0:T(8,128)S(1)}, f32[4,64,1024]{2,1,0:T(8,128)}, bf16[4,64,1024]{2,1,0:T(8,128)(2,1)S(1)}) fusion(pred[4]{0:T(512)(128)(4,1)S(1)} %get-tuple-element.30, pred[4]{0:T(512)(128)(4,1)S(1)} %get-tuple-element.28, f32[1,1,4,64,1024]{4,3,2,1,0:T(8,128)S(1)} %copy-done.1, ...), kind=kOutput, calls=%fused_computation.62 | convolution fusion | flops 538574848 | bytes 6817280 | tf_op jit(solution)/shard_map/dot_general | solution.py:183
  12.1 0.0 copy-start.15
  12.1 0.8 pad_maximum_fusion.refs_3_
  12.9 0.7 fusion.12
  13.6 0.0 copy-done.15
  13.6 0.0 copy-start.2
  13.7 0.0 copy-start.3
  13.7 0.0 copy-start.4
  13.7 0.0 copy-start.5
  13.7 1.9 %select_reduce_fusion.5 = (f32[64,1024]{1,0:T(8,128)S(1)}, f32[64,1024]{1,0:T(8,128)S(1)}, f32[4,64,1024]{2,1,0:T(8,128)}) fusion(pred[4]{0:T(512)(128)(4,1)S(1)} %get-tuple-element.34, pred[4]{0:T(512)(128)(4,1)S(1)} %get-tuple-element.35, f32[1,1,4,64,1024]{4,3,2,1,0:T(8,128)S(1)} %copy-done.15, f32[4,64,1024]{2,1,0:T(8,128)S(1)} %fusion.12, ...), kind=kOutput, calls=%fused_computation.60 | convolution fusion | flops 538312704 | bytes 6292992 | tf_op jit(solution)/shard_map/dot_general | solution.py:183
  15.6 0.0 copy-start
  15.6 0.0 copy-start.6
  15.6 0.8 pad_maximum_fusion.1.refs_4_
  16.5 42.0 %shard_map.176 = (f32[72,2048]{1,0:T(8,128)}, f32[72,2048]{1,0:T(8,128)}) custom-call(s32[4]{0:T(128)} %bitcast.108, s32[4]{0:T(128)} %bitcast.109, s32[1]{0:T(128)} %bitcast.102.refs_2_, f32[64,2048]{1,0:T(8,128)} %pad_maximum_fusion.refs_3_, f32[64,2048]{1,0:T(8,128)} %pad_maximum_fusion.1.refs_4_), custom_call_target="tpu_custom_call" | custom-call | tf_op jit(solution)/shard_map/pallas_call | solution.py:162
  58.5 0.0 copy-start.12
  58.5 0.0 copy-start.7
  58.5 0.0 copy-start.8
  58.5 0.0 copy-start.9
  58.5 1.0 slice_add_fusion.1
  59.5 0.8 slice_add_fusion
  60.4 0.0 copy-done.2
  60.4 0.0 copy-done.3
  60.4 0.0 copy-done.4
  60.4 0.0 copy-done.5
  60.4 1.2 %subtract_divide_fusion = f32[64,2048]{1,0:T(8,128)S(1)} fusion(f32[72,2048]{1,0:T(8,128)} %get-tuple-element.7, f32[2048]{0:T(1024)S(1)} %bitcast.106, f32[64,2048]{1,0:T(8,128)S(1)} %copy-done.2, f32[64,2048]{1,0:T(8,128)S(1)} %copy-done.3, f32[64,2048]{1,0:T(8,128)S(1)} %copy-done.4, f32[64,2048]{1,0:T(8,128)S(1)} %copy-done.5), kind=kLoop, calls=%fused_computation.77 | loop fusion | flops 786432 | bytes 3153920 | tf_op jit(solution)/shard_map/div | solution.py:271
  61.6 0.0 copy-start.11
  61.7 0.0 copy-done.12
  61.7 0.2 subtract_convert_fusion
  61.9 0.0 copy-done
  62.0 0.0 copy-done.6
  62.0 0.0 copy-done.7
  62.0 0.0 copy-done.8
  62.0 0.0 copy-done.9
  62.0 0.0 copy-start.16
  62.0 0.2 add_divide_fusion
  62.3 1.6 %copy-done.11 = bf16[2,1024,1024]{2,1,0:T(8,128)(2,1)S(1)} copy-done((bf16[2,1024,1024]{2,1,0:T(8,128)(2,1)S(1)}, bf16[2,1024,1024]{2,1,0:T(8,128)(2,1)}, u32[]{:S(2)}) %copy-start.11) | copy-done | bytes 4194328
  63.8 0.0 copy-start.14
  63.8 0.7 fusion.10
  64.6 0.0 copy-done.16
  64.6 0.9 fusion.66
  65.5 0.6 copy-done.14
  66.1 0.7 fusion
  66.8 1.0 select_reduce_fusion.3
  67.8 0.8 pad_maximum_fusion.2.refs_0_
  68.7 0.7 fusion.8
  69.4 1.0 select_reduce_fusion.1
  70.4 0.8 pad_maximum_fusion.3.refs_1_
  71.2 36.9 %shard_map.177 = (f32[64,2048]{1,0:T(8,128)}, f32[64,2048]{1,0:T(8,128)}) custom-call(f32[64,2048]{1,0:T(8,128)} %pad_maximum_fusion.2.refs_0_, f32[64,2048]{1,0:T(8,128)} %pad_maximum_fusion.3.refs_1_), custom_call_target="tpu_custom_call" | custom-call | tf_op jit(solution)/shard_map/pallas_call | solution.py:162
  108.1 2.4 %fusion.78 = f32[64,2048]{1,0:T(8,128)} fusion(f32[64,2048]{1,0:T(8,128)S(1)} %copy-done.3, f32[64,2048]{1,0:T(8,128)S(1)} %copy-done.4, f32[64,2048]{1,0:T(8,128)} %get-tuple-element.9, f32[2048]{0:T(1024)S(1)} %bitcast.107, f32[64,2048]{1,0:T(8,128)S(1)} %copy-done.2, f32[64,2048]{1,0:T(8,128)S(1)} %copy-done.5, f32[72,2048]{1,0:T(8,128)} %get-tuple-element.7), kind=kLoop, calls=%fused_computation.71 | loop fusion | flops 2490368 | bytes 3678208 | tf_op jit(solution)/shard_map/jit(clip)/min | solution.py:279
  110.5 2.7 %fusion.76 = f32[64,2048]{1,0:T(8,128)} fusion(f32[64,2048]{1,0:T(8,128)S(1)} %copy-done.6, f32[64,2048]{1,0:T(8,128)} %param.25, f32[64,2048]{1,0:T(8,128)} %get-tuple-element.8, f32[2048]{0:T(1024)S(1)} %bitcast.105, f32[64,2048]{1,0:T(8,128)} %param.24, f32[64,2048]{1,0:T(8,128)S(1)} %copy-done, f32[72,2048]{1,0:T(8,128)} %get-tuple-element.6), kind=kLoop, calls=%fused_computation.69 | loop fusion | flops 2621440 | bytes 3678208 | tf_op jit(solution)/shard_map/jit(clip)/min | solution.py:278
  (2 shorter events, 0.1 us)
Async XLA Ops:
  0.6 7.8 %copy-start.10 = (bf16[2,1024,1024]{2,1,0:T(8,128)(2,1)S(1)}, bf16[2,1024,1024]{2,1,0:T(8,128)(2,1)}, u32[]{:S(2)}) copy-start(bf16[2,1024,1024]{2,1,0:T(8,128)(2,1)} %param.17) | copy-start | bytes 12582916
  0.6 7.8 %copy-start.1 = (f32[1,1,4,64,1024]{4,3,2,1,0:T(8,128)S(1)}, f32[1,1,4,64,1024]{4,3,2,1,0:T(8,128)}, u32[]{:S(2)}) copy-start(f32[1,1,4,64,1024]{4,3,2,1,0:T(8,128)} %param.33) | copy-start | bytes 3145732
  6.0 3.5 %copy-start.13 = (bf16[2,1024,1024]{2,1,0:T(8,128)(2,1)S(1)}, bf16[2,1024,1024]{2,1,0:T(8,128)(2,1)}, u32[]{:S(2)}) copy-start(bf16[2,1024,1024]{2,1,0:T(8,128)(2,1)} %param.18) | copy-start | bytes 12582916
  12.1 1.6 %copy-start.15 = (f32[1,1,4,64,1024]{4,3,2,1,0:T(8,128)S(1)}, f32[1,1,4,64,1024]{4,3,2,1,0:T(8,128)}, u32[]{:S(2)}) copy-start(f32[1,1,4,64,1024]{4,3,2,1,0:T(8,128)} %param.32) | copy-start | bytes 3145732
  13.6 46.7 %copy-start.2 = (f32[64,2048]{1,0:T(8,128)S(1)}, f32[64,2048]{1,0:T(8,128)}, u32[]{:S(2)}) copy-start(f32[64,2048]{1,0:T(8,128)} %param.28) | copy-start | bytes 1572868
  13.7 46.7 %copy-start.3 = (f32[64,2048]{1,0:T(8,128)S(1)}, f32[64,2048]{1,0:T(8,128)}, u32[]{:S(2)}) copy-start(f32[64,2048]{1,0:T(8,128)} %param.30) | copy-start | bytes 1572868
  13.7 46.7 %copy-start.4 = (f32[64,2048]{1,0:T(8,128)S(1)}, f32[64,2048]{1,0:T(8,128)}, u32[]{:S(2)}) copy-start(f32[64,2048]{1,0:T(8,128)} %param.29) | copy-start | bytes 1572868
  13.7 46.7 %copy-start.5 = (f32[64,2048]{1,0:T(8,128)S(1)}, f32[64,2048]{1,0:T(8,128)}, u32[]{:S(2)}) copy-start(f32[64,2048]{1,0:T(8,128)} %param.27) | copy-start | bytes 1572868
  15.6 46.3 %copy-start = (f32[64,2048]{1,0:T(8,128)S(1)}, f32[64,2048]{1,0:T(8,128)}, u32[]{:S(2)}) copy-start(f32[64,2048]{1,0:T(8,128)} %param.23) | copy-start | bytes 1572868
  15.6 46.3 %copy-start.6 = (f32[64,2048]{1,0:T(8,128)S(1)}, f32[64,2048]{1,0:T(8,128)}, u32[]{:S(2)}) copy-start(f32[64,2048]{1,0:T(8,128)} %param.26) | copy-start | bytes 1572868
  58.5 3.2 %copy-start.12 = (f32[4,64,1024]{2,1,0:T(8,128)S(1)}, f32[4,64,1024]{2,1,0:T(8,128)}, u32[]{:S(2)}) copy-start(f32[4,64,1024]{2,1,0:T(8,128)} %get-tuple-element.32) | copy-start | bytes 3145732
  58.5 3.5 %copy-start.7 = (f32[64,2048]{1,0:T(8,128)S(1)}, f32[64,2048]{1,0:T(8,128)}, u32[]{:S(2)}) copy-start(f32[64,2048]{1,0:T(8,128)} %param.25) | copy-start | bytes 1572868
  58.5 3.5 %copy-start.8 = (f32[64,2048]{1,0:T(8,128)S(1)}, f32[64,2048]{1,0:T(8,128)}, u32[]{:S(2)}) copy-start(f32[64,2048]{1,0:T(8,128)} %param.24) | copy-start | bytes 1572868
  58.5 3.5 %copy-start.9 = (f32[72,2048]{1,0:T(8,128)S(1)}, f32[72,2048]{1,0:T(8,128)}, u32[]{:S(2)}) copy-start(f32[72,2048]{1,0:T(8,128)} %get-tuple-element.6) | copy-start | bytes 1769476
  61.6 2.2 %copy-start.11 = (bf16[2,1024,1024]{2,1,0:T(8,128)(2,1)S(1)}, bf16[2,1024,1024]{2,1,0:T(8,128)(2,1)}, u32[]{:S(2)}) copy-start(bf16[2,1024,1024]{2,1,0:T(8,128)(2,1)} %param.17) | copy-start | bytes 12582916
  62.0 2.6 %copy-start.16 = (f32[4,64,1024]{2,1,0:T(8,128)S(1)}, f32[4,64,1024]{2,1,0:T(8,128)}, u32[]{:S(2)}) copy-start(f32[4,64,1024]{2,1,0:T(8,128)} %get-tuple-element.18) | copy-start | bytes 3145732
  63.8 2.3 %copy-start.14 = (bf16[2,1024,1024]{2,1,0:T(8,128)(2,1)S(1)}, bf16[2,1024,1024]{2,1,0:T(8,128)(2,1)}, u32[]{:S(2)}) copy-start(bf16[2,1024,1024]{2,1,0:T(8,128)(2,1)} %param.18) | copy-start | bytes 12582916

commit v15 on v14

--- a/solution.py
+++ b/solution.py
@@ -165,7 +165,9 @@
         in_specs=in_specs,
         out_specs=tuple(pl.BlockSpec(memory_space=pltpu.VMEM) for _ in shapes),
         scratch_shapes=scratch,
-        compiler_params=pltpu.CompilerParams(collective_id=collective_id, has_side_effects=True),
+        compiler_params=pltpu.CompilerParams(
+            collective_id=collective_id, has_side_effects=True, vmem_limit_bytes=16 * 1024 * 1024
+        ),
     )(*arrays)
 
 

time: 114 us -> 97.7 us (0.86)
  the two profiles are of different devices: /device:TPU:1 before, /device:TPU:65 now
where the time goes in v15:
time: 97.7 us; the launch traced here: 97.5 us
  Pallas kernels  75.8 us (78%)
  matrix products  11.7 us (12%)
  other arithmetic  6.58 us (7%)
  between operations  1.81 us (2%)
  local copies, waits for them, and re-layouts  1.67 us (2%)
    pallas_call x2, Pallas kernels, all_reduce(): pl.pallas_call(functools.partial(reduce_kernel, n, group_axes, block_widt...  75.8 us
    dot_general x12, matrix products, by_tile(): lax.dot_general(stacked, matrices[t], (((1,), (contract,)), ((), ())), pr...  11.7 us

profile of v15, /device:TPU:65, one launch (start us, length us, event | category | flops | bytes accessed | tf_op | source)
XLA Modules:
  0.0 97.5 jit_solution(2634961611330701330)
XLA Ops:
  0.6 0.0 copy-start.11
  0.6 0.0 copy-start.3
  1.4 1.1 %compare_bitcast_fusion = pred[4]{0:T(512)(128)(4,1)S(1)} fusion(s32[1,1,4]{2,1,0:T(1,128)} %param.21), kind=kLoop, calls=%fused_computation.88 | loop fusion | flops 4 | bytes 20 | tf_op jit(solution)/shard_map/eq | solution.py:194
  2.5 0.7 fusion.85
  3.2 1.7 %fusion.79 = bf16[4,64,1024]{2,1,0:T(8,128)(2,1)S(1)} fusion(f32[1,1,4,64,1024]{4,3,2,1,0:T(8,128)} %param.31, f32[1,1,4,64,1024]{4,3,2,1,0:T(8,128)} %param.32), kind=kLoop, calls=%fused_computation.72 | loop fusion | flops 524288 | bytes 2621440 | tf_op jit(solution)/shard_map/convert_element_type | solution.py:243
  4.9 1.1 %fusion.88 = (f32[64,1024]{1,0:T(8,128)S(1)}, f32[64,1024]{1,0:T(8,128)S(1)}) fusion(f32[64,2048]{1,0:T(8,128)} %param.23), kind=kLoop, calls=%fused_computation.97 | loop fusion | bytes 1048576 | tf_op jit(solution)/shard_map/slice | solution.py:178
  6.0 0.0 copy-start.12
  6.0 2.5 %fusion.14 = f32[4,64,1024]{2,1,0:T(8,128)S(1)} fusion(bf16[4,64,1024]{2,1,0:T(8,128)(2,1)S(1)} %fusion.79, bf16[2,1024,1024]{2,1,0:T(8,128)(2,1)} %param.17), kind=kOutput, calls=%fused_computation.14 | convolution fusion | flops 536870912 | bytes 3670016 | tf_op jit(solution)/shard_map/dot_general | solution.py:185
  8.5 0.0 copy-done.11
  8.5 0.0 copy-done.3
  8.5 0.9 fusion.69
  9.4 0.0 copy-done.12
  9.4 0.7 fusion.2
  10.2 0.9 select_reduce_fusion.7
  11.0 0.0 copy-start.13
  11.1 0.7 fusion.12
  11.8 0.5 copy-done.13
  12.3 0.0 copy-start
  12.3 0.0 copy-start.1
  12.3 0.0 copy-start.4
  12.3 0.0 copy-start.5
  12.3 0.0 copy-start.6
  12.3 0.0 copy-start.7
  12.3 0.9 select_reduce_fusion.5
  13.2 0.0 copy-start.2
  13.2 0.0 copy-start.8
  13.2 0.0 copy-start.9
  13.2 0.0 copy-start.10
  13.3 0.0 copy-done
  13.3 0.0 copy-done.1
  13.3 40.4 %shard_map.176 = (f32[72,2048]{1,0:T(8,128)S(1)}, f32[72,2048]{1,0:T(8,128)S(1)}) custom-call(s32[4]{0:T(128)S(1)} %bitcast.104, s32[4]{0:T(128)S(1)} %bitcast.105, s32[1]{0:T(128)} %bitcast.102.refs_2_, f32[64,2048]{1,0:T(8,128)S(1)} %pad_maximum_fusion.refs_3_, f32[64,2048]{1,0:T(8,128)S(1)} %pad_maximum_fusion.1.refs_4_), custom_call_target="tpu_custom_call" | custom-call | tf_op jit(solution)/shard_map/pallas_call | solution.py:162
  53.7 0.0 copy-done.4
  53.7 0.0 copy-done.5
  53.8 0.0 copy-done.6
  53.8 0.0 copy-done.7
  53.8 0.2 subtract_divide_fusion
  54.0 0.2 subtract_convert_fusion
  54.2 0.0 copy-done.2
  54.2 0.0 copy-done.8
  54.3 0.0 copy-done.9
  54.3 0.0 copy-done.10
  54.3 0.2 add_divide_fusion
  54.5 0.7 fusion.10
  55.2 0.9 fusion.66
  56.2 0.7 fusion
  56.9 1.0 %select_reduce_fusion.3 = (f32[64,1024]{1,0:T(8,128)S(1)}, f32[64,1024]{1,0:T(8,128)S(1)}, bf16[4,64,1024]{2,1,0:T(8,128)(2,1)S(1)}) fusion(pred[4]{0:T(512)(128)(4,1)S(1)} %get-tuple-element.30, f32[4,64,1024]{2,1,0:T(8,128)S(1)} %get-tuple-element.18, f32[64,1024]{1,0:T(8,128)S(1)} %get-tuple-element.20, f32[64,1024]{1,0:T(8,128)S(1)} %get-tuple-element.19, ...), kind=kOutput, calls=%fused_computation.55 | convolution fusion | flops 539099136 | bytes 6293504 | tf_op jit(solution)/shard_map/dot_general | solution.py:185
  58.0 0.7 fusion.8
  58.7 1.0 select_reduce_fusion.1
  59.7 35.4 %shard_map.177 = (f32[64,2048]{1,0:T(8,128)S(1)}, f32[64,2048]{1,0:T(8,128)S(1)}) custom-call(f32[64,2048]{1,0:T(8,128)S(1)} %pad_maximum_fusion.2.refs_0_, f32[64,2048]{1,0:T(8,128)S(1)} %pad_maximum_fusion.3.refs_1_), custom_call_target="tpu_custom_call" | custom-call | tf_op jit(solution)/shard_map/pallas_call | solution.py:162
  95.1 1.2 %fusion.78 = f32[64,2048]{1,0:T(8,128)} fusion(f32[64,2048]{1,0:T(8,128)S(1)} %copy-done.5, f32[64,2048]{1,0:T(8,128)S(1)} %copy-done.6, f32[64,2048]{1,0:T(8,128)S(1)} %get-tuple-element.9, f32[2048]{0:T(1024)S(1)} %bitcast.109, f32[64,2048]{1,0:T(8,128)S(1)} %copy-done.4, f32[64,2048]{1,0:T(8,128)S(1)} %copy-done.7, f32[72,2048]{1,0:T(8,128)S(1)} %get-tuple-element.7), kind=kLoop, calls=%fused_computation.71 | loop fusion | flops 2490368 | bytes 3678208 | tf_op jit(solution)/shard_map/jit(clip)/min | solution.py:281
  96.3 1.2 %fusion.76 = f32[64,2048]{1,0:T(8,128)} fusion(f32[64,2048]{1,0:T(8,128)S(1)} %copy-done.8, f32[64,2048]{1,0:T(8,128)S(1)} %copy-done.9, f32[64,2048]{1,0:T(8,128)S(1)} %get-tuple-element.8, f32[2048]{0:T(1024)S(1)} %bitcast.107, f32[64,2048]{1,0:T(8,128)S(1)} %copy-done.10, f32[64,2048]{1,0:T(8,128)S(1)} %copy-done.2, f32[72,2048]{1,0:T(8,128)S(1)} %get-tuple-element.6), kind=kLoop, calls=%fused_computation.69 | loop fusion | flops 2621440 | bytes 3678208 | tf_op jit(solution)/shard_map/jit(clip)/min | solution.py:280
  (8 shorter events, 0.2 us)
Async XLA Ops:
  0.6 7.8 %copy-start.11 = (bf16[2,1024,1024]{2,1,0:T(8,128)(2,1)S(1)}, bf16[2,1024,1024]{2,1,0:T(8,128)(2,1)}, u32[]{:S(2)}) copy-start(bf16[2,1024,1024]{2,1,0:T(8,128)(2,1)} %param.17) | copy-start | bytes 12582916
  0.6 7.8 %copy-start.3 = (f32[1,1,4,64,1024]{4,3,2,1,0:T(8,128)S(1)}, f32[1,1,4,64,1024]{4,3,2,1,0:T(8,128)}, u32[]{:S(2)}) copy-start(f32[1,1,4,64,1024]{4,3,2,1,0:T(8,128)} %param.33) | copy-start | bytes 3145732
  6.0 3.5 %copy-start.12 = (bf16[2,1024,1024]{2,1,0:T(8,128)(2,1)S(1)}, bf16[2,1024,1024]{2,1,0:T(8,128)(2,1)}, u32[]{:S(2)}) copy-start(bf16[2,1024,1024]{2,1,0:T(8,128)(2,1)} %param.18) | copy-start | bytes 12582916
  11.0 1.2 %copy-start.13 = (f32[1,1,4,64,1024]{4,3,2,1,0:T(8,128)S(1)}, f32[1,1,4,64,1024]{4,3,2,1,0:T(8,128)}, u32[]{:S(2)}) copy-start(f32[1,1,4,64,1024]{4,3,2,1,0:T(8,128)} %param.32) | copy-start | bytes 3145732
  12.3 1.0 %copy-start = (s32[1,1,4]{2,1,0:T(1,128)S(1)}, s32[1,1,4]{2,1,0:T(1,128)}, u32[]{:S(2)}) copy-start(s32[1,1,4]{2,1,0:T(1,128)} %param.20) | copy-start | bytes 52
  12.3 1.0 %copy-start.1 = (s32[1,1,4]{2,1,0:T(1,128)S(1)}, s32[1,1,4]{2,1,0:T(1,128)}, u32[]{:S(2)}) copy-start(s32[1,1,4]{2,1,0:T(1,128)} %param.19) | copy-start | bytes 52
  12.3 41.5 %copy-start.4 = (f32[64,2048]{1,0:T(8,128)S(1)}, f32[64,2048]{1,0:T(8,128)}, u32[]{:S(2)}) copy-start(f32[64,2048]{1,0:T(8,128)} %param.28) | copy-start | bytes 1572868
  12.3 41.5 %copy-start.5 = (f32[64,2048]{1,0:T(8,128)S(1)}, f32[64,2048]{1,0:T(8,128)}, u32[]{:S(2)}) copy-start(f32[64,2048]{1,0:T(8,128)} %param.30) | copy-start | bytes 1572868
  12.3 41.5 %copy-start.6 = (f32[64,2048]{1,0:T(8,128)S(1)}, f32[64,2048]{1,0:T(8,128)}, u32[]{:S(2)}) copy-start(f32[64,2048]{1,0:T(8,128)} %param.29) | copy-start | bytes 1572868
  12.3 41.5 %copy-start.7 = (f32[64,2048]{1,0:T(8,128)S(1)}, f32[64,2048]{1,0:T(8,128)}, u32[]{:S(2)}) copy-start(f32[64,2048]{1,0:T(8,128)} %param.27) | copy-start | bytes 1572868
  13.2 41.1 %copy-start.2 = (f32[64,2048]{1,0:T(8,128)S(1)}, f32[64,2048]{1,0:T(8,128)}, u32[]{:S(2)}) copy-start(f32[64,2048]{1,0:T(8,128)} %param.23) | copy-start | bytes 1572868
  13.2 41.1 %copy-start.8 = (f32[64,2048]{1,0:T(8,128)S(1)}, f32[64,2048]{1,0:T(8,128)}, u32[]{:S(2)}) copy-start(f32[64,2048]{1,0:T(8,128)} %param.26) | copy-start | bytes 1572868
  13.2 41.1 %copy-start.9 = (f32[64,2048]{1,0:T(8,128)S(1)}, f32[64,2048]{1,0:T(8,128)}, u32[]{:S(2)}) copy-start(f32[64,2048]{1,0:T(8,128)} %param.25) | copy-start | bytes 1572868
  13.2 41.1 %copy-start.10 = (f32[64,2048]{1,0:T(8,128)S(1)}, f32[64,2048]{1,0:T(8,128)}, u32[]{:S(2)}) copy-start(f32[64,2048]{1,0:T(8,128)} %param.24) | copy-start | bytes 1572868

commit v16 on v15

--- a/solution.py
+++ b/solution.py
@@ -45,17 +45,20 @@
             send = scratch[size * g + 6]
             data_rows = ins[g].shape[0]
             extra = send.shape[1] - data_rows
-            for p in range(n):
-                block = (p * width) // block_width
+            counts = []
+            for b in range(extra):
                 count = jnp.int32(0)
                 for k in range(slots):
                     count = count + jnp.where(
-                        (k < live) & (info[g][k] == block), 1, 0
+                        (k < live) & (info[g][k] == b), 1, 0
                     ).astype(jnp.int32)
+                counts.append(count)
+            count_rows = jnp.concatenate(
+                [jnp.full((1, width), c, jnp.int32) for c in counts], axis=0
+            ).astype(jnp.float32)
+            for p in range(n):
                 send[p, :data_rows, :] = ins[g][:, p * width : (p + 1) * width]
-                send[p, data_rows:, :] = jnp.full((extra, width), count, jnp.int32).astype(
-                    jnp.float32
-                )
+                send[p, data_rows:, :] = count_rows
             sources[g] = send
     issue_order = sorted(range(groups), key=lambda g: group_axes[g] != "col")
     barrier = pltpu.get_barrier_semaphore()
@@ -104,13 +107,22 @@
         total = piece(sources[g], me)[...]
         for k in range(1, n):
             total = total + recv[lax.rem(me + k, n)]
-        outs[g][:, cols(me)] = total
+        if with_counts:
+            data_rows = ins[g].shape[0]
+            outs[g][:data_rows, cols(me)] = total[:data_rows]
+            blocks = outs[g].shape[1] // block_width
+            for b in range(blocks):
+                outs[g][data_rows : data_rows + 1, b * block_width : (b + 1) * block_width] = (
+                    jnp.tile(total[data_rows + b : data_rows + b + 1, :], (1, block_width // width))
+                )
+        else:
+            outs[g][:, cols(me)] = total
         copies = []
         for k in range(1, n):
             peer = lax.rem(me + k, n)
             copy = pltpu.make_async_remote_copy(
-                src_ref=outs[g].at[:, cols(me)],
-                dst_ref=outs[g].at[:, cols(me)],
+                src_ref=outs[g].at[pl.ds(0, ins[g].shape[0]), cols(me)],
+                dst_ref=outs[g].at[pl.ds(0, ins[g].shape[0]), cols(me)],
                 send_sem=s2.at[peer],
                 recv_sem=r2.at[me],
                 device_id=peer_id(axis, peer),
@@ -128,8 +140,8 @@
         for k in range(1, n):
             source = lax.rem(me + n - k, n)
             pltpu.make_async_remote_copy(
-                src_ref=outs[g].at[:, cols(source)],
-                dst_ref=outs[g].at[:, cols(source)],
+                src_ref=outs[g].at[pl.ds(0, ins[g].shape[0]), cols(source)],
+                dst_ref=outs[g].at[pl.ds(0, ins[g].shape[0]), cols(source)],
                 send_sem=s2.at[source],
                 recv_sem=r2.at[source],
                 device_id=peer_id(axis, source),

time: 97.7 us -> 96.5 us (0.988)
  the two profiles are of different devices: /device:TPU:65 before, /device:TPU:1 now
where the time goes in v16:
time: 96.5 us; the launch traced here: 96 us
  Pallas kernels  74.3 us (77%)
  matrix products  11.7 us (12%)
  other arithmetic  6.58 us (7%)
  between operations  1.81 us (2%)
  local copies, waits for them, and re-layouts  1.67 us (2%)
    pallas_call x2, Pallas kernels, all_reduce(): pl.pallas_call(functools.partial(reduce_kernel, n, group_axes, block_widt...  74.3 us
    dot_general x12, matrix products, by_tile(): lax.dot_general(stacked, matrices[t], (((1,), (contract,)), ((), ())), pr...  11.7 us

profile of v16, /device:TPU:1, one launch (start us, length us, event | category | flops | bytes accessed | tf_op | source)
XLA Modules:
  0.0 96.0 jit_solution(3913295697944584278)
XLA Ops:
  0.6 0.0 copy-start.11
  0.6 0.0 copy-start.3
  1.4 1.1 %compare_bitcast_fusion = pred[4]{0:T(512)(128)(4,1)S(1)} fusion(s32[1,1,4]{2,1,0:T(1,128)} %param.21), kind=kLoop, calls=%fused_computation.88 | loop fusion | flops 4 | bytes 20 | tf_op jit(solution)/shard_map/eq | solution.py:206
  2.5 0.7 fusion.85
  3.2 1.7 %fusion.79 = bf16[4,64,1024]{2,1,0:T(8,128)(2,1)S(1)} fusion(f32[1,1,4,64,1024]{4,3,2,1,0:T(8,128)} %param.31, f32[1,1,4,64,1024]{4,3,2,1,0:T(8,128)} %param.32), kind=kLoop, calls=%fused_computation.72 | loop fusion | flops 524288 | bytes 2621440 | tf_op jit(solution)/shard_map/convert_element_type | solution.py:255
  4.9 1.1 %fusion.88 = (f32[64,1024]{1,0:T(8,128)S(1)}, f32[64,1024]{1,0:T(8,128)S(1)}) fusion(f32[64,2048]{1,0:T(8,128)} %param.23), kind=kLoop, calls=%fused_computation.97 | loop fusion | bytes 1048576 | tf_op jit(solution)/shard_map/slice | solution.py:190
  6.0 0.0 copy-start.12
  6.0 2.5 %fusion.14 = f32[4,64,1024]{2,1,0:T(8,128)S(1)} fusion(bf16[4,64,1024]{2,1,0:T(8,128)(2,1)S(1)} %fusion.79, bf16[2,1024,1024]{2,1,0:T(8,128)(2,1)} %param.17), kind=kOutput, calls=%fused_computation.14 | convolution fusion | flops 536870912 | bytes 3670016 | tf_op jit(solution)/shard_map/dot_general | solution.py:197
  8.5 0.0 copy-done.11
  8.5 0.0 copy-done.3
  8.5 0.9 fusion.69
  9.4 0.0 copy-done.12
  9.4 0.7 fusion.2
  10.2 0.9 select_reduce_fusion.7
  11.1 0.0 copy-start.13
  11.1 0.7 fusion.12
  11.8 0.5 copy-done.13
  12.3 0.0 copy-start
  12.3 0.0 copy-start.1
  12.3 0.0 copy-start.4
  12.3 0.0 copy-start.5
  12.3 0.0 copy-start.6
  12.3 0.0 copy-start.7
  12.3 0.9 select_reduce_fusion.5
  13.2 0.0 copy-start.2
  13.2 0.0 copy-start.8
  13.2 0.0 copy-start.9
  13.2 0.0 copy-start.10
  13.3 0.0 copy-done
  13.3 0.0 copy-done.1
  13.3 39.5 %shard_map.176 = (f32[72,2048]{1,0:T(8,128)S(1)}, f32[72,2048]{1,0:T(8,128)S(1)}) custom-call(s32[4]{0:T(128)S(1)} %bitcast.104, s32[4]{0:T(128)S(1)} %bitcast.105, s32[1]{0:T(128)} %bitcast.102.refs_2_, f32[64,2048]{1,0:T(8,128)S(1)} %pad_maximum_fusion.refs_3_, f32[64,2048]{1,0:T(8,128)S(1)} %pad_maximum_fusion.1.refs_4_), custom_call_target="tpu_custom_call" | custom-call | tf_op jit(solution)/shard_map/pallas_call | solution.py:174
  52.9 0.0 copy-done.4
  52.9 0.0 copy-done.5
  52.9 0.0 copy-done.6
  52.9 0.0 copy-done.7
  52.9 0.2 subtract_divide_fusion
  53.1 0.2 subtract_convert_fusion
  53.4 0.0 copy-done.2
  53.4 0.0 copy-done.8
  53.4 0.0 copy-done.9
  53.4 0.0 copy-done.10
  53.4 0.2 add_divide_fusion
  53.6 0.7 fusion.10
  54.4 0.9 fusion.66
  55.3 0.7 fusion
  56.0 1.0 %select_reduce_fusion.3 = (f32[64,1024]{1,0:T(8,128)S(1)}, f32[64,1024]{1,0:T(8,128)S(1)}, bf16[4,64,1024]{2,1,0:T(8,128)(2,1)S(1)}) fusion(pred[4]{0:T(512)(128)(4,1)S(1)} %get-tuple-element.30, f32[4,64,1024]{2,1,0:T(8,128)S(1)} %get-tuple-element.18, f32[64,1024]{1,0:T(8,128)S(1)} %get-tuple-element.20, f32[64,1024]{1,0:T(8,128)S(1)} %get-tuple-element.19, ...), kind=kOutput, calls=%fused_computation.55 | convolution fusion | flops 539099136 | bytes 6293504 | tf_op jit(solution)/shard_map/dot_general | solution.py:197
  57.1 0.7 fusion.8
  57.8 1.0 select_reduce_fusion.1
  58.9 34.7 %shard_map.177 = (f32[64,2048]{1,0:T(8,128)S(1)}, f32[64,2048]{1,0:T(8,128)S(1)}) custom-call(f32[64,2048]{1,0:T(8,128)S(1)} %pad_maximum_fusion.2.refs_0_, f32[64,2048]{1,0:T(8,128)S(1)} %pad_maximum_fusion.3.refs_1_), custom_call_target="tpu_custom_call" | custom-call | tf_op jit(solution)/shard_map/pallas_call | solution.py:174
  93.6 1.2 %fusion.78 = f32[64,2048]{1,0:T(8,128)} fusion(f32[64,2048]{1,0:T(8,128)S(1)} %copy-done.5, f32[64,2048]{1,0:T(8,128)S(1)} %copy-done.6, f32[64,2048]{1,0:T(8,128)S(1)} %get-tuple-element.9, f32[2048]{0:T(1024)S(1)} %bitcast.109, f32[64,2048]{1,0:T(8,128)S(1)} %copy-done.4, f32[64,2048]{1,0:T(8,128)S(1)} %copy-done.7, f32[72,2048]{1,0:T(8,128)S(1)} %get-tuple-element.7), kind=kLoop, calls=%fused_computation.71 | loop fusion | flops 2490368 | bytes 3678208 | tf_op jit(solution)/shard_map/jit(clip)/min | solution.py:293
  94.8 1.2 %fusion.76 = f32[64,2048]{1,0:T(8,128)} fusion(f32[64,2048]{1,0:T(8,128)S(1)} %copy-done.8, f32[64,2048]{1,0:T(8,128)S(1)} %copy-done.9, f32[64,2048]{1,0:T(8,128)S(1)} %get-tuple-element.8, f32[2048]{0:T(1024)S(1)} %bitcast.107, f32[64,2048]{1,0:T(8,128)S(1)} %copy-done.10, f32[64,2048]{1,0:T(8,128)S(1)} %copy-done.2, f32[72,2048]{1,0:T(8,128)S(1)} %get-tuple-element.6), kind=kLoop, calls=%fused_computation.69 | loop fusion | flops 2621440 | bytes 3678208 | tf_op jit(solution)/shard_map/jit(clip)/min | solution.py:292
  (8 shorter events, 0.2 us)
Async XLA Ops:
  0.6 7.8 %copy-start.11 = (bf16[2,1024,1024]{2,1,0:T(8,128)(2,1)S(1)}, bf16[2,1024,1024]{2,1,0:T(8,128)(2,1)}, u32[]{:S(2)}) copy-start(bf16[2,1024,1024]{2,1,0:T(8,128)(2,1)} %param.17) | copy-start | bytes 12582916
  0.6 7.8 %copy-start.3 = (f32[1,1,4,64,1024]{4,3,2,1,0:T(8,128)S(1)}, f32[1,1,4,64,1024]{4,3,2,1,0:T(8,128)}, u32[]{:S(2)}) copy-start(f32[1,1,4,64,1024]{4,3,2,1,0:T(8,128)} %param.33) | copy-start | bytes 3145732
  6.0 3.5 %copy-start.12 = (bf16[2,1024,1024]{2,1,0:T(8,128)(2,1)S(1)}, bf16[2,1024,1024]{2,1,0:T(8,128)(2,1)}, u32[]{:S(2)}) copy-start(bf16[2,1024,1024]{2,1,0:T(8,128)(2,1)} %param.18) | copy-start | bytes 12582916
  11.1 1.2 %copy-start.13 = (f32[1,1,4,64,1024]{4,3,2,1,0:T(8,128)S(1)}, f32[1,1,4,64,1024]{4,3,2,1,0:T(8,128)}, u32[]{:S(2)}) copy-start(f32[1,1,4,64,1024]{4,3,2,1,0:T(8,128)} %param.32) | copy-start | bytes 3145732
  12.3 1.0 %copy-start = (s32[1,1,4]{2,1,0:T(1,128)S(1)}, s32[1,1,4]{2,1,0:T(1,128)}, u32[]{:S(2)}) copy-start(s32[1,1,4]{2,1,0:T(1,128)} %param.20) | copy-start | bytes 52
  12.3 1.0 %copy-start.1 = (s32[1,1,4]{2,1,0:T(1,128)S(1)}, s32[1,1,4]{2,1,0:T(1,128)}, u32[]{:S(2)}) copy-start(s32[1,1,4]{2,1,0:T(1,128)} %param.19) | copy-start | bytes 52
  12.3 40.6 %copy-start.4 = (f32[64,2048]{1,0:T(8,128)S(1)}, f32[64,2048]{1,0:T(8,128)}, u32[]{:S(2)}) copy-start(f32[64,2048]{1,0:T(8,128)} %param.28) | copy-start | bytes 1572868
  12.3 40.6 %copy-start.5 = (f32[64,2048]{1,0:T(8,128)S(1)}, f32[64,2048]{1,0:T(8,128)}, u32[]{:S(2)}) copy-start(f32[64,2048]{1,0:T(8,128)} %param.30) | copy-start | bytes 1572868
  12.3 40.6 %copy-start.6 = (f32[64,2048]{1,0:T(8,128)S(1)}, f32[64,2048]{1,0:T(8,128)}, u32[]{:S(2)}) copy-start(f32[64,2048]{1,0:T(8,128)} %param.29) | copy-start | bytes 1572868
  12.3 40.6 %copy-start.7 = (f32[64,2048]{1,0:T(8,128)S(1)}, f32[64,2048]{1,0:T(8,128)}, u32[]{:S(2)}) copy-start(f32[64,2048]{1,0:T(8,128)} %param.27) | copy-start | bytes 1572868
  13.2 40.2 %copy-start.2 = (f32[64,2048]{1,0:T(8,128)S(1)}, f32[64,2048]{1,0:T(8,128)}, u32[]{:S(2)}) copy-start(f32[64,2048]{1,0:T(8,128)} %param.23) | copy-start | bytes 1572868
  13.2 40.2 %copy-start.8 = (f32[64,2048]{1,0:T(8,128)S(1)}, f32[64,2048]{1,0:T(8,128)}, u32[]{:S(2)}) copy-start(f32[64,2048]{1,0:T(8,128)} %param.26) | copy-start | bytes 1572868
  13.2 40.2 %copy-start.9 = (f32[64,2048]{1,0:T(8,128)S(1)}, f32[64,2048]{1,0:T(8,128)}, u32[]{:S(2)}) copy-start(f32[64,2048]{1,0:T(8,128)} %param.25) | copy-start | bytes 1572868
  13.2 40.2 %copy-start.10 = (f32[64,2048]{1,0:T(8,128)S(1)}, f32[64,2048]{1,0:T(8,128)}, u32[]{:S(2)}) copy-start(f32[64,2048]{1,0:T(8,128)} %param.24) | copy-start | bytes 1572868

commit v17 on v16

--- a/solution.py
+++ b/solution.py
@@ -18,13 +18,19 @@
     return (lax.axis_index("row"), peer)
 
 
-def reduce_kernel(n, group_axes, block_width, with_counts, *refs):
+def reduce_kernel(n, group_axes, block_width, with_counts, finish, *refs):
     groups = len(group_axes)
     if with_counts:
         info, live_ref, refs = refs[:groups], refs[groups], refs[groups + 1 :]
     ins = refs[:groups]
-    outs = refs[groups : 2 * groups]
-    scratch = refs[2 * groups :]
+    refs = refs[groups:]
+    operands = []
+    if finish is not None:
+        for g in range(groups):
+            operands.append(refs[: finish[g][1]])
+            refs = refs[finish[g][1] :]
+    outs = refs[:groups]
+    scratch = refs[groups:]
     size = 7 if with_counts else 6
     per = [scratch[size * g : size * g + 6] for g in range(groups)]
     width = ins[0].shape[1] // n
@@ -116,6 +122,8 @@
                     jnp.tile(total[data_rows + b : data_rows + b + 1, :], (1, block_width // width))
                 )
         else:
+            if finish is not None:
+                total = finish[g][0](total, *[ref[:, cols(me)] for ref in operands[g]])
             outs[g][:, cols(me)] = total
         copies = []
         for k in range(1, n):
@@ -151,7 +159,7 @@
             copy.wait_send()
 
 
-def all_reduce(arrays, group_axes, n, collective_id, block_width, info=None):
+def all_reduce(arrays, group_axes, n, collective_id, block_width, info=None, finish=None):
     extra = 0 if info is None else 8
     shapes = [(a.shape[0] + extra, a.shape[1]) for a in arrays]
     width = shapes[0][1] // n
@@ -167,12 +175,16 @@
         ]
         if info is not None:
             scratch.append(pltpu.VMEM((n, rows, width), jnp.float32))
+    rules = None
+    if finish is not None:
+        rules = tuple((rule, len(extra)) for rule, extra in finish)
+        arrays = arrays + [a for _, extra in finish for a in extra]
     in_specs = [pl.BlockSpec(memory_space=pltpu.VMEM)] * len(arrays)
     if info is not None:
         in_specs = [pl.BlockSpec(memory_space=pltpu.SMEM)] * len(info) + in_specs
         arrays = list(info) + arrays
     return pl.pallas_call(
-        functools.partial(reduce_kernel, n, group_axes, block_width, info is not None),
+        functools.partial(reduce_kernel, n, group_axes, block_width, info is not None, rules),
         out_shape=tuple(jax.ShapeDtypeStruct(s, jnp.float32) for s in shapes),
         in_specs=in_specs,
         out_specs=tuple(pl.BlockSpec(memory_space=pltpu.VMEM) for _ in shapes),
@@ -181,6 +193,21 @@
             collective_id=collective_id, has_side_effects=True, vmem_limit_bytes=16 * 1024 * 1024
         ),
     )(*arrays)
+
+
+def column_rule(total, x_own, x_dual, cost, capacity, denom):
+    x_half = jnp.minimum(jnp.maximum(x_own - x_dual - cost, 0.0), capacity)
+    x_own = (x_half + x_dual + total) / denom
+    x_dual = x_dual + x_half - x_own
+    return jnp.minimum(jnp.maximum(x_own - x_dual - cost, 0.0), capacity)
+
+
+def row_rule(total, y_state, y_dual, lower, upper, denom):
+    y_half = jnp.minimum(jnp.maximum(y_state - y_dual, lower), upper)
+    y_anchor = y_half + y_dual
+    y_state = y_anchor + (total - y_anchor) / denom
+    y_dual = y_dual + y_half - y_state
+    return jnp.minimum(jnp.maximum(y_state - y_dual, lower), upper)
 
 
 def pick_blocks(full, index, blocks, block_width):
@@ -278,8 +305,20 @@
             row_denom = 1.0 + row_total[scenarios : scenarios + 1]
             col_total = col_total[:scenarios]
             row_total = row_total[:scenarios]
+        elif iteration == ITERS - 1:
+            return all_reduce(
+                [col_terms, row_terms],
+                AXES,
+                n_row,
+                1,
+                block_width,
+                finish=[
+                    (column_rule, [x_own, x_dual, unit_cost, capacity, col_denom]),
+                    (row_rule, [y_state, y_dual, row_lower, row_upper, row_denom]),
+                ],
+            )
         else:
-            col_total, row_total = all_reduce([col_terms, row_terms], AXES, n_row, 1, block_width)
+            col_total, row_total = all_reduce([col_terms, row_terms], AXES, n_row, 2, block_width)
         x_own = (x_half + x_dual + col_total) / col_denom
         x_dual = x_dual + x_half - x_own
         shift_full = (row_total - y_anchor) / row_denom

time: 96.5 us -> 95.8 us (level)
  other arithmetic: 6.58 us -> 4.29 us
  local copies, waits for them, and re-layouts: 1.67 us -> 3.27 us
    min x2 -> x0, other arithmetic: 2.42 us -> none  [the longest x1 1.21 us: per_device(): column_final = jnp.clip(x_own - x_dual - unit_cost, 0.0, capacity)]
    unnamed x28 -> x30, local copies, waits for them, and re-layouts: 0.53 us -> 2.12 us
where the time goes in v17:
time: 95.8 us; the launch traced here: 95.4 us
  Pallas kernels  74.4 us (78%)
  matrix products  11.6 us (12%)
  other arithmetic  4.29 us (4%)
  local copies, waits for them, and re-layouts  3.27 us (3%)
  between operations  1.82 us (2%)
    pallas_call x2, Pallas kernels, all_reduce(): pl.pallas_call(functools.partial(reduce_kernel, n, group_axes, block_widt...  74.4 us
    dot_general x12, matrix products, by_tile(): lax.dot_general(stacked, matrices[t], (((1,), (contract,)), ((), ())), pr...  11.6 us
    unnamed x30, local copies, waits for them, and re-layouts  2.12 us

profile of v17, /device:TPU:1, one launch (start us, length us, event | category | flops | bytes accessed | tf_op | source)
XLA Modules:
  0.0 95.4 jit_solution(13787951124775367337)
XLA Ops:
  0.6 0.0 copy-start.8
  0.6 0.0 copy-start.6
  1.4 1.1 %compare_bitcast_fusion = pred[4]{0:T(512)(128)(4,1)S(1)} fusion(s32[1,1,4]{2,1,0:T(1,128)} %param.21), kind=kLoop, calls=%fused_computation.81 | loop fusion | flops 4 | bytes 20 | tf_op jit(solution)/shard_map/eq | solution.py:233
  2.5 0.7 fusion.80
  3.2 1.7 %fusion.74 = bf16[4,64,1024]{2,1,0:T(8,128)(2,1)S(1)} fusion(f32[1,1,4,64,1024]{4,3,2,1,0:T(8,128)} %param.31, f32[1,1,4,64,1024]{4,3,2,1,0:T(8,128)} %param.32), kind=kLoop, calls=%fused_computation.65 | loop fusion | flops 524288 | bytes 2621440 | tf_op jit(solution)/shard_map/convert_element_type | solution.py:282
  4.9 1.1 %fusion.85 = (f32[64,1024]{1,0:T(8,128)S(1)}, f32[64,1024]{1,0:T(8,128)S(1)}) fusion(f32[64,2048]{1,0:T(8,128)} %param.23), kind=kLoop, calls=%fused_computation.92 | loop fusion | bytes 1048576 | tf_op jit(solution)/shard_map/slice | solution.py:217
  6.0 0.0 copy-start.9
  6.0 2.5 %fusion.14 = f32[4,64,1024]{2,1,0:T(8,128)S(1)} fusion(bf16[4,64,1024]{2,1,0:T(8,128)(2,1)S(1)} %fusion.74, bf16[2,1024,1024]{2,1,0:T(8,128)(2,1)} %param.17), kind=kOutput, calls=%fused_computation.14 | convolution fusion | flops 536870912 | bytes 3670016 | tf_op jit(solution)/shard_map/dot_general | solution.py:224
  8.5 0.0 copy-done.8
  8.5 0.0 copy-done.6
  8.5 0.9 fusion.69
  9.4 0.0 copy-done.9
  9.5 0.7 fusion.2
  10.2 0.9 select_reduce_fusion.7
  11.1 0.0 copy-start.10
  11.1 0.7 fusion.12
  11.8 0.5 copy-done.10
  12.3 0.0 copy-start.4
  12.3 0.0 copy-start.5
  12.3 0.0 copy-start
  12.3 0.0 copy-start.1
  12.3 0.0 copy-start.7
  12.3 0.0 copy-start.11
  12.3 0.9 select_reduce_fusion.5
  13.2 0.0 copy-start.2
  13.2 0.0 copy-start.3
  13.2 0.0 copy-start.12
  13.2 0.0 copy-start.13
  13.3 0.0 copy-done.4
  13.3 0.0 copy-done.5
  13.3 39.5 %shard_map.176 = (f32[72,2048]{1,0:T(8,128)S(1)}, f32[72,2048]{1,0:T(8,128)S(1)}) custom-call(s32[4]{0:T(128)S(1)} %bitcast.106, s32[4]{0:T(128)S(1)} %bitcast.107, s32[1]{0:T(128)} %bitcast.103.refs_2_, f32[64,2048]{1,0:T(8,128)S(1)} %pad_maximum_fusion.refs_3_, f32[64,2048]{1,0:T(8,128)S(1)} %pad_maximum_fusion.1.refs_4_), custom_call_target="tpu_custom_call" | custom-call | tf_op jit(solution)/shard_map/pallas_call | solution.py:186
  52.9 0.0 copy-done
  52.9 0.0 copy-done.1
  52.9 0.0 copy-done.7
  52.9 0.0 copy-done.11
  52.9 0.2 fusion.82
  53.2 0.0 copy-done.2
  53.2 0.0 copy-done.3
  53.2 0.0 copy-done.12
  53.2 0.0 copy-done.13
  53.2 0.3 fusion.81
  53.5 0.2 subtract_convert_fusion
  53.8 0.7 fusion.10
  54.5 0.9 fusion.66
  55.4 0.7 fusion
  56.1 1.0 %select_reduce_fusion.3 = (f32[64,1024]{1,0:T(8,128)S(1)}, f32[64,1024]{1,0:T(8,128)S(1)}, bf16[4,64,1024]{2,1,0:T(8,128)(2,1)S(1)}) fusion(pred[4]{0:T(512)(128)(4,1)S(1)} %get-tuple-element.31, f32[4,64,1024]{2,1,0:T(8,128)S(1)} %get-tuple-element.19, f32[64,1024]{1,0:T(8,128)S(1)} %get-tuple-element.21, f32[64,1024]{1,0:T(8,128)S(1)} %get-tuple-element.20, ...), kind=kOutput, calls=%fused_computation.55 | convolution fusion | flops 539099136 | bytes 6293504 | tf_op jit(solution)/shard_map/dot_general | solution.py:224
  57.2 0.7 fusion.8
  57.9 1.0 %select_reduce_fusion.1 = (f32[64,1024]{1,0:T(8,128)S(1)}, f32[64,1024]{1,0:T(8,128)S(1)}) fusion(pred[4]{0:T(512)(128)(4,1)S(1)} %get-tuple-element.35, pred[4]{0:T(512)(128)(4,1)S(1)} %get-tuple-element.36, f32[4,64,1024]{2,1,0:T(8,128)S(1)} %get-tuple-element.33, f32[64,1024]{1,0:T(8,128)S(1)} %get-tuple-element.23, ...), kind=kOutput, calls=%fused_computation.53 | convolution fusion | flops 539099136 | bytes 5769216 | tf_op jit(solution)/shard_map/dot_general | solution.py:224
  59.0 34.8 %shard_map.177 = (f32[64,2048]{1,0:T(8,128)S(1)}, f32[64,2048]{1,0:T(8,128)S(1)}) custom-call(f32[64,2048]{1,0:T(8,128)S(1)} %pad_maximum_fusion.2.refs_0_, f32[64,2048]{1,0:T(8,128)S(1)} %pad_maximum_fusion.3.refs_1_, f32[64,2048]{1,0:T(8,128)S(1)} %get-tuple-element.18.refs_2_, f32[64,2048]{1,0:T(8,128)S(1)} %get-tuple-element.17.refs_3_, ...), custom_call_target="tpu_custom_call" | custom-call | tf_op jit(solution)/shard_map/pallas_call | solution.py:186
  93.8 0.8 copy.22
  94.6 0.8 copy.23
  (8 shorter events, 0.2 us)
Async XLA Ops:
  0.6 7.8 %copy-start.8 = (bf16[2,1024,1024]{2,1,0:T(8,128)(2,1)S(1)}, bf16[2,1024,1024]{2,1,0:T(8,128)(2,1)}, u32[]{:S(2)}) copy-start(bf16[2,1024,1024]{2,1,0:T(8,128)(2,1)} %param.17) | copy-start | bytes 12582916
  0.6 7.8 %copy-start.6 = (f32[1,1,4,64,1024]{4,3,2,1,0:T(8,128)S(1)}, f32[1,1,4,64,1024]{4,3,2,1,0:T(8,128)}, u32[]{:S(2)}) copy-start(f32[1,1,4,64,1024]{4,3,2,1,0:T(8,128)} %param.33) | copy-start | bytes 3145732
  6.0 3.5 %copy-start.9 = (bf16[2,1024,1024]{2,1,0:T(8,128)(2,1)S(1)}, bf16[2,1024,1024]{2,1,0:T(8,128)(2,1)}, u32[]{:S(2)}) copy-start(bf16[2,1024,1024]{2,1,0:T(8,128)(2,1)} %param.18) | copy-start | bytes 12582916
  11.1 1.2 %copy-start.10 = (f32[1,1,4,64,1024]{4,3,2,1,0:T(8,128)S(1)}, f32[1,1,4,64,1024]{4,3,2,1,0:T(8,128)}, u32[]{:S(2)}) copy-start(f32[1,1,4,64,1024]{4,3,2,1,0:T(8,128)} %param.32) | copy-start | bytes 3145732
  12.3 1.0 %copy-start.4 = (s32[1,1,4]{2,1,0:T(1,128)S(1)}, s32[1,1,4]{2,1,0:T(1,128)}, u32[]{:S(2)}) copy-start(s32[1,1,4]{2,1,0:T(1,128)} %param.20) | copy-start | bytes 52
  12.3 1.0 %copy-start.5 = (s32[1,1,4]{2,1,0:T(1,128)S(1)}, s32[1,1,4]{2,1,0:T(1,128)}, u32[]{:S(2)}) copy-start(s32[1,1,4]{2,1,0:T(1,128)} %param.19) | copy-start | bytes 52
  12.3 40.6 %copy-start = (f32[64,2048]{1,0:T(8,128)S(1)}, f32[64,2048]{1,0:T(8,128)}, u32[]{:S(2)}) copy-start(f32[64,2048]{1,0:T(8,128)} %refs_5_.1) | copy-start | bytes 1572868
  12.3 40.6 %copy-start.1 = (f32[64,2048]{1,0:T(8,128)S(1)}, f32[64,2048]{1,0:T(8,128)}, u32[]{:S(2)}) copy-start(f32[64,2048]{1,0:T(8,128)} %refs_4_.1) | copy-start | bytes 1572868
  12.3 40.6 %copy-start.7 = (f32[64,2048]{1,0:T(8,128)S(1)}, f32[64,2048]{1,0:T(8,128)}, u32[]{:S(2)}) copy-start(f32[64,2048]{1,0:T(8,128)} %param.23) | copy-start | bytes 1572868
  12.3 40.6 %copy-start.11 = (f32[64,2048]{1,0:T(8,128)S(1)}, f32[64,2048]{1,0:T(8,128)}, u32[]{:S(2)}) copy-start(f32[64,2048]{1,0:T(8,128)} %param.24) | copy-start | bytes 1572868
  13.2 40.0 %copy-start.2 = (f32[64,2048]{1,0:T(8,128)S(1)}, f32[64,2048]{1,0:T(8,128)}, u32[]{:S(2)}) copy-start(f32[64,2048]{1,0:T(8,128)} %refs_10_.1) | copy-start | bytes 1572868
  13.2 40.0 %copy-start.3 = (f32[64,2048]{1,0:T(8,128)S(1)}, f32[64,2048]{1,0:T(8,128)}, u32[]{:S(2)}) copy-start(f32[64,2048]{1,0:T(8,128)} %refs_9_.1) | copy-start | bytes 1572868
  13.2 40.0 %copy-start.12 = (f32[64,2048]{1,0:T(8,128)S(1)}, f32[64,2048]{1,0:T(8,128)}, u32[]{:S(2)}) copy-start(f32[64,2048]{1,0:T(8,128)} %param.28) | copy-start | bytes 1572868
  13.2 40.0 %copy-start.13 = (f32[64,2048]{1,0:T(8,128)S(1)}, f32[64,2048]{1,0:T(8,128)}, u32[]{:S(2)}) copy-start(f32[64,2048]{1,0:T(8,128)} %param.27) | copy-start | bytes 1572868

commit v18 on v17

--- a/solution.py
+++ b/solution.py
@@ -44,6 +44,13 @@
             return ref.at[index]
         return ref.at[:, cols(index)]
 
+    issue_order = sorted(range(groups), key=lambda g: group_axes[g] != "col")
+    barrier = pltpu.get_barrier_semaphore()
+    for axis in [group_axes[g] for g in issue_order]:
+        me = lax.axis_index(axis)
+        for k in range(1, n):
+            peer = lax.rem(me + k, n)
+            pl.semaphore_signal(barrier, inc=1, device_id=peer_id(axis, peer), device_id_type=MESH)
     if with_counts:
         slots = info[0].shape[0]
         live = live_ref[0]
@@ -66,13 +73,6 @@
                 send[p, :data_rows, :] = ins[g][:, p * width : (p + 1) * width]
                 send[p, data_rows:, :] = count_rows
             sources[g] = send
-    issue_order = sorted(range(groups), key=lambda g: group_axes[g] != "col")
-    barrier = pltpu.get_barrier_semaphore()
-    for axis in [group_axes[g] for g in issue_order]:
-        me = lax.axis_index(axis)
-        for k in range(1, n):
-            peer = lax.rem(me + k, n)
-            pl.semaphore_signal(barrier, inc=1, device_id=peer_id(axis, peer), device_id_type=MESH)
     pl.semaphore_wait(barrier, groups * (n - 1))
 
     scatter = [None] * groups

time: 95.8 us -> 95.7 us (level)
  no operation moved by 1% of the time
where the time goes in v18:
time: 95.7 us; the launch traced here: 95.3 us
  Pallas kernels  74.3 us (78%)
  matrix products  11.6 us (12%)
  other arithmetic  4.29 us (4%)
  local copies, waits for them, and re-layouts  3.27 us (3%)
  between operations  1.82 us (2%)
    pallas_call x2, Pallas kernels, all_reduce(): pl.pallas_call(functools.partial(reduce_kernel, n, group_axes, block_widt...  74.3 us
    dot_general x12, matrix products, by_tile(): lax.dot_general(stacked, matrices[t], (((1,), (contract,)), ((), ())), pr...  11.6 us
    unnamed x30, local copies, waits for them, and re-layouts  2.12 us
    convert_element_type x2, other arithmetic, per_device(): (images - image_duals).astype(jnp.bfloat16).reshape(-1, block_width)  1.91 us

profile of v18, /device:TPU:1, one launch (start us, length us, event | category | flops | bytes accessed | tf_op | source)
XLA Modules:
  0.0 95.3 jit_solution(18225748214779293157)
XLA Ops:
  0.6 0.0 copy-start.8
  0.6 0.0 copy-start.6
  1.4 1.1 %compare_bitcast_fusion = pred[4]{0:T(512)(128)(4,1)S(1)} fusion(s32[1,1,4]{2,1,0:T(1,128)} %param.21), kind=kLoop, calls=%fused_computation.81 | loop fusion | flops 4 | bytes 20 | tf_op jit(solution)/shard_map/eq | solution.py:233
  2.5 0.7 fusion.80
  3.2 1.7 %fusion.74 = bf16[4,64,1024]{2,1,0:T(8,128)(2,1)S(1)} fusion(f32[1,1,4,64,1024]{4,3,2,1,0:T(8,128)} %param.31, f32[1,1,4,64,1024]{4,3,2,1,0:T(8,128)} %param.32), kind=kLoop, calls=%fused_computation.65 | loop fusion | flops 524288 | bytes 2621440 | tf_op jit(solution)/shard_map/convert_element_type | solution.py:282
  4.9 1.1 %fusion.85 = (f32[64,1024]{1,0:T(8,128)S(1)}, f32[64,1024]{1,0:T(8,128)S(1)}) fusion(f32[64,2048]{1,0:T(8,128)} %param.23), kind=kLoop, calls=%fused_computation.92 | loop fusion | bytes 1048576 | tf_op jit(solution)/shard_map/slice | solution.py:217
  6.0 0.0 copy-start.9
  6.0 2.5 %fusion.14 = f32[4,64,1024]{2,1,0:T(8,128)S(1)} fusion(bf16[4,64,1024]{2,1,0:T(8,128)(2,1)S(1)} %fusion.74, bf16[2,1024,1024]{2,1,0:T(8,128)(2,1)} %param.17), kind=kOutput, calls=%fused_computation.14 | convolution fusion | flops 536870912 | bytes 3670016 | tf_op jit(solution)/shard_map/dot_general | solution.py:224
  8.5 0.0 copy-done.8
  8.5 0.0 copy-done.6
  8.5 0.9 fusion.69
  9.4 0.0 copy-done.9
  9.5 0.7 fusion.2
  10.2 0.9 select_reduce_fusion.7
  11.1 0.0 copy-start.10
  11.1 0.7 fusion.12
  11.8 0.5 copy-done.10
  12.3 0.0 copy-start.4
  12.3 0.0 copy-start.5
  12.3 0.0 copy-start
  12.3 0.0 copy-start.1
  12.3 0.0 copy-start.7
  12.3 0.0 copy-start.11
  12.3 0.9 select_reduce_fusion.5
  13.2 0.0 copy-start.2
  13.2 0.0 copy-start.3
  13.2 0.0 copy-start.12
  13.2 0.0 copy-start.13
  13.3 0.0 copy-done.4
  13.3 0.0 copy-done.5
  13.3 39.5 %shard_map.176 = (f32[72,2048]{1,0:T(8,128)S(1)}, f32[72,2048]{1,0:T(8,128)S(1)}) custom-call(s32[4]{0:T(128)S(1)} %bitcast.106, s32[4]{0:T(128)S(1)} %bitcast.107, s32[1]{0:T(128)} %bitcast.103.refs_2_, f32[64,2048]{1,0:T(8,128)S(1)} %pad_maximum_fusion.refs_3_, f32[64,2048]{1,0:T(8,128)S(1)} %pad_maximum_fusion.1.refs_4_), custom_call_target="tpu_custom_call" | custom-call | tf_op jit(solution)/shard_map/pallas_call | solution.py:186
  52.8 0.0 copy-done
  52.8 0.0 copy-done.1
  52.8 0.0 copy-done.7
  52.8 0.0 copy-done.11
  52.8 0.2 fusion.82
  53.1 0.0 copy-done.2
  53.1 0.0 copy-done.3
  53.1 0.0 copy-done.12
  53.1 0.0 copy-done.13
  53.1 0.3 fusion.81
  53.4 0.2 subtract_convert_fusion
  53.7 0.7 fusion.10
  54.4 0.9 fusion.66
  55.3 0.7 fusion
  56.1 1.0 %select_reduce_fusion.3 = (f32[64,1024]{1,0:T(8,128)S(1)}, f32[64,1024]{1,0:T(8,128)S(1)}, bf16[4,64,1024]{2,1,0:T(8,128)(2,1)S(1)}) fusion(pred[4]{0:T(512)(128)(4,1)S(1)} %get-tuple-element.31, f32[4,64,1024]{2,1,0:T(8,128)S(1)} %get-tuple-element.19, f32[64,1024]{1,0:T(8,128)S(1)} %get-tuple-element.21, f32[64,1024]{1,0:T(8,128)S(1)} %get-tuple-element.20, ...), kind=kOutput, calls=%fused_computation.55 | convolution fusion | flops 539099136 | bytes 6293504 | tf_op jit(solution)/shard_map/dot_general | solution.py:224
  57.1 0.7 fusion.8
  57.9 1.0 %select_reduce_fusion.1 = (f32[64,1024]{1,0:T(8,128)S(1)}, f32[64,1024]{1,0:T(8,128)S(1)}) fusion(pred[4]{0:T(512)(128)(4,1)S(1)} %get-tuple-element.35, pred[4]{0:T(512)(128)(4,1)S(1)} %get-tuple-element.36, f32[4,64,1024]{2,1,0:T(8,128)S(1)} %get-tuple-element.33, f32[64,1024]{1,0:T(8,128)S(1)} %get-tuple-element.23, ...), kind=kOutput, calls=%fused_computation.53 | convolution fusion | flops 539099136 | bytes 5769216 | tf_op jit(solution)/shard_map/dot_general | solution.py:224
  58.9 34.8 %shard_map.177 = (f32[64,2048]{1,0:T(8,128)S(1)}, f32[64,2048]{1,0:T(8,128)S(1)}) custom-call(f32[64,2048]{1,0:T(8,128)S(1)} %pad_maximum_fusion.2.refs_0_, f32[64,2048]{1,0:T(8,128)S(1)} %pad_maximum_fusion.3.refs_1_, f32[64,2048]{1,0:T(8,128)S(1)} %get-tuple-element.18.refs_2_, f32[64,2048]{1,0:T(8,128)S(1)} %get-tuple-element.17.refs_3_, ...), custom_call_target="tpu_custom_call" | custom-call | tf_op jit(solution)/shard_map/pallas_call | solution.py:186
  93.7 0.8 copy.22
  94.5 0.8 copy.23
  (8 shorter events, 0.2 us)
Async XLA Ops:
  0.6 7.8 %copy-start.8 = (bf16[2,1024,1024]{2,1,0:T(8,128)(2,1)S(1)}, bf16[2,1024,1024]{2,1,0:T(8,128)(2,1)}, u32[]{:S(2)}) copy-start(bf16[2,1024,1024]{2,1,0:T(8,128)(2,1)} %param.17) | copy-start | bytes 12582916
  0.6 7.8 %copy-start.6 = (f32[1,1,4,64,1024]{4,3,2,1,0:T(8,128)S(1)}, f32[1,1,4,64,1024]{4,3,2,1,0:T(8,128)}, u32[]{:S(2)}) copy-start(f32[1,1,4,64,1024]{4,3,2,1,0:T(8,128)} %param.33) | copy-start | bytes 3145732
  6.0 3.5 %copy-start.9 = (bf16[2,1024,1024]{2,1,0:T(8,128)(2,1)S(1)}, bf16[2,1024,1024]{2,1,0:T(8,128)(2,1)}, u32[]{:S(2)}) copy-start(bf16[2,1024,1024]{2,1,0:T(8,128)(2,1)} %param.18) | copy-start | bytes 12582916
  11.1 1.2 %copy-start.10 = (f32[1,1,4,64,1024]{4,3,2,1,0:T(8,128)S(1)}, f32[1,1,4,64,1024]{4,3,2,1,0:T(8,128)}, u32[]{:S(2)}) copy-start(f32[1,1,4,64,1024]{4,3,2,1,0:T(8,128)} %param.32) | copy-start | bytes 3145732
  12.3 1.0 %copy-start.4 = (s32[1,1,4]{2,1,0:T(1,128)S(1)}, s32[1,1,4]{2,1,0:T(1,128)}, u32[]{:S(2)}) copy-start(s32[1,1,4]{2,1,0:T(1,128)} %param.20) | copy-start | bytes 52
  12.3 1.0 %copy-start.5 = (s32[1,1,4]{2,1,0:T(1,128)S(1)}, s32[1,1,4]{2,1,0:T(1,128)}, u32[]{:S(2)}) copy-start(s32[1,1,4]{2,1,0:T(1,128)} %param.19) | copy-start | bytes 52
  12.3 40.5 %copy-start = (f32[64,2048]{1,0:T(8,128)S(1)}, f32[64,2048]{1,0:T(8,128)}, u32[]{:S(2)}) copy-start(f32[64,2048]{1,0:T(8,128)} %refs_5_.1) | copy-start | bytes 1572868
  12.3 40.5 %copy-start.1 = (f32[64,2048]{1,0:T(8,128)S(1)}, f32[64,2048]{1,0:T(8,128)}, u32[]{:S(2)}) copy-start(f32[64,2048]{1,0:T(8,128)} %refs_4_.1) | copy-start | bytes 1572868
  12.3 40.5 %copy-start.7 = (f32[64,2048]{1,0:T(8,128)S(1)}, f32[64,2048]{1,0:T(8,128)}, u32[]{:S(2)}) copy-start(f32[64,2048]{1,0:T(8,128)} %param.23) | copy-start | bytes 1572868
  12.3 40.5 %copy-start.11 = (f32[64,2048]{1,0:T(8,128)S(1)}, f32[64,2048]{1,0:T(8,128)}, u32[]{:S(2)}) copy-start(f32[64,2048]{1,0:T(8,128)} %param.24) | copy-start | bytes 1572868
  13.2 39.9 %copy-start.2 = (f32[64,2048]{1,0:T(8,128)S(1)}, f32[64,2048]{1,0:T(8,128)}, u32[]{:S(2)}) copy-start(f32[64,2048]{1,0:T(8,128)} %refs_10_.1) | copy-start | bytes 1572868
  13.2 39.9 %copy-start.3 = (f32[64,2048]{1,0:T(8,128)S(1)}, f32[64,2048]{1,0:T(8,128)}, u32[]{:S(2)}) copy-start(f32[64,2048]{1,0:T(8,128)} %refs_9_.1) | copy-start | bytes 1572868
  13.2 39.9 %copy-start.12 = (f32[64,2048]{1,0:T(8,128)S(1)}, f32[64,2048]{1,0:T(8,128)}, u32[]{:S(2)}) copy-start(f32[64,2048]{1,0:T(8,128)} %param.28) | copy-start | bytes 1572868
  13.2 39.9 %copy-start.13 = (f32[64,2048]{1,0:T(8,128)S(1)}, f32[64,2048]{1,0:T(8,128)}, u32[]{:S(2)}) copy-start(f32[64,2048]{1,0:T(8,128)} %param.27) | copy-start | bytes 1572868
